TPU v7x, 32 devices: a whole 2x2x4 slice. The times are simulated.
32 devices in a mesh: strip: 8 (over y, x, core), frame: 4 (over z).
Axes of the slice: x: 2, y: 2, z: 4, core: 2. Of those that a mesh axis runs over, the one named last changes fastest.
Arguments:
- estimate: float32 [1024, 2048], P('strip'), may hold values from -6 to 6
- observed: float32 [8, 1024, 2048], P('frame', 'strip'), may hold values from -6 to 6
- weights: float32 [8, 1024, 2048], P('frame', 'strip'), may hold values from 0.3 to 9, as said below
- column_kernels: float32 [8, 65], P('frame'), may hold values from 0.05 to 1
- row_kernels: float32 [8, 65], P('frame'), may hold values from 0.05 to 1
Outputs:
- solution: float32 [1024, 2048], P('strip')
- residual: float32 [1024, 2048], P('strip')
Inputs may be any that keep to these rules, and one draw needn't show every extreme that they name: Positive weights of each pixel.
All inputs are finite; a program needn't handle non-finite values.
Results may differ from a plain program's by a relative error of at most 0.00013.
Values sent between devices are 32-bit elements; how exact they have to be, the bound alone decides.
No kernel may reach another device: no remote copies, remote signals or barrier semaphores. Data moves between devices by JAX's collectives and lax.ppermute only.
A program may use at most 128 MiB of HBM per device.

v0:
```python
import functools

import jax
import jax.numpy as jnp
from jax import lax
from jax.experimental import pallas as pl
from jax.experimental.pallas import tpu as pltpu
from jax.sharding import PartitionSpec as P

damping = 0.05
f32 = jnp.float32
bf16 = jnp.bfloat16
LANE = 128
VMEM = pl.BlockSpec(memory_space=pltpu.VMEM)
ANY = pl.BlockSpec(memory_space=pl.ANY)


def split(x):
    hi = x.astype(bf16)
    lo = (x - hi.astype(f32)).astype(bf16)
    return hi, lo


def dot(a, b):
    return jnp.dot(a, b, preferred_element_type=f32)


def tiles(width, step=256):
    return [(s, min(step, width - s)) for s in range(0, width, step)]


def kernel_bases(col_unit, row_unit):
    count, taps = col_unit.shape
    wide = 2 * LANE

    def at(values, start):
        return jnp.pad(values, ((0, 0), (start, wide - taps - start)))

    def turned(values):
        gap = jnp.zeros((count, wide - taps), f32)
        return jnp.concatenate([values[:, :1], gap, values[:, :0:-1]], axis=1)

    return jnp.stack(
        [at(row_unit, 0), turned(col_unit), at(col_unit, LANE), turned(row_unit)], axis=1
    )


def setup_kernel(per_group, rows, halo, base_ref, t_ref, b_ref, bp_ref, ta_ref):
    frames = base_ref.shape[0]

    def toeplitz(f, which, count):
        base = jnp.broadcast_to(base_ref[f, which : which + 1, :], (count, 2 * LANE))
        return pltpu.roll(base, 0, 1, stride=1, stride_axis=0)

    ext = rows + 2 * halo
    for f in range(frames):
        hi, lo = split(toeplitz(f, 0, rows))
        t_ref[f, :rows, :] = hi
        t_ref[f, rows:, :] = lo
        hi, lo = split(toeplitz(f, 1, 2 * LANE)[:, :LANE])
        b_ref[f, :, :LANE] = hi
        b_ref[f, :, LANE:] = lo
        hi, lo = split(toeplitz(f, 2, 2 * LANE)[:, :LANE])
        bp_ref[f, :, :LANE] = hi
        bp_ref[f, :, LANE:] = lo
        hi, lo = split(toeplitz(f, 3, ext)[:, :rows])
        g, s = divmod(f, per_group)
        ta_ref[g, :ext, s * rows : (s + 1) * rows] = hi
        ta_ref[g, ext:, s * rows : (s + 1) * rows] = lo


def setup_matrices(bases, per_group, rows, halo):
    frames = bases.shape[0]
    ext = rows + 2 * halo
    shapes = (
        (frames, 2 * rows, 2 * LANE),
        (frames, 2 * LANE, 2 * LANE),
        (frames, 2 * LANE, 2 * LANE),
        (frames // per_group, 2 * ext, per_group * rows),
    )
    return pl.pallas_call(
        functools.partial(setup_kernel, per_group, rows, halo),
        out_shape=[jax.ShapeDtypeStruct(s, bf16) for s in shapes],
        in_specs=[VMEM],
        out_specs=[VMEM] * 4,
        name="setup_matrices",
    )(bases)


def load_image(y_hi, y_lo, image, halo):
    ext, full = image.shape
    shift = LANE - halo
    y = pltpu.roll(image, full - shift, 1)[:, : full - LANE]
    hi, lo = split(y)
    y_hi[:ext, :] = hi
    y_lo[:ext, :] = lo


def group_terms(frames, rows, w, y_hi, y_lo, t, b, bp, ta, weight, data, us, qs, vs_hi, vs_lo, acc, stat):
    total = None
    for f in range(frames):
        for c, size in tiles(w + LANE):
            r1 = dot(t(f)[...], y_hi[:, c : c + size])
            r2 = dot(t(f)[:rows, :], y_lo[:, c : c + size])
            hi, lo = split(r1[:rows] + r1[rows:] + r2)
            us[:rows, c : c + size] = hi
            us[rows:, c : c + size] = lo
        for k in range(w // LANE):
            c = k * LANE
            r = dot(us[:, c : c + 2 * LANE], b(f)[...])
            a = r[:rows, :LANE] + r[:rows, LANE:] + r[rows:, :LANE]
            if data is not None:
                a = a - data(f)[:, c : c + LANE]
            q = weight(f)[:, c : c + LANE] * a
            if stat is not None:
                part = jnp.sum((a * q).reshape(rows // 8, 8, LANE), axis=0)
                total = part if total is None else total + part
            hi, lo = split(q)
            qs[:rows, c + LANE : c + 2 * LANE] = hi
            qs[rows:, c + LANE : c + 2 * LANE] = lo
        for k in range(w // LANE + 1):
            c = k * LANE
            r = dot(qs[:, c : c + 2 * LANE], bp(f)[...])
            hi, lo = split(r[:rows, :LANE] + r[:rows, LANE:] + r[rows:, :LANE])
            vs_hi[f * rows : (f + 1) * rows, c : c + LANE] = hi
            vs_lo[f * rows : (f + 1) * rows, c : c + LANE] = lo
    ext = acc.shape[0]
    for c, size in tiles(w + LANE):
        r1 = dot(ta[...], vs_hi[:, c : c + size])
        r2 = dot(ta[:ext, :], vs_lo[:, c : c + size])
        acc[:, c : c + size] += r1[:ext] + r1[ext:] + r2
    if stat is not None:
        stat[...] += total


def work_scratch(frames, rows, halo, w):
    ext = rows + 2 * halo
    return [
        pltpu.VMEM((2 * LANE, w + LANE), bf16),
        pltpu.VMEM((2 * LANE, w + LANE), bf16),
        pltpu.VMEM((2 * rows, w + LANE), bf16),
        pltpu.VMEM((2 * rows, w + 2 * LANE), bf16),
        pltpu.VMEM((frames * rows, w + LANE), bf16),
        pltpu.VMEM((frames * rows, w + LANE), bf16),
        pltpu.VMEM((ext, w + LANE), f32),
    ]


def clear_edges(y_hi, y_lo, qs, ext, rows, w):
    zero = jnp.zeros((y_hi.shape[0] - ext, y_hi.shape[1]), bf16)
    y_hi[ext:, :] = zero
    y_lo[ext:, :] = zero
    qs[:, :LANE] = jnp.zeros((2 * rows, LANE), bf16)
    qs[:, w + LANE :] = jnp.zeros((2 * rows, LANE), bf16)


def unshift(acc, halo):
    return pltpu.roll(acc, acc.shape[1] - halo, 1)


def first_kernel(
    frames, rows, halo, w,
    est, lo, hi, t_ref, b_ref, bp_ref, ta_ref, w_hbm, d_hbm,
    top, mid, bot,
    y_hi, y_lo, us, qs, vs_hi, vs_lo, acc, estp, outp, wbuf, dbuf, sem,
):
    ext = rows + 2 * halo
    cols = est.shape[1]
    blocks = cols // w

    def copies(j, slot):
        window = pl.ds(pl.multiple_of(j * w, LANE), w)
        return (
            pltpu.make_async_copy(w_hbm.at[:, :, window], wbuf.at[slot], sem.at[0, slot]),
            pltpu.make_async_copy(d_hbm.at[:, :, window], dbuf.at[slot], sem.at[1, slot]),
        )

    for c in copies(0, 0):
        c.start()
    clear_edges(y_hi, y_lo, qs, ext, rows, w)
    for edge in (0, LANE + cols):
        estp[:, edge : edge + LANE] = jnp.zeros((ext, LANE), f32)
    inner = slice(LANE, LANE + cols)
    estp[:halo, inner] = lo[...]
    estp[halo : halo + rows, inner] = est[...]
    estp[halo + rows :, inner] = hi[...]
    outp[...] = jnp.zeros_like(outp)
    lane = lax.broadcasted_iota(jnp.int32, (ext, LANE), 1)

    @pl.loop(0, blocks)
    def _(j):
        slot = lax.rem(j, 2)

        @pl.when(j + 1 < blocks)
        def _():
            for c in copies(j + 1, 1 - slot):
                c.start()

        start = pl.multiple_of(j * w, LANE)
        load_image(y_hi, y_lo, estp[:, pl.ds(start, w + 2 * LANE)], halo)
        acc[...] = jnp.zeros_like(acc)
        for c in copies(j, slot):
            c.wait()
        group_terms(
            frames, rows, w, y_hi, y_lo,
            lambda f: t_ref.at[f], lambda f: b_ref.at[f], lambda f: bp_ref.at[f], ta_ref.at[0],
            lambda f: wbuf.at[slot, f], lambda f: dbuf.at[slot, f],
            us, qs, vs_hi, vs_lo, acc, None,
        )
        z = unshift(acc[...], halo)
        edge = z[:, w:]
        outp[:, pl.ds(start, LANE)] += jnp.where(lane >= LANE - halo, edge, 0.0)
        outp[:, pl.ds(pl.multiple_of(start + LANE, LANE), w)] += z[:, :w]
        outp[:, pl.ds(pl.multiple_of(start + LANE + w, LANE), LANE)] += jnp.where(lane < halo, edge, 0.0)

    top[...] = outp[:halo, inner]
    mid[...] = outp[halo : halo + rows, inner]
    bot[...] = outp[halo + rows :, inner]


def first_terms(est, lo, hi, mats, weights, observed, w):
    frames, rows, cols = weights.shape
    halo = lo.shape[0]
    ext = rows + 2 * halo
    return pl.pallas_call(
        functools.partial(first_kernel, frames, rows, halo, w),
        out_shape=[
            jax.ShapeDtypeStruct((halo, cols), f32),
            jax.ShapeDtypeStruct((rows, cols), f32),
            jax.ShapeDtypeStruct((halo, cols), f32),
        ],
        in_specs=[VMEM] * 7 + [ANY, ANY],
        out_specs=[VMEM] * 3,
        scratch_shapes=work_scratch(frames, rows, halo, w)
        + [
            pltpu.VMEM((ext, cols + 2 * LANE), f32),
            pltpu.VMEM((ext, cols + 2 * LANE), f32),
            pltpu.VMEM((2, frames, rows, w), f32),
            pltpu.VMEM((2, frames, rows, w), f32),
            pltpu.SemaphoreType.DMA((2, 2)),
        ],
        cost_estimate=pl.CostEstimate(flops=8 * 10**9, bytes_accessed=8 * 2**20, transcendentals=0),
        name="first_terms",
    )(est, lo, hi, *mats, weights, observed)


def apply_kernel(frames, rows, halo, w, groups, base, has_acc, final, *refs):
    image, t_hbm, b_hbm, bp_hbm, ta_hbm = refs[:5]
    weights = refs[5 : 5 + groups]
    refs = refs[5 + groups :]
    if has_acc:
        acc_in, stat_in = refs[:2]
        refs = refs[2:]
    out, stat, y_hi, y_lo, us, qs, vs_hi, vs_lo, acc, tb, bb, bpb, tab, wbuf, sem = refs
    ext = rows + 2 * halo

    def copies(g):
        span = pl.ds((base + g) * frames, frames)
        return [
            pltpu.make_async_copy(t_hbm.at[span], tb.at[g], sem.at[0, g]),
            pltpu.make_async_copy(b_hbm.at[span], bb.at[g], sem.at[1, g]),
            pltpu.make_async_copy(bp_hbm.at[span], bpb.at[g], sem.at[2, g]),
            pltpu.make_async_copy(ta_hbm.at[base + g], tab.at[g], sem.at[3, g]),
        ]

    for g in range(groups):
        for c in copies(g):
            c.start()
        pltpu.make_async_copy(weights[g], wbuf.at[g], sem.at[4, g]).start()
    clear_edges(y_hi, y_lo, qs, ext, rows, w)
    load_image(y_hi, y_lo, image[...], halo)
    if has_acc:
        acc[...] = acc_in[...]
        stat[...] = stat_in[...]
    else:
        acc[...] = jnp.zeros_like(acc)
        stat[...] = jnp.zeros_like(stat)

    @pl.loop(0, groups)
    def _(g):
        for c in copies(g):
            c.wait()
        pltpu.make_async_copy(weights[0], wbuf.at[g], sem.at[4, g]).wait()
        group_terms(
            frames, rows, w, y_hi, y_lo,
            lambda f: tb.at[g, f], lambda f: bb.at[g, f], lambda f: bpb.at[g, f], tab.at[g],
            lambda f: wbuf.at[g, f], None,
            us, qs, vs_hi, vs_lo, acc, stat,
        )

    out[...] = unshift(acc[...], halo) if final else acc[...]


def apply_terms(image, mats, weights, base, halo, carry=None, final=True):
    frames, rows, w = weights[0].shape
    ext = rows + 2 * halo
    groups = len(weights)
    t, b, bp, ta = mats
    args = [image, t, b, bp, ta, *weights]
    specs = [VMEM] + [ANY] * (4 + groups)
    if carry is not None:
        args += list(carry)
        specs += [VMEM, VMEM]
    return pl.pallas_call(
        functools.partial(apply_kernel, frames, rows, halo, w, groups, base, carry is not None, final),
        out_shape=[
            jax.ShapeDtypeStruct((ext, w + LANE), f32),
            jax.ShapeDtypeStruct((8, LANE), f32),
        ],
        in_specs=specs,
        out_specs=[VMEM, VMEM],
        scratch_shapes=work_scratch(frames, rows, halo, w)
        + [
            pltpu.VMEM((groups, frames) + t.shape[1:], bf16),
            pltpu.VMEM((groups, frames) + b.shape[1:], bf16),
            pltpu.VMEM((groups, frames) + bp.shape[1:], bf16),
            pltpu.VMEM((groups,) + ta.shape[1:], bf16),
            pltpu.VMEM((groups, frames, rows, w), f32),
            pltpu.SemaphoreType.DMA((5, groups)),
        ],
        cost_estimate=pl.CostEstimate(
            flops=groups * 3 * 10**9, bytes_accessed=groups * 2**20, transcendentals=0
        ),
        name="apply_terms",
    )(*args)


def shift_up(x, axis):
    n = lax.axis_size(axis)
    return lax.ppermute(x, axis, [(i, i + 1) for i in range(n - 1)])


def shift_down(x, axis):
    n = lax.axis_size(axis)
    return lax.ppermute(x, axis, [(i + 1, i) for i in range(n - 1)])


def swap(x, axis, distance):
    n = lax.axis_size(axis)
    return lax.ppermute(x, axis, [(i, i ^ distance) for i in range(n)])


def body(estimate, observed, weights, column_kernels, row_kernels):
    n = lax.axis_size("frame")
    me = lax.axis_index("frame")
    strips = lax.axis_size("strip")
    strip = lax.axis_index("strip")
    rows, cols = estimate.shape
    frames = weights.shape[0]
    halo = column_kernels.shape[1] // 2
    w = cols // n
    ext = rows + 2 * halo
    distances = [1 << k for k in range(n.bit_length() - 1)]

    unit = lambda k: k / jnp.sum(k, axis=1, keepdims=True)
    bases = kernel_bases(unit(column_kernels), unit(row_kernels))
    est_lo = shift_up(estimate[rows - halo :], "strip")
    est_hi = shift_down(estimate[:halo], "strip")

    def block_of(x, j):
        return lax.dynamic_slice_in_dim(x, j * w, w, axis=x.ndim - 1)

    my_weights = [block_of(weights, me)]
    for d in range(1, n):
        my_weights.append(swap(block_of(weights, me ^ d), "frame", d))

    own_mats = setup_matrices(bases, frames, rows, halo)
    top, mid, bot = first_terms(estimate, est_lo, est_hi, own_mats, weights, observed, w)

    all_bases = bases
    for d in distances:
        all_bases = jnp.concatenate([all_bases, swap(all_bases, "frame", d)], axis=0)
    mats = setup_matrices(all_bases, frames, rows, halo)

    from_up = shift_up(bot, "strip")
    from_dn = shift_down(top, "strip")
    terms = jnp.concatenate(
        [mid[:halo] + from_up, mid[halo : rows - halo], mid[rows - halo :] + from_dn], axis=0
    )

    left = terms
    for k, d in enumerate(distances):
        bit = (me // d) % 2
        half = left.shape[1] // w // 2

        def pick(which, left=left, half=half):
            return jnp.concatenate(
                [block_of(left, 2 * i + which) for i in range(half)], axis=1
            )

        left = pick(bit) + swap(pick(1 - bit), "frame", d)
    k0 = -(left + damping * block_of(estimate, me))

    lane = lax.broadcasted_iota(jnp.int32, (ext, LANE), 1)
    row = lax.broadcasted_iota(jnp.int32, (ext, 1), 0)
    inside = ((row >= halo) | (strip > 0)) & ((row < halo + rows) | (strip < strips - 1))
    first = me == 0
    last = me == n - 1

    k0_rows = jnp.concatenate(
        [shift_up(k0[rows - halo :], "strip"), k0, shift_down(k0[:halo], "strip")], axis=0
    )
    k0x = jnp.concatenate(
        [
            shift_up(k0_rows[:, w - LANE :], "frame"),
            k0_rows,
            shift_down(k0_rows[:, :LANE], "frame"),
        ],
        axis=1,
    )

    def complete(part, before):
        up = shift_up(part[rows:], "strip")
        dn = shift_down(part[: 2 * halo], "strip")
        q = jnp.concatenate(
            [part[: 2 * halo] + up, part[2 * halo : rows], part[rows:] + dn], axis=0
        )
        q = jnp.where(inside, q, 0.0)
        edge = q[:, w:]
        to_right = jnp.where(lane >= LANE - halo, q[:, w - LANE : w], edge)
        to_left = jnp.where(lane < halo, q[:, :LANE], edge)
        from_left = shift_up(to_right, "frame")
        from_right = shift_down(to_left, "frame")
        left_tile = jnp.where(first, 0.0, edge + from_left)
        right_tile = jnp.where(last, 0.0, edge + from_right)
        own_left = jnp.where(lane < halo, from_left, 0.0)
        own_right = jnp.where(lane >= LANE - halo, from_right, 0.0)
        pad = jnp.zeros((ext, w - LANE), f32)
        own = (
            q[:, :w]
            + jnp.concatenate([own_left, pad], axis=1)
            + jnp.concatenate([pad, own_right], axis=1)
        )
        return jnp.concatenate([left_tile, own, right_tile], axis=1) + damping * before

    def own_block(x):
        return x[halo : halo + rows, LANE : LANE + w]

    carry = apply_terms(k0x, mats, my_weights[: n - 1], 0, halo, final=False)
    part1, stat1 = apply_terms(k0x, mats, my_weights[n - 1 :], n - 1, halo, carry)
    k1x = complete(part1, k0x)
    part2, stat2 = apply_terms(k1x, mats, my_weights, 0, halo)
    k1 = own_block(k1x)
    k2 = own_block(complete(part2, k1x))

    def fold(x):
        return jnp.sum(x.reshape(rows * w // (8 * LANE), 8, LANE), axis=0)

    sums = jnp.stack([fold(k0 * k0), stat1, fold(k1 * k1), stat2])
    for axis, size in (("strip", strips), ("frame", n)):
        d = 1
        while d < size:
            sums = sums + swap(sums, axis, d)
            d *= 2
    sums = jnp.sum(sums, axis=(1, 2))
    k00, k11 = sums[0], sums[2]
    k01 = sums[1] + damping * k00
    k12 = sums[3] + damping * k11
    alpha0 = k00 / k01
    norm1 = k00 - 2.0 * alpha0 * k01 + alpha0 * alpha0 * k11
    beta = norm1 / k00
    curve1 = (1.0 + beta) ** 2 * k01 - 2.0 * (1.0 + beta) * alpha0 * k11 + alpha0 * alpha0 * k12
    alpha1 = norm1 / curve1
    c1 = alpha0 + alpha1 * (1.0 + beta)
    c2 = alpha0 * alpha1

    def gathered(x):
        parts = [x] + [None] * (n - 1)
        for d in reversed(distances):
            known = [i for i in range(n) if parts[i] is not None]
            sent = swap(jnp.stack([parts[i] for i in known]), "frame", d)
            for s, i in enumerate(known):
                parts[i ^ d] = sent[s]
        both = jnp.stack(parts)
        return jnp.concatenate(
            [lax.dynamic_index_in_dim(both, me ^ j, 0, keepdims=False) for j in range(n)], axis=1
        )

    g0, g1, g2 = gathered(k0), gathered(k1), gathered(k2)
    return estimate + c1 * g0 - c2 * g1, g0 - c1 * g1 + c2 * g2


def solution(mesh):
    return jax.shard_map(
        body,
        mesh=mesh,
        in_specs=(
            P("strip", None),
            P("frame", "strip", None),
            P("frame", "strip", None),
            P("frame", None),
            P("frame", None),
        ),
        out_specs=(P("strip", None), P("strip", None)),
        check_vma=False,
    )
```

profile of v0, /device:TPU:2, one launch (start us, length us, event | category | flops | bytes accessed | tf_op | source)
XLA Modules:
  0.0 265.4 jit_solution(5252114483478767546)
XLA Ops:
  1.7 1.9 collective-permute-start
  3.6 3.6 %collective-permute-start.1 = (f32[32,2048]{1,0:T(8,128)S(1)}, f32[32,2048]{1,0:T(8,128)S(1)}, u32[]{:S(2)}, u32[]{:S(2)}) collective-permute-start(f32[32,2048]{1,0:T(8,128)S(1)} %get-tuple-element.60), channel_id=1, source_target_pairs={{4,0},{8,4},{12,8},{16,12},{20,16},{24,20},{28,24},{5,1},{9,5},{13... | collective-permute-start | bytes 786440 | tf_op jit(solution)/shard_map/ppermute | solution.py:335
  11.6 1.9 setup_matrices.2
  14.3 11.9 %first_terms.1 = (f32[32,2048]{1,0:T(8,128)}, f32[128,2048]{1,0:T(8,128)}, f32[32,2048]{1,0:T(8,128)}) custom-call(f32[128,2048]{1,0:T(8,128)} %est.1, f32[32,2048]{1,0:T(8,128)} %copy-done.8, f32[32,2048]{1,0:T(8,128)} %copy-done.9, bf16[2,256,256]{2,1,0:T(8,128)(2,1)} %get-tuple-element.19.t_ref, bf16[2,256,256]{2,1,0:T(8,128)(2,1)} %get-tuple-element.20.b_ref, ...), custom_call_target="tpu_custom_call" | custom-call | flops 8000000000 | bytes 8388608 | tf_op jit(solution)/shard_map/first_terms/pallas_call | solution.py:225
  26.2 2.2 collective-permute-start.2
  28.4 3.4 %collective-permute-start.3 = (f32[32,2048]{1,0:T(8,128)}, f32[32,2048]{1,0:T(8,128)S(1)}, u32[]{:S(2)}, u32[]{:S(2)}) collective-permute-start(f32[32,2048]{1,0:T(8,128)} %get-tuple-element.25), channel_id=1, source_target_pairs={{4,0},{8,4},{12,8},{16,12},{20,16},{24,20},{28,24},{5,1},{9,5},{13... | collective-permute-start | bytes 786440 | tf_op jit(solution)/shard_map/ppermute | solution.py:335
  32.9 1.2 collective-permute-done.2
  34.1 2.8 %collective-permute-done.3 = f32[32,2048]{1,0:T(8,128)S(1)} collective-permute-done((f32[32,2048]{1,0:T(8,128)}, f32[32,2048]{1,0:T(8,128)S(1)}, u32[]{:S(2)}, u32[]{:S(2)}) %collective-permute-start.3) | collective-permute-done | bytes 262176 | tf_op jit(solution)/shard_map/ppermute | solution.py:335
  38.3 1.7 collective-permute-start.4
  39.9 11.7 %collective-permute-done.4 = f32[128,1024]{1,0:T(8,128)S(1)} collective-permute-done((f32[128,1024]{1,0:T(8,128)S(1)}, f32[128,1024]{1,0:T(8,128)S(1)}, u32[]{:S(2)}, u32[]{:S(2)}) %collective-permute-start.4) | collective-permute-done | bytes 524320 | tf_op jit(solution)/shard_map/ppermute | solution.py:340
  51.7 2.7 %collective-permute-start.5 = (f32[128,512]{1,0:T(8,128)S(1)}, f32[128,512]{1,0:T(8,128)}, u32[]{:S(2)}, u32[]{:S(2)}) collective-permute-start(f32[128,512]{1,0:T(8,128)S(1)} %constant_dynamic-slice_fusion.4), channel_id=1, source_target_pairs={{0,2},{1,3},{2,0},{3,1},{4,6},{5,7},{6,4},{7,5},{8,10},{9,11},{10,... | collective-permute-start | bytes 786440 | tf_op jit(solution)/shard_map/ppermute | solution.py:340
  54.4 1.6 collective-permute-start.10
  55.9 2.9 %constant_dynamic-slice_fusion = (f32[2,128,512]{2,1,0:T(8,128)S(1)}, f32[2,128,512]{2,1,0:T(8,128)}, f32[2,128,512]{2,1,0:T(8,128)S(1)}, f32[2,128,512]{2,1,0:T(8,128)}) fusion(f32[2,128,2048]{2,1,0:T(8,128)} %w_hbm.1, s32[]{:T(128)S(6)} %select_n.135, s32[]{:T(128)S(6)} %select_n.132, s32[]{:T(128)S(6)} %select_n.133, s32[]{:T(128)S(6)} %select_n.134), kind=kLoop, calls=%fused_computation.63 | loop fusion | bytes 4194320 | tf_op jit(solution)/shard_map/dynamic_slice | solution.py:361
  59.8 3.5 %collective-permute-start.14 = (f32[2,128,512]{2,1,0:T(8,128)S(1)}, f32[2,128,512]{2,1,0:T(8,128)}, u32[]{:S(2)}, u32[]{:S(2)}) collective-permute-start(f32[2,128,512]{2,1,0:T(8,128)S(1)} %get-tuple-element.38), channel_id=1, source_target_pairs={{0,2},{1,3},{2,0},{3,1},{4,6},{5,7},{6,4},{7,5},{8,10},{9,11},{10,... | collective-permute-start | bytes 1572872 | tf_op jit(solution)/shard_map/ppermute | solution.py:340
  63.2 15.3 %collective-permute-done.5 = f32[128,512]{1,0:T(8,128)} collective-permute-done((f32[128,512]{1,0:T(8,128)S(1)}, f32[128,512]{1,0:T(8,128)}, u32[]{:S(2)}, u32[]{:S(2)}) %collective-permute-start.5) | collective-permute-done | bytes 262176 | tf_op jit(solution)/shard_map/ppermute | solution.py:340
  79.6 1.9 collective-permute-start.7
  81.6 2.4 collective-permute-start.6
  84.1 3.0 %collective-permute-done.6 = f32[32,512]{1,0:T(8,128)S(1)} collective-permute-done((f32[32,512]{1,0:T(8,128)S(1)}, f32[32,512]{1,0:T(8,128)S(1)}, u32[]{:S(2)}, u32[]{:S(2)}) %collective-permute-start.6) | collective-permute-done | bytes 65568 | tf_op jit(solution)/shard_map/ppermute | solution.py:330
  87.2 1.3 collective-permute-start.9
  88.5 24.3 %collective-permute-done.11 = f32[4,4,256]{2,1,0:T(4,128)S(1)} collective-permute-done((f32[4,4,256]{2,1,0:T(4,128)S(1)}, f32[4,4,256]{2,1,0:T(4,128)S(1)}, u32[]{:S(2)}, u32[]{:S(2)}) %collective-permute-start.11) | collective-permute-done | bytes 16416 | tf_op jit(solution)/shard_map/ppermute | solution.py:340
  112.8 2.9 %collective-permute-start.8 = (f32[192,128]{1,0:T(8,128)S(1)}, f32[192,128]{1,0:T(8,128)S(1)}, u32[]{:S(2)}, u32[]{:S(2)}) collective-permute-start(f32[192,128]{1,0:T(8,128)S(1)} %get-tuple-element.89), channel_id=1, source_target_pairs={{0,1},{1,2},{2,3},{4,5},{5,6},{6,7},{8,9},{9,10},{10,11},{12,13},{... | collective-permute-start | bytes 294920 | tf_op jit(solution)/shard_map/ppermute | solution.py:330
  116.3 3.7 %setup_matrices.3 = (bf16[8,256,256]{2,1,0:T(8,128)(2,1)}, bf16[8,256,256]{2,1,0:T(8,128)(2,1)}, bf16[8,256,256]{2,1,0:T(8,128)(2,1)}, bf16[4,384,256]{2,1,0:T(8,128)(2,1)}) custom-call(f32[8,4,256]{2,1,0:T(4,128)} %pad_maximum_fusion.16.base_ref), custom_call_target="tpu_custom_call" | custom-call | tf_op jit(solution)/shard_map/setup_matrices/pallas_call | solution.py:81
  120.9 8.4 %apply_terms.3 = (f32[192,640]{1,0:T(8,128)}, f32[8,128]{1,0:T(8,128)}) custom-call(f32[192,768]{1,0:T(8,128)} %pad_maximum_fusion.6.refs_0_, bf16[8,256,256]{2,1,0:T(8,128)(2,1)} %get-tuple-element.26.refs_1_, bf16[8,256,256]{2,1,0:T(8,128)(2,1)} %get-tuple-element.27.refs_2_, bf16[8,256,256]{2,1,0:T(8,128)(2,1)} %get-tuple-element.28.refs_3_, ...), custom_call_target="tpu_custom_call" | custom-call | flops 8999999488 | bytes 3145728 | tf_op jit(solution)/shard_map/apply_terms/pallas_call | solution.py:304
  129.4 5.1 %apply_terms.4 = (f32[192,640]{1,0:T(8,128)}, f32[8,128]{1,0:T(8,128)}) custom-call(f32[192,768]{1,0:T(8,128)} %pad_maximum_fusion.6.refs_0_, bf16[8,256,256]{2,1,0:T(8,128)(2,1)} %get-tuple-element.26.refs_1_, bf16[8,256,256]{2,1,0:T(8,128)(2,1)} %get-tuple-element.27.refs_2_, bf16[8,256,256]{2,1,0:T(8,128)(2,1)} %get-tuple-element.28.refs_3_, ...), custom_call_target="tpu_custom_call" | custom-call | flops 3000000000 | bytes 1048576 | tf_op jit(solution)/shard_map/apply_terms/pallas_call | solution.py:304
  135.6 1.9 collective-permute-start.15
  137.5 3.6 %collective-permute-start.16 = (f32[64,640]{1,0:T(8,128)S(1)}, f32[64,640]{1,0:T(8,128)S(1)}, u32[]{:S(2)}, u32[]{:S(2)}) collective-permute-start(f32[64,640]{1,0:T(8,128)S(1)} %get-tuple-element.88), channel_id=1, source_target_pairs={{4,0},{8,4},{12,8},{16,12},{20,16},{24,20},{28,24},{5,1},{9,5},{13... | collective-permute-start | bytes 491528 | tf_op jit(solution)/shard_map/ppermute | solution.py:335
  142.2 1.8 collective-permute-done.16
  145.2 2.4 collective-permute-start.17
  147.6 1.3 collective-permute-start.18
  149.8 5.8 %collective-permute-done.18 = f32[192,128]{1,0:T(8,128)S(1)} collective-permute-done((f32[192,128]{1,0:T(8,128)S(1)}, f32[192,128]{1,0:T(8,128)S(1)}, u32[]{:S(2)}, u32[]{:S(2)}) %collective-permute-start.18) | collective-permute-done | bytes 98336 | tf_op jit(solution)/shard_map/ppermute | solution.py:335
  156.6 10.3 %apply_terms.5 = (f32[192,640]{1,0:T(8,128)}, f32[8,128]{1,0:T(8,128)}) custom-call(f32[192,768]{1,0:T(8,128)} %maximum_add_fusion.refs_0_, bf16[8,256,256]{2,1,0:T(8,128)(2,1)} %get-tuple-element.26.refs_1_, bf16[8,256,256]{2,1,0:T(8,128)(2,1)} %get-tuple-element.27.refs_2_, bf16[8,256,256]{2,1,0:T(8,128)(2,1)} %get-tuple-element.28.refs_3_, ...), custom_call_target="tpu_custom_call" | custom-call | flops 12000000000 | bytes 4194304 | tf_op jit(solution)/shard_map/apply_terms/pallas_call | solution.py:304
  167.9 2.9 %collective-permute-start.28 = (f32[64,640]{1,0:T(8,128)S(1)}, f32[64,640]{1,0:T(8,128)S(1)}, u32[]{:S(2)}, u32[]{:S(2)}) collective-permute-start(f32[64,640]{1,0:T(8,128)S(1)} %get-tuple-element.78), channel_id=1, source_target_pairs={{0,4},{4,8},{8,12},{12,16},{16,20},{20,24},{24,28},{1,5},{5,9},{9,... | collective-permute-start | bytes 491528 | tf_op jit(solution)/shard_map/ppermute | solution.py:330
  170.9 2.8 %collective-permute-start.29 = (f32[64,640]{1,0:T(8,128)S(1)}, f32[64,640]{1,0:T(8,128)S(1)}, u32[]{:S(2)}, u32[]{:S(2)}) collective-permute-start(f32[64,640]{1,0:T(8,128)S(1)} %get-tuple-element.79), channel_id=1, source_target_pairs={{4,0},{8,4},{12,8},{16,12},{20,16},{24,20},{28,24},{5,1},{9,5},{13... | collective-permute-start | bytes 491528 | tf_op jit(solution)/shard_map/ppermute | solution.py:335
  174.6 1.9 collective-permute-done.29
  177.8 4.2 %collective-permute-start.30 = (f32[192,128]{1,0:T(8,128)S(1)}, f32[192,128]{1,0:T(8,128)S(1)}, u32[]{:S(2)}, u32[]{:S(2)}) collective-permute-start(f32[192,128]{1,0:T(8,128)S(1)} %get-tuple-element.73), channel_id=1, source_target_pairs={{0,1},{1,2},{2,3},{4,5},{5,6},{6,7},{8,9},{9,10},{10,11},{12,13},{... | collective-permute-start | bytes 294920 | tf_op jit(solution)/shard_map/ppermute | solution.py:330
  182.0 1.3 collective-permute-start.31
  183.3 2.6 collective-permute-start.24
  186.0 2.5 collective-permute-done.31
  189.8 2.1 collective-permute-start.19
  192.7 6.8 %collective-permute-done.24 = f32[1,128,512]{2,1,0:T(8,128)S(1)} collective-permute-done((f32[1,128,512]{2,1,0:T(8,128)S(1)}, f32[1,128,512]{2,1,0:T(8,128)S(1)}, u32[]{:S(2)}, u32[]{:S(2)}) %collective-permute-start.24) | collective-permute-done | bytes 262176 | tf_op jit(solution)/shard_map/ppermute | solution.py:340
  201.8 2.5 collective-permute-done.21
  204.3 2.0 collective-permute-start.22
  206.3 15.0 %collective-permute-done.22 = f32[4,8,128]{2,1,0:T(8,128)S(1)} collective-permute-done((f32[4,8,128]{2,1,0:T(8,128)S(1)}, f32[4,8,128]{2,1,0:T(8,128)S(1)}, u32[]{:S(2)}, u32[]{:S(2)}) %collective-permute-start.22) | collective-permute-done | bytes 16416 | tf_op jit(solution)/shard_map/ppermute | solution.py:340
  221.3 2.9 %collective-permute-start.32 = (f32[1,128,512]{2,1,0:T(8,128)S(1)}, f32[1,128,512]{2,1,0:T(8,128)S(1)}, u32[]{:S(2)}, u32[]{:S(2)}) collective-permute-start(f32[1,128,512]{2,1,0:T(8,128)S(1)} %get-tuple-element.62), channel_id=1, source_target_pairs={{0,2},{1,3},{2,0},{3,1},{4,6},{5,7},{6,4},{7,5},{8,10},{9,11},{10,... | collective-permute-start | bytes 786440 | tf_op jit(solution)/shard_map/ppermute | solution.py:340
  224.2 6.8 %collective-permute-done.23 = f32[4,8,128]{2,1,0:T(8,128)S(1)} collective-permute-done((f32[4,8,128]{2,1,0:T(8,128)S(1)}, f32[4,8,128]{2,1,0:T(8,128)S(1)}, u32[]{:S(2)}, u32[]{:S(2)}) %collective-permute-start.23) | collective-permute-done | bytes 16416 | tf_op jit(solution)/shard_map/ppermute | solution.py:340
  238.0 2.1 collective-permute-start.33
  240.1 12.4 %collective-permute-done.27 = f32[2,128,512]{2,1,0:T(8,128)S(1)} collective-permute-done((f32[2,128,512]{2,1,0:T(8,128)S(1)}, f32[2,128,512]{2,1,0:T(8,128)S(1)}, u32[]{:S(2)}, u32[]{:S(2)}) %collective-permute-start.27) | collective-permute-done | bytes 524320 | tf_op jit(solution)/shard_map/ppermute | solution.py:340
  252.8 10.0 %collective-permute-done.33 = f32[2,128,512]{2,1,0:T(8,128)S(1)} collective-permute-done((f32[2,128,512]{2,1,0:T(8,128)S(1)}, f32[2,128,512]{2,1,0:T(8,128)S(1)}, u32[]{:S(2)}, u32[]{:S(2)}) %collective-permute-start.33) | collective-permute-done | bytes 524320 | tf_op jit(solution)/shard_map/ppermute | solution.py:340
  (121 shorter events, 28.7 us)
Async XLA Ops:
  1.7 11.8 %collective-permute-start = (f32[32,2048]{1,0:T(8,128)S(1)}, f32[32,2048]{1,0:T(8,128)S(1)}, u32[]{:S(2)}, u32[]{:S(2)}) collective-permute-start(f32[32,2048]{1,0:T(8,128)S(1)} %get-tuple-element.61), channel_id=1, source_target_pairs={{0,4},{4,8},{8,12},{12,16},{16,20},{20,24},{24,28},{1,5},{5,9},{9,... | collective-permute-start | bytes 786440 | tf_op jit(solution)/shard_map/ppermute | solution.py:330
  3.6 9.9 %collective-permute-start.1 = (f32[32,2048]{1,0:T(8,128)S(1)}, f32[32,2048]{1,0:T(8,128)S(1)}, u32[]{:S(2)}, u32[]{:S(2)}) collective-permute-start(f32[32,2048]{1,0:T(8,128)S(1)} %get-tuple-element.60), channel_id=1, source_target_pairs={{4,0},{8,4},{12,8},{16,12},{20,16},{24,20},{28,24},{5,1},{9,5},{13... | collective-permute-start | bytes 786440 | tf_op jit(solution)/shard_map/ppermute | solution.py:335
  13.5 0.7 copy-start.8
  13.5 0.8 copy-start.9
  26.2 7.9 %collective-permute-start.2 = (f32[32,2048]{1,0:T(8,128)}, f32[32,2048]{1,0:T(8,128)S(1)}, u32[]{:S(2)}, u32[]{:S(2)}) collective-permute-start(f32[32,2048]{1,0:T(8,128)} %get-tuple-element.24), channel_id=1, source_target_pairs={{0,4},{4,8},{8,12},{12,16},{16,20},{20,24},{24,28},{1,5},{5,9},{9,... | collective-permute-start | bytes 786440 | tf_op jit(solution)/shard_map/ppermute | solution.py:330
  28.4 8.5 %collective-permute-start.3 = (f32[32,2048]{1,0:T(8,128)}, f32[32,2048]{1,0:T(8,128)S(1)}, u32[]{:S(2)}, u32[]{:S(2)}) collective-permute-start(f32[32,2048]{1,0:T(8,128)} %get-tuple-element.25), channel_id=1, source_target_pairs={{4,0},{8,4},{12,8},{16,12},{20,16},{24,20},{28,24},{5,1},{9,5},{13... | collective-permute-start | bytes 786440 | tf_op jit(solution)/shard_map/ppermute | solution.py:335
  38.2 16.1 %copy-start.7 = (f32[2,4,256]{2,1,0:T(4,128)S(1)}, f32[2,4,256]{2,1,0:T(4,128)}, u32[]{:S(2)}) copy-start(f32[2,4,256]{2,1,0:T(4,128)} %pad_maximum_fusion.19.base_ref) | copy-start | bytes 24580
  38.3 13.3 %collective-permute-start.4 = (f32[128,1024]{1,0:T(8,128)S(1)}, f32[128,1024]{1,0:T(8,128)S(1)}, u32[]{:S(2)}, u32[]{:S(2)}) collective-permute-start(f32[128,1024]{1,0:T(8,128)S(1)} %pad_maximum_fusion.7), channel_id=1, source_target_pairs={{0,1},{1,0},{2,3},{3,2},{4,5},{5,4},{6,7},{7,6},{8,9},{9,8},{10,11... | collective-permute-start | bytes 1572872 | tf_op jit(solution)/shard_map/ppermute | solution.py:340
  51.7 26.8 %collective-permute-start.5 = (f32[128,512]{1,0:T(8,128)S(1)}, f32[128,512]{1,0:T(8,128)}, u32[]{:S(2)}, u32[]{:S(2)}) collective-permute-start(f32[128,512]{1,0:T(8,128)S(1)} %constant_dynamic-slice_fusion.4), channel_id=1, source_target_pairs={{0,2},{1,3},{2,0},{3,1},{4,6},{5,7},{6,4},{7,5},{8,10},{9,11},{10,... | collective-permute-start | bytes 786440 | tf_op jit(solution)/shard_map/ppermute | solution.py:340
  54.4 27.2 %collective-permute-start.10 = (f32[2,4,256]{2,1,0:T(4,128)S(1)}, f32[2,4,256]{2,1,0:T(4,128)S(1)}, u32[]{:S(2)}, u32[]{:S(2)}) collective-permute-start(f32[2,4,256]{2,1,0:T(4,128)S(1)} %copy-done.7), channel_id=1, source_target_pairs={{0,1},{1,0},{2,3},{3,2},{4,5},{5,4},{6,7},{7,6},{8,9},{9,8},{10,11... | collective-permute-start | bytes 24584 | tf_op jit(solution)/shard_map/ppermute | solution.py:340
  55.9 22.6 %copy-start = (f32[128,2048]{1,0:T(8,128)S(1)}, f32[128,2048]{1,0:T(8,128)}, u32[]{:S(2)}) copy-start(f32[128,2048]{1,0:T(8,128)} %est.1) | copy-start | bytes 3145732
  58.8 70.6 %collective-permute-start.12 = (f32[2,128,512]{2,1,0:T(8,128)S(1)}, f32[2,128,512]{2,1,0:T(8,128)}, u32[]{:S(2)}, u32[]{:S(2)}) collective-permute-start(f32[2,128,512]{2,1,0:T(8,128)S(1)} %get-tuple-element.40), channel_id=1, source_target_pairs={{0,3},{1,2},{2,1},{3,0},{4,7},{5,6},{6,5},{7,4},{8,11},{9,10},{10,... | collective-permute-start | bytes 1572872 | tf_op jit(solution)/shard_map/ppermute | solution.py:340
  59.1 61.9 %collective-permute-start.13 = (f32[2,128,512]{2,1,0:T(8,128)}, f32[2,128,512]{2,1,0:T(8,128)}, u32[]{:S(2)}, u32[]{:S(2)}) collective-permute-start(f32[2,128,512]{2,1,0:T(8,128)} %get-tuple-element.41), channel_id=1, source_target_pairs={{0,1},{1,0},{2,3},{3,2},{4,5},{5,4},{6,7},{7,6},{8,9},{9,8},{10,11... | collective-permute-start | bytes 1572872 | tf_op jit(solution)/shard_map/ppermute | solution.py:340
  59.8 61.2 %collective-permute-start.14 = (f32[2,128,512]{2,1,0:T(8,128)S(1)}, f32[2,128,512]{2,1,0:T(8,128)}, u32[]{:S(2)}, u32[]{:S(2)}) collective-permute-start(f32[2,128,512]{2,1,0:T(8,128)S(1)} %get-tuple-element.38), channel_id=1, source_target_pairs={{0,2},{1,3},{2,0},{3,1},{4,6},{5,7},{6,4},{7,5},{8,10},{9,11},{10,... | collective-permute-start | bytes 1572872 | tf_op jit(solution)/shard_map/ppermute | solution.py:340
  79.6 4.4 %collective-permute-start.7 = (f32[32,512]{1,0:T(8,128)S(1)}, f32[32,512]{1,0:T(8,128)S(1)}, u32[]{:S(2)}, u32[]{:S(2)}) collective-permute-start(f32[32,512]{1,0:T(8,128)S(1)} %get-tuple-element.94), channel_id=1, source_target_pairs={{4,0},{8,4},{12,8},{16,12},{20,16},{24,20},{28,24},{5,1},{9,5},{13... | collective-permute-start | bytes 196616 | tf_op jit(solution)/shard_map/ppermute | solution.py:335
  81.6 5.6 %collective-permute-start.6 = (f32[32,512]{1,0:T(8,128)S(1)}, f32[32,512]{1,0:T(8,128)S(1)}, u32[]{:S(2)}, u32[]{:S(2)}) collective-permute-start(f32[32,512]{1,0:T(8,128)S(1)} %get-tuple-element.93), channel_id=1, source_target_pairs={{0,4},{4,8},{8,12},{12,16},{16,20},{20,24},{24,28},{1,5},{5,9},{9,... | collective-permute-start | bytes 196616 | tf_op jit(solution)/shard_map/ppermute | solution.py:330
  84.0 28.7 %collective-permute-start.11 = (f32[4,4,256]{2,1,0:T(4,128)S(1)}, f32[4,4,256]{2,1,0:T(4,128)S(1)}, u32[]{:S(2)}, u32[]{:S(2)}) collective-permute-start(f32[4,4,256]{2,1,0:T(4,128)S(1)} %pad_maximum_fusion.17), channel_id=1, source_target_pairs={{0,2},{1,3},{2,0},{3,1},{4,6},{5,7},{6,4},{7,5},{8,10},{9,11},{10,... | collective-permute-start | bytes 49160 | tf_op jit(solution)/shard_map/ppermute | solution.py:340
  87.2 32.9 %collective-permute-start.9 = (f32[192,128]{1,0:T(8,128)S(1)}, f32[192,128]{1,0:T(8,128)S(1)}, u32[]{:S(2)}, u32[]{:S(2)}) collective-permute-start(f32[192,128]{1,0:T(8,128)S(1)} %get-tuple-element.90), channel_id=1, source_target_pairs={{1,0},{2,1},{3,2},{5,4},{6,5},{7,6},{9,8},{10,9},{11,10},{13,12},{... | collective-permute-start | bytes 294920 | tf_op jit(solution)/shard_map/ppermute | solution.py:335
  112.8 7.3 %collective-permute-start.8 = (f32[192,128]{1,0:T(8,128)S(1)}, f32[192,128]{1,0:T(8,128)S(1)}, u32[]{:S(2)}, u32[]{:S(2)}) collective-permute-start(f32[192,128]{1,0:T(8,128)S(1)} %get-tuple-element.89), channel_id=1, source_target_pairs={{0,1},{1,2},{2,3},{4,5},{5,6},{6,7},{8,9},{9,10},{10,11},{12,13},{... | collective-permute-start | bytes 294920 | tf_op jit(solution)/shard_map/ppermute | solution.py:330
  120.1 9.3 %copy-start.1 = (f32[192,128]{1,0:T(8,128)}, f32[192,128]{1,0:T(8,128)S(1)}, u32[]{:S(2)}) copy-start(f32[192,128]{1,0:T(8,128)S(1)} %collective-permute-done.9) | copy-start | bytes 294916
  120.1 9.3 %copy-start.3 = (f32[192,128]{1,0:T(8,128)}, f32[192,128]{1,0:T(8,128)S(1)}, u32[]{:S(2)}) copy-start(f32[192,128]{1,0:T(8,128)S(1)} %collective-permute-done.8) | copy-start | bytes 294916
  135.6 6.6 %collective-permute-start.15 = (f32[64,640]{1,0:T(8,128)S(1)}, f32[64,640]{1,0:T(8,128)S(1)}, u32[]{:S(2)}, u32[]{:S(2)}) collective-permute-start(f32[64,640]{1,0:T(8,128)S(1)} %get-tuple-element.87), channel_id=1, source_target_pairs={{0,4},{4,8},{8,12},{12,16},{16,20},{20,24},{24,28},{1,5},{5,9},{9,... | collective-permute-start | bytes 491528 | tf_op jit(solution)/shard_map/ppermute | solution.py:330
  137.5 6.5 %collective-permute-start.16 = (f32[64,640]{1,0:T(8,128)S(1)}, f32[64,640]{1,0:T(8,128)S(1)}, u32[]{:S(2)}, u32[]{:S(2)}) collective-permute-start(f32[64,640]{1,0:T(8,128)S(1)} %get-tuple-element.88), channel_id=1, source_target_pairs={{4,0},{8,4},{12,8},{16,12},{20,16},{24,20},{28,24},{5,1},{9,5},{13... | collective-permute-start | bytes 491528 | tf_op jit(solution)/shard_map/ppermute | solution.py:335
  141.2 14.5 %copy-start.2 = (f32[192,128]{1,0:T(8,128)S(1)}, f32[192,128]{1,0:T(8,128)}, u32[]{:S(2)}) copy-start(f32[192,128]{1,0:T(8,128)} %copy-done.1) | copy-start | bytes 294916
  141.2 14.5 %copy-start.4 = (f32[192,128]{1,0:T(8,128)S(1)}, f32[192,128]{1,0:T(8,128)}, u32[]{:S(2)}) copy-start(f32[192,128]{1,0:T(8,128)} %copy-done.3) | copy-start | bytes 294916
  145.2 4.6 %collective-permute-start.17 = (f32[192,128]{1,0:T(8,128)S(1)}, f32[192,128]{1,0:T(8,128)S(1)}, u32[]{:S(2)}, u32[]{:S(2)}) collective-permute-start(f32[192,128]{1,0:T(8,128)S(1)} %get-tuple-element.82), channel_id=1, source_target_pairs={{0,1},{1,2},{2,3},{4,5},{5,6},{6,7},{8,9},{9,10},{10,11},{12,13},{... | collective-permute-start | bytes 294920 | tf_op jit(solution)/shard_map/ppermute | solution.py:330
  147.6 8.0 %collective-permute-start.18 = (f32[192,128]{1,0:T(8,128)S(1)}, f32[192,128]{1,0:T(8,128)S(1)}, u32[]{:S(2)}, u32[]{:S(2)}) collective-permute-start(f32[192,128]{1,0:T(8,128)S(1)} %get-tuple-element.83), channel_id=1, source_target_pairs={{1,0},{2,1},{3,2},{5,4},{6,5},{7,6},{9,8},{10,9},{11,10},{13,12},{... | collective-permute-start | bytes 294920 | tf_op jit(solution)/shard_map/ppermute | solution.py:335
  167.9 6.6 %collective-permute-start.28 = (f32[64,640]{1,0:T(8,128)S(1)}, f32[64,640]{1,0:T(8,128)S(1)}, u32[]{:S(2)}, u32[]{:S(2)}) collective-permute-start(f32[64,640]{1,0:T(8,128)S(1)} %get-tuple-element.78), channel_id=1, source_target_pairs={{0,4},{4,8},{8,12},{12,16},{16,20},{20,24},{24,28},{1,5},{5,9},{9,... | collective-permute-start | bytes 491528 | tf_op jit(solution)/shard_map/ppermute | solution.py:330
  170.9 5.6 %collective-permute-start.29 = (f32[64,640]{1,0:T(8,128)S(1)}, f32[64,640]{1,0:T(8,128)S(1)}, u32[]{:S(2)}, u32[]{:S(2)}) collective-permute-start(f32[64,640]{1,0:T(8,128)S(1)} %get-tuple-element.79), channel_id=1, source_target_pairs={{4,0},{8,4},{12,8},{16,12},{20,16},{24,20},{28,24},{5,1},{9,5},{13... | collective-permute-start | bytes 491528 | tf_op jit(solution)/shard_map/ppermute | solution.py:335
  177.8 8.3 %collective-permute-start.30 = (f32[192,128]{1,0:T(8,128)S(1)}, f32[192,128]{1,0:T(8,128)S(1)}, u32[]{:S(2)}, u32[]{:S(2)}) collective-permute-start(f32[192,128]{1,0:T(8,128)S(1)} %get-tuple-element.73), channel_id=1, source_target_pairs={{0,1},{1,2},{2,3},{4,5},{5,6},{6,7},{8,9},{9,10},{10,11},{12,13},{... | collective-permute-start | bytes 294920 | tf_op jit(solution)/shard_map/ppermute | solution.py:330
  182.0 6.5 %collective-permute-start.31 = (f32[192,128]{1,0:T(8,128)S(1)}, f32[192,128]{1,0:T(8,128)S(1)}, u32[]{:S(2)}, u32[]{:S(2)}) collective-permute-start(f32[192,128]{1,0:T(8,128)S(1)} %get-tuple-element.74), channel_id=1, source_target_pairs={{1,0},{2,1},{3,2},{5,4},{6,5},{7,6},{9,8},{10,9},{11,10},{13,12},{... | collective-permute-start | bytes 294920 | tf_op jit(solution)/shard_map/ppermute | solution.py:335
  183.3 16.2 %collective-permute-start.24 = (f32[1,128,512]{2,1,0:T(8,128)S(1)}, f32[1,128,512]{2,1,0:T(8,128)S(1)}, u32[]{:S(2)}, u32[]{:S(2)}) collective-permute-start(f32[1,128,512]{2,1,0:T(8,128)S(1)} %get-tuple-element.91), channel_id=1, source_target_pairs={{0,2},{1,3},{2,0},{3,1},{4,6},{5,7},{6,4},{7,5},{8,10},{9,11},{10,... | collective-permute-start | bytes 786440 | tf_op jit(solution)/shard_map/ppermute | solution.py:340
  186.0 3.7 %copy-start.5 = (f32[8,128]{1,0:T(8,128)S(1)}, f32[8,128]{1,0:T(8,128)}, u32[]{:S(2)}) copy-start(f32[8,128]{1,0:T(8,128)} %get-tuple-element.32) | copy-start | bytes 12292
  186.0 3.7 %copy-start.6 = (f32[8,128]{1,0:T(8,128)S(1)}, f32[8,128]{1,0:T(8,128)}, u32[]{:S(2)}) copy-start(f32[8,128]{1,0:T(8,128)} %get-tuple-element.34) | copy-start | bytes 12292
  189.8 3.0 %collective-permute-start.19 = (f32[4,8,128]{2,1,0:T(8,128)S(1)}, f32[4,8,128]{2,1,0:T(8,128)S(1)}, u32[]{:S(2)}, u32[]{:S(2)}) collective-permute-start(f32[4,8,128]{2,1,0:T(8,128)S(1)} %pad_maximum_fusion.18), channel_id=1, source_target_pairs={{0,4},{4,0},{8,12},{12,8},{16,20},{20,16},{24,28},{28,24},{1,5},{5... | collective-permute-start | bytes 49160 | tf_op jit(solution)/shard_map/ppermute | solution.py:340
  192.7 7.6 %collective-permute-start.20 = (f32[4,8,128]{2,1,0:T(8,128)S(1)}, f32[4,8,128]{2,1,0:T(8,128)S(1)}, u32[]{:S(2)}, u32[]{:S(2)}) collective-permute-start(f32[4,8,128]{2,1,0:T(8,128)S(1)} %fusion.5), channel_id=1, source_target_pairs={{0,8},{4,12},{8,0},{12,4},{16,24},{20,28},{24,16},{28,20},{1,9},{5... | collective-permute-start | bytes 49160 | tf_op jit(solution)/shard_map/ppermute | solution.py:340
  200.4 37.4 %collective-permute-start.25 = (f32[2,128,512]{2,1,0:T(8,128)}, f32[2,128,512]{2,1,0:T(8,128)S(1)}, u32[]{:S(2)}, u32[]{:S(2)}) collective-permute-start(f32[2,128,512]{2,1,0:T(8,128)} %pad_maximum_fusion.8), channel_id=1, source_target_pairs={{0,1},{1,0},{2,3},{3,2},{4,5},{5,4},{6,7},{7,6},{8,9},{9,8},{10,11... | collective-permute-start | bytes 1572872 | tf_op jit(solution)/shard_map/ppermute | solution.py:340
  200.4 3.9 %collective-permute-start.21 = (f32[4,8,128]{2,1,0:T(8,128)S(1)}, f32[4,8,128]{2,1,0:T(8,128)S(1)}, u32[]{:S(2)}, u32[]{:S(2)}) collective-permute-start(f32[4,8,128]{2,1,0:T(8,128)S(1)} %fusion.15), channel_id=1, source_target_pairs={{0,16},{4,20},{8,24},{12,28},{16,0},{20,4},{24,8},{28,12},{1,17},{... | collective-permute-start | bytes 49160 | tf_op jit(solution)/shard_map/ppermute | solution.py:340
  201.4 36.2 %collective-permute-start.26 = (f32[1,128,512]{2,1,0:T(8,128)S(1)}, f32[1,128,512]{2,1,0:T(8,128)S(1)}, u32[]{:S(2)}, u32[]{:S(2)}) collective-permute-start(f32[1,128,512]{2,1,0:T(8,128)S(1)} %get-tuple-element.63), channel_id=1, source_target_pairs={{0,2},{1,3},{2,0},{3,1},{4,6},{5,7},{6,4},{7,5},{8,10},{9,11},{10,... | collective-permute-start | bytes 786440 | tf_op jit(solution)/shard_map/ppermute | solution.py:340
  204.3 17.0 %collective-permute-start.22 = (f32[4,8,128]{2,1,0:T(8,128)S(1)}, f32[4,8,128]{2,1,0:T(8,128)S(1)}, u32[]{:S(2)}, u32[]{:S(2)}) collective-permute-start(f32[4,8,128]{2,1,0:T(8,128)S(1)} %add.206), channel_id=1, source_target_pairs={{0,1},{1,0},{2,3},{3,2},{4,5},{5,4},{6,7},{7,6},{8,9},{9,8},{10,11... | collective-permute-start | bytes 49160 | tf_op jit(solution)/shard_map/ppermute | solution.py:340
  221.3 9.7 %collective-permute-start.23 = (f32[4,8,128]{2,1,0:T(8,128)S(1)}, f32[4,8,128]{2,1,0:T(8,128)S(1)}, u32[]{:S(2)}, u32[]{:S(2)}) collective-permute-start(f32[4,8,128]{2,1,0:T(8,128)S(1)} %add.207), channel_id=1, source_target_pairs={{0,2},{1,3},{2,0},{3,1},{4,6},{5,7},{6,4},{7,5},{8,10},{9,11},{10,... | collective-permute-start | bytes 49160 | tf_op jit(solution)/shard_map/ppermute | solution.py:340
  221.3 16.6 %collective-permute-start.32 = (f32[1,128,512]{2,1,0:T(8,128)S(1)}, f32[1,128,512]{2,1,0:T(8,128)S(1)}, u32[]{:S(2)}, u32[]{:S(2)}) collective-permute-start(f32[1,128,512]{2,1,0:T(8,128)S(1)} %get-tuple-element.62), channel_id=1, source_target_pairs={{0,2},{1,3},{2,0},{3,1},{4,6},{5,7},{6,4},{7,5},{8,10},{9,11},{10,... | collective-permute-start | bytes 786440 | tf_op jit(solution)/shard_map/ppermute | solution.py:340
  237.7 14.9 %collective-permute-start.27 = (f32[2,128,512]{2,1,0:T(8,128)S(1)}, f32[2,128,512]{2,1,0:T(8,128)S(1)}, u32[]{:S(2)}, u32[]{:S(2)}) collective-permute-start(f32[2,128,512]{2,1,0:T(8,128)S(1)} %pad_maximum_fusion.9), channel_id=1, source_target_pairs={{0,1},{1,0},{2,3},{3,2},{4,5},{5,4},{6,7},{7,6},{8,9},{9,8},{10,11... | collective-permute-start | bytes 1572872 | tf_op jit(solution)/shard_map/ppermute | solution.py:340
  238.0 24.8 %collective-permute-start.33 = (f32[2,128,512]{2,1,0:T(8,128)S(1)}, f32[2,128,512]{2,1,0:T(8,128)S(1)}, u32[]{:S(2)}, u32[]{:S(2)}) collective-permute-start(f32[2,128,512]{2,1,0:T(8,128)S(1)} %pad_maximum_fusion.10), channel_id=1, source_target_pairs={{0,1},{1,0},{2,3},{3,2},{4,5},{5,4},{6,7},{7,6},{8,9},{9,8},{10,11... | collective-permute-start | bytes 1572872 | tf_op jit(solution)/shard_map/ppermute | solution.py:340
where the time goes:
time: 267 us; the launch traced here: 265 us
  waiting for transfers between devices  127 us (48%)
  starting transfers between devices  63.7 us (24%)
  Pallas kernels  41.5 us (16%)
  other arithmetic  16 us (6%)
  local copies, waits for them, and re-layouts  9.52 us (4%)
  between operations  7.24 us (3%)
    ppermute x18, waiting for transfers between devices, swap(): return lax.ppermute(x, axis, [(i, i ^ distance) for i in range(n)])  106 us
    pallas_call x3, Pallas kernels, apply_terms(): pl.pallas_call(functools.partial(apply_kernel, frames, rows, halo, w, gro...  23.9 us
    ppermute x18, starting transfers between devices, swap(): return lax.ppermute(x, axis, [(i, i ^ distance) for i in range(n)])  23.5 us
    ppermute x8, starting transfers between devices, shift_up(): return lax.ppermute(x, axis, [(i, i + 1) for i in range(n - 1)])  20.9 us
    ppermute x8, starting transfers between devices, shift_down(): return lax.ppermute(x, axis, [(i + 1, i) for i in range(n - 1)])  19.3 us
    ppermute x8, waiting for transfers between devices, shift_down(): return lax.ppermute(x, axis, [(i + 1, i) for i in range(n - 1)])  14.8 us
    pallas_call x1, Pallas kernels, first_terms(): pl.pallas_call(functools.partial(first_kernel, frames, rows, halo, w), ou...  11.9 us
    ppermute x8, waiting for transfers between devices, shift_up(): return lax.ppermute(x, axis, [(i, i + 1) for i in range(n - 1)])  7.02 us
  transfers between devices with their start and end apart: 34, of which 20 were waited for; matrix products, arithmetic and copies ran while one was open for 5% of the time, Pallas kernels for 5%

commit v1 on v0

--- a/solution.py
+++ b/solution.py
@@ -6,6 +6,7 @@
 from jax.experimental import pallas as pl
 from jax.experimental.pallas import tpu as pltpu
 from jax.sharding import PartitionSpec as P
+
 
 damping = 0.05
 f32 = jnp.float32
@@ -321,7 +322,6 @@
         cost_estimate=pl.CostEstimate(
             flops=groups * 3 * 10**9, bytes_accessed=groups * 2**20, transcendentals=0
         ),
-        name="apply_terms",
     )(*args)
 
 
@@ -340,7 +340,7 @@
     return lax.ppermute(x, axis, [(i, i ^ distance) for i in range(n)])
 
 
-def body(estimate, observed, weights, column_kernels, row_kernels):
+def steps(estimate, observed, weights, column_kernels, row_kernels):
     n = lax.axis_size("frame")
     me = lax.axis_index("frame")
     strips = lax.axis_size("strip")
@@ -353,9 +353,14 @@
     distances = [1 << k for k in range(n.bit_length() - 1)]
 
     unit = lambda k: k / jnp.sum(k, axis=1, keepdims=True)
-    bases = kernel_bases(unit(column_kernels), unit(row_kernels))
     est_lo = shift_up(estimate[rows - halo :], "strip")
     est_hi = shift_down(estimate[:halo], "strip")
+    taps = jnp.stack([column_kernels, row_kernels])
+    all_taps = [taps]
+    for d in range(1, n):
+        all_taps.append(swap(taps, "frame", d))
+    bases = kernel_bases(unit(column_kernels), unit(row_kernels))
+    all_taps = jnp.concatenate(all_taps, axis=1)
 
     def block_of(x, j):
         return lax.dynamic_slice_in_dim(x, j * w, w, axis=x.ndim - 1)
@@ -367,9 +372,7 @@
     own_mats = setup_matrices(bases, frames, rows, halo)
     top, mid, bot = first_terms(estimate, est_lo, est_hi, own_mats, weights, observed, w)
 
-    all_bases = bases
-    for d in distances:
-        all_bases = jnp.concatenate([all_bases, swap(all_bases, "frame", d)], axis=0)
+    all_bases = kernel_bases(unit(all_taps[0]), unit(all_taps[1]))
     mats = setup_matrices(all_bases, frames, rows, halo)
 
     from_up = shift_up(bot, "strip")
@@ -379,7 +382,7 @@
     )
 
     left = terms
-    for k, d in enumerate(distances):
+    for d in distances:
         bit = (me // d) % 2
         half = left.shape[1] // w // 2
 
@@ -436,18 +439,20 @@
     def own_block(x):
         return x[halo : halo + rows, LANE : LANE + w]
 
+    def fold(x):
+        return jnp.sum(x.reshape(rows * w // (8 * LANE), 8, LANE), axis=0)
+
+    k00_part = fold(k0 * k0)
     carry = apply_terms(k0x, mats, my_weights[: n - 1], 0, halo, final=False)
     part1, stat1 = apply_terms(k0x, mats, my_weights[n - 1 :], n - 1, halo, carry)
     k1x = complete(part1, k0x)
+    k1, k1x = lax.optimization_barrier((own_block(k1x), k1x))
+    k11_part = fold(k1 * k1)
     part2, stat2 = apply_terms(k1x, mats, my_weights, 0, halo)
-    k1 = own_block(k1x)
     k2 = own_block(complete(part2, k1x))
 
-    def fold(x):
-        return jnp.sum(x.reshape(rows * w // (8 * LANE), 8, LANE), axis=0)
-
-    sums = jnp.stack([fold(k0 * k0), stat1, fold(k1 * k1), stat2])
-    for axis, size in (("strip", strips), ("frame", n)):
+    sums = jnp.stack([k00_part, stat1, k11_part, stat2])
+    for axis, size in (("frame", n), ("strip", strips)):
         d = 1
         while d < size:
             sums = sums + swap(sums, axis, d)
@@ -464,6 +469,12 @@
     c1 = alpha0 + alpha1 * (1.0 + beta)
     c2 = alpha0 * alpha1
 
+    def ordered(parts):
+        both = jnp.stack(parts)
+        return jnp.concatenate(
+            [lax.dynamic_index_in_dim(both, me ^ j, 0, keepdims=False) for j in range(n)], axis=1
+        )
+
     def gathered(x):
         parts = [x] + [None] * (n - 1)
         for d in reversed(distances):
@@ -471,18 +482,23 @@
             sent = swap(jnp.stack([parts[i] for i in known]), "frame", d)
             for s, i in enumerate(known):
                 parts[i ^ d] = sent[s]
-        both = jnp.stack(parts)
-        return jnp.concatenate(
-            [lax.dynamic_index_in_dim(both, me ^ j, 0, keepdims=False) for j in range(n)], axis=1
-        )
-
-    g0, g1, g2 = gathered(k0), gathered(k1), gathered(k2)
+        return ordered(parts)
+
+    def gathered_soon(x):
+        parts = [x] + [None] * (n - 1)
+        for i in range(0, n):
+            for d in reversed(distances):
+                if i % (2 * d) == 0:
+                    parts[i + d] = swap(parts[i], "frame", d)
+        return ordered(parts)
+
+    g0, g1, g2 = gathered(k0), gathered(k1), gathered_soon(k2)
     return estimate + c1 * g0 - c2 * g1, g0 - c1 * g1 + c2 * g2
 
 
 def solution(mesh):
     return jax.shard_map(
-        body,
+        steps,
         mesh=mesh,
         in_specs=(
             P("strip", None),

time: 267 us -> 259 us (0.970)
  waiting for transfers between devices: 127 us -> 114 us
  starting transfers between devices: 63.7 us -> 69.9 us
    ppermute x18 -> x20, waiting for transfers between devices: 106 us -> 90.8 us  [swap(): return lax.ppermute(x, axis, [(i, i ^ distance) for i in range(n)])]
    ppermute x8, starting transfers between devices: 20.9 us -> 24.8 us  [shift_up(): return lax.ppermute(x, axis, [(i, i + 1) for i in range(n - 1)])]
    ppermute x18 -> x20, starting transfers between devices: 23.5 us -> 26.7 us  [swap(): return lax.ppermute(x, axis, [(i, i ^ distance) for i in range(n)])]
  transfers between devices with their start and end apart: 34 -> 36, of which waited for: 20 -> 19; matrix products, arithmetic and copies ran while one was open for 5% -> 6% of each run, Pallas kernels for 5% -> 5%
where the time goes in v1:
time: 259 us; the launch traced here: 257 us
  waiting for transfers between devices  114 us (44%)
  starting transfers between devices  69.9 us (27%)
  Pallas kernels  41.5 us (16%)
  other arithmetic  16.3 us (6%)
  local copies, waits for them, and re-layouts  9 us (3%)
  between operations  6.85 us (3%)
    ppermute x20, waiting for transfers between devices, swap(): return lax.ppermute(x, axis, [(i, i ^ distance) for i in range(n)])  90.8 us
    ppermute x20, starting transfers between devices, swap(): return lax.ppermute(x, axis, [(i, i ^ distance) for i in range(n)])  26.7 us
    ppermute x8, starting transfers between devices, shift_up(): return lax.ppermute(x, axis, [(i, i + 1) for i in range(n - 1)])  24.8 us
    pallas_call x3, Pallas kernels, apply_terms(): pl.pallas_call(functools.partial(apply_kernel, frames, rows, halo, w, gro...  23.9 us
    ppermute x8, starting transfers between devices, shift_down(): return lax.ppermute(x, axis, [(i + 1, i) for i in range(n - 1)])  18.5 us
    ppermute x8, waiting for transfers between devices, shift_down(): return lax.ppermute(x, axis, [(i + 1, i) for i in range(n - 1)])  14.8 us
    pallas_call x1, Pallas kernels, first_terms(): pl.pallas_call(functools.partial(first_kernel, frames, rows, halo, w), ou...  11.9 us
    ppermute x8, waiting for transfers between devices, shift_up(): return lax.ppermute(x, axis, [(i, i + 1) for i in range(n - 1)])  8.01 us
  transfers between devices with their start and end apart: 36, of which 19 were waited for; matrix products, arithmetic and copies ran while one was open for 6% of the time, Pallas kernels for 5%

profile of v1, /device:TPU:2, one launch (start us, length us, event | category | flops | bytes accessed | tf_op | source)
XLA Modules:
  0.0 257.3 jit_solution(1671495502810264484)
XLA Ops:
  1.7 1.9 collective-permute-start
  3.6 3.6 %collective-permute-start.1 = (f32[32,2048]{1,0:T(8,128)S(1)}, f32[32,2048]{1,0:T(8,128)S(1)}, u32[]{:S(2)}, u32[]{:S(2)}) collective-permute-start(f32[32,2048]{1,0:T(8,128)S(1)} %get-tuple-element.66), channel_id=1, source_target_pairs={{4,0},{8,4},{12,8},{16,12},{20,16},{24,20},{28,24},{5,1},{9,5},{13... | collective-permute-start | bytes 786440 | tf_op jit(solution)/shard_map/ppermute | solution.py:335
  11.6 2.0 setup_matrices.2
  14.3 11.9 %first_terms.1 = (f32[32,2048]{1,0:T(8,128)}, f32[128,2048]{1,0:T(8,128)}, f32[32,2048]{1,0:T(8,128)}) custom-call(f32[128,2048]{1,0:T(8,128)} %est.1, f32[32,2048]{1,0:T(8,128)} %copy-done.7, f32[32,2048]{1,0:T(8,128)} %copy-done.8, bf16[2,256,256]{2,1,0:T(8,128)(2,1)} %get-tuple-element.21.t_ref, bf16[2,256,256]{2,1,0:T(8,128)(2,1)} %get-tuple-element.22.b_ref, ...), custom_call_target="tpu_custom_call" | custom-call | flops 8000000000 | bytes 8388608 | tf_op jit(solution)/shard_map/first_terms/pallas_call | solution.py:226
  26.3 2.1 collective-permute-start.2
  28.4 3.4 %collective-permute-start.3 = (f32[32,2048]{1,0:T(8,128)}, f32[32,2048]{1,0:T(8,128)S(1)}, u32[]{:S(2)}, u32[]{:S(2)}) collective-permute-start(f32[32,2048]{1,0:T(8,128)} %get-tuple-element.27), channel_id=1, source_target_pairs={{4,0},{8,4},{12,8},{16,12},{20,16},{24,20},{28,24},{5,1},{9,5},{13... | collective-permute-start | bytes 786440 | tf_op jit(solution)/shard_map/ppermute | solution.py:335
  32.9 1.2 collective-permute-done.2
  34.2 2.8 %collective-permute-done.3 = f32[32,2048]{1,0:T(8,128)S(1)} collective-permute-done((f32[32,2048]{1,0:T(8,128)}, f32[32,2048]{1,0:T(8,128)S(1)}, u32[]{:S(2)}, u32[]{:S(2)}) %collective-permute-start.3) | collective-permute-done | bytes 262176 | tf_op jit(solution)/shard_map/ppermute | solution.py:335
  39.1 1.6 collective-permute-start.4
  41.2 2.6 %collective-permute-start.11 = (f32[2,2,65]{2,1,0:T(2,128)S(1)}, f32[2,2,65]{2,1,0:T(2,128)S(1)}, u32[]{:S(2)}, u32[]{:S(2)}) collective-permute-start(f32[2,2,65]{2,1,0:T(2,128)S(1)} %pad_maximum_fusion.21), channel_id=1, source_target_pairs={{0,2},{1,3},{2,0},{3,1},{4,6},{5,7},{6,4},{7,5},{8,10},{9,11},{10,... | collective-permute-start | bytes 3128 | tf_op jit(solution)/shard_map/ppermute | solution.py:340
  43.8 1.4 collective-permute-start.12
  45.2 1.4 constant_dynamic-slice_fusion
  46.8 5.9 %collective-permute-done.10 = f32[2,2,65]{2,1,0:T(2,128)S(1)} collective-permute-done((f32[2,2,65]{2,1,0:T(2,128)S(1)}, f32[2,2,65]{2,1,0:T(2,128)S(1)}, u32[]{:S(2)}, u32[]{:S(2)}) %collective-permute-start.10) | collective-permute-done | bytes 1072 | tf_op jit(solution)/shard_map/ppermute | solution.py:340
  52.7 2.5 collective-permute-start.15
  55.2 1.4 collective-permute-start.13
  56.9 1.8 collective-permute-start.5
  59.2 52.2 %collective-permute-done.5 = f32[128,512]{1,0:T(8,128)S(1)} collective-permute-done((f32[128,512]{1,0:T(8,128)S(1)}, f32[128,512]{1,0:T(8,128)S(1)}, u32[]{:S(2)}, u32[]{:S(2)}) %collective-permute-start.5) | collective-permute-done | bytes 262176 | tf_op jit(solution)/shard_map/ppermute | solution.py:340
  111.5 4.0 %collective-permute-start.6 = (f32[32,512]{1,0:T(8,128)S(1)}, f32[32,512]{1,0:T(8,128)S(1)}, u32[]{:S(2)}, u32[]{:S(2)}) collective-permute-start(f32[32,512]{1,0:T(8,128)S(1)} %get-tuple-element.94), channel_id=1, source_target_pairs={{0,4},{4,8},{8,12},{12,16},{16,20},{20,24},{24,28},{1,5},{5,9},{9,... | collective-permute-start | bytes 196616 | tf_op jit(solution)/shard_map/ppermute | solution.py:330
  115.5 1.9 collective-permute-start.7
  117.5 1.8 collective-permute-done.7
  119.3 3.0 %collective-permute-start.8 = (f32[192,128]{1,0:T(8,128)S(1)}, f32[192,128]{1,0:T(8,128)S(1)}, u32[]{:S(2)}, u32[]{:S(2)}) collective-permute-start(f32[192,128]{1,0:T(8,128)S(1)} %get-tuple-element.90), channel_id=1, source_target_pairs={{0,1},{1,2},{2,3},{4,5},{5,6},{6,7},{8,9},{9,10},{10,11},{12,13},{... | collective-permute-start | bytes 294920 | tf_op jit(solution)/shard_map/ppermute | solution.py:330
  122.3 1.3 collective-permute-start.9
  124.3 3.7 %setup_matrices.3 = (bf16[8,256,256]{2,1,0:T(8,128)(2,1)}, bf16[8,256,256]{2,1,0:T(8,128)(2,1)}, bf16[8,256,256]{2,1,0:T(8,128)(2,1)}, bf16[4,384,256]{2,1,0:T(8,128)(2,1)}) custom-call(f32[8,4,256]{2,1,0:T(4,128)} %pad_maximum_fusion.15.base_ref), custom_call_target="tpu_custom_call" | custom-call | tf_op jit(solution)/shard_map/setup_matrices/pallas_call | solution.py:82
  129.7 8.4 %shard_map.68 = (f32[192,640]{1,0:T(8,128)}, f32[8,128]{1,0:T(8,128)}) custom-call(f32[192,768]{1,0:T(8,128)} %pad_maximum_fusion.6.refs_0_, bf16[8,256,256]{2,1,0:T(8,128)(2,1)} %get-tuple-element.28.refs_1_, bf16[8,256,256]{2,1,0:T(8,128)(2,1)} %get-tuple-element.29.refs_2_, bf16[8,256,256]{2,1,0:T(8,128)(2,1)} %get-tuple-element.30.refs_3_, ...), custom_call_target="tpu_custom_call" | custom-call | flops 8999999488 | bytes 3145728 | tf_op jit(solution)/shard_map/pallas_call | solution.py:305
  138.1 5.2 %shard_map.69 = (f32[192,640]{1,0:T(8,128)}, f32[8,128]{1,0:T(8,128)}) custom-call(f32[192,768]{1,0:T(8,128)} %pad_maximum_fusion.6.refs_0_, bf16[8,256,256]{2,1,0:T(8,128)(2,1)} %get-tuple-element.28.refs_1_, bf16[8,256,256]{2,1,0:T(8,128)(2,1)} %get-tuple-element.29.refs_2_, bf16[8,256,256]{2,1,0:T(8,128)(2,1)} %get-tuple-element.30.refs_3_, ...), custom_call_target="tpu_custom_call" | custom-call | flops 3000000000 | bytes 1048576 | tf_op jit(solution)/shard_map/pallas_call | solution.py:305
  144.3 4.3 %collective-permute-start.16 = (f32[64,640]{1,0:T(8,128)S(1)}, f32[64,640]{1,0:T(8,128)S(1)}, u32[]{:S(2)}, u32[]{:S(2)}) collective-permute-start(f32[64,640]{1,0:T(8,128)S(1)} %get-tuple-element.88), channel_id=1, source_target_pairs={{0,4},{4,8},{8,12},{12,16},{16,20},{20,24},{24,28},{1,5},{5,9},{9,... | collective-permute-start | bytes 491528 | tf_op jit(solution)/shard_map/ppermute | solution.py:330
  148.6 1.9 collective-permute-start.17
  151.0 2.6 %collective-permute-done.17 = f32[64,640]{1,0:T(8,128)S(1)} collective-permute-done((f32[64,640]{1,0:T(8,128)S(1)}, f32[64,640]{1,0:T(8,128)S(1)}, u32[]{:S(2)}, u32[]{:S(2)}) %collective-permute-start.17) | collective-permute-done | bytes 163872 | tf_op jit(solution)/shard_map/ppermute | solution.py:335
  154.8 4.1 %collective-permute-start.18 = (f32[192,128]{1,0:T(8,128)S(1)}, f32[192,128]{1,0:T(8,128)S(1)}, u32[]{:S(2)}, u32[]{:S(2)}) collective-permute-start(f32[192,128]{1,0:T(8,128)S(1)} %get-tuple-element.83), channel_id=1, source_target_pairs={{0,1},{1,2},{2,3},{4,5},{5,6},{6,7},{8,9},{9,10},{10,11},{12,13},{... | collective-permute-start | bytes 294920 | tf_op jit(solution)/shard_map/ppermute | solution.py:330
  158.9 1.5 collective-permute-start.19
  161.1 4.5 %collective-permute-done.19 = f32[192,128]{1,0:T(8,128)S(1)} collective-permute-done((f32[192,128]{1,0:T(8,128)S(1)}, f32[192,128]{1,0:T(8,128)S(1)}, u32[]{:S(2)}, u32[]{:S(2)}) %collective-permute-start.19) | collective-permute-done | bytes 98336 | tf_op jit(solution)/shard_map/ppermute | solution.py:335
  166.6 10.3 %shard_map.70 = (f32[192,640]{1,0:T(8,128)}, f32[8,128]{1,0:T(8,128)}) custom-call(f32[192,768]{1,0:T(8,128)} %copy-done.1, bf16[8,256,256]{2,1,0:T(8,128)(2,1)} %get-tuple-element.28.refs_1_, bf16[8,256,256]{2,1,0:T(8,128)(2,1)} %get-tuple-element.29.refs_2_, bf16[8,256,256]{2,1,0:T(8,128)(2,1)} %get-tuple-element.30.refs_3_, ...), custom_call_target="tpu_custom_call" | custom-call | flops 12000000000 | bytes 4194304 | tf_op jit(solution)/shard_map/pallas_call | solution.py:305
  177.7 2.0 collective-permute-start.20
  179.7 1.7 collective-permute-done.20
  182.1 3.2 %collective-permute-start.21 = (f32[4,8,128]{2,1,0:T(8,128)S(1)}, f32[4,8,128]{2,1,0:T(8,128)S(1)}, u32[]{:S(2)}, u32[]{:S(2)}) collective-permute-start(f32[4,8,128]{2,1,0:T(8,128)S(1)} %fusion.4), channel_id=1, source_target_pairs={{0,2},{1,3},{2,0},{3,1},{4,6},{5,7},{6,4},{7,5},{8,10},{9,11},{10,... | collective-permute-start | bytes 49160 | tf_op jit(solution)/shard_map/ppermute | solution.py:340
  185.3 1.8 collective-permute-done.21
  190.1 2.1 collective-permute-start.29
  192.1 3.5 %collective-permute-start.30 = (f32[64,640]{1,0:T(8,128)S(1)}, f32[64,640]{1,0:T(8,128)S(1)}, u32[]{:S(2)}, u32[]{:S(2)}) collective-permute-start(f32[64,640]{1,0:T(8,128)S(1)} %get-tuple-element.80), channel_id=1, source_target_pairs={{4,0},{8,4},{12,8},{16,12},{20,16},{24,20},{28,24},{5,1},{9,5},{13... | collective-permute-start | bytes 491528 | tf_op jit(solution)/shard_map/ppermute | solution.py:335
  195.7 3.9 %collective-permute-start.24 = (f32[4,8,128]{2,1,0:T(8,128)S(1)}, f32[4,8,128]{2,1,0:T(8,128)S(1)}, u32[]{:S(2)}, u32[]{:S(2)}) collective-permute-start(f32[4,8,128]{2,1,0:T(8,128)S(1)} %add.211), channel_id=1, source_target_pairs={{0,16},{4,20},{8,24},{12,28},{16,0},{20,4},{24,8},{28,12},{1,17},{... | collective-permute-start | bytes 49160 | tf_op jit(solution)/shard_map/ppermute | solution.py:340
  201.9 1.8 collective-permute-start.27
  204.1 3.3 %collective-permute-start.31 = (f32[192,128]{1,0:T(8,128)S(1)}, f32[192,128]{1,0:T(8,128)S(1)}, u32[]{:S(2)}, u32[]{:S(2)}) collective-permute-start(f32[192,128]{1,0:T(8,128)S(1)} %get-tuple-element.74), channel_id=1, source_target_pairs={{0,1},{1,2},{2,3},{4,5},{5,6},{6,7},{8,9},{9,10},{10,11},{12,13},{... | collective-permute-start | bytes 294920 | tf_op jit(solution)/shard_map/ppermute | solution.py:330
  207.4 1.3 collective-permute-start.32
  214.9 5.8 %collective-permute-done.31 = f32[192,128]{1,0:T(8,128)S(1)} collective-permute-done((f32[192,128]{1,0:T(8,128)S(1)}, f32[192,128]{1,0:T(8,128)S(1)}, u32[]{:S(2)}, u32[]{:S(2)}) %collective-permute-start.31) | collective-permute-done | bytes 98336 | tf_op jit(solution)/shard_map/ppermute | solution.py:330
  220.7 2.2 collective-permute-done.32
  224.7 1.8 collective-permute-start.28
  226.8 10.5 %collective-permute-done.34 = f32[128,512]{1,0:T(8,128)S(1)} collective-permute-done((f32[128,512]{1,0:T(8,128)S(1)}, f32[128,512]{1,0:T(8,128)S(1)}, u32[]{:S(2)}, u32[]{:S(2)}) %collective-permute-start.34) | collective-permute-done | bytes 262176 | tf_op jit(solution)/shard_map/ppermute | solution.py:340
  237.6 13.2 %collective-permute-done.33 = f32[128,512]{1,0:T(8,128)S(1)} collective-permute-done((f32[128,512]{1,0:T(8,128)S(1)}, f32[128,512]{1,0:T(8,128)S(1)}, u32[]{:S(2)}, u32[]{:S(2)}) %collective-permute-start.33) | collective-permute-done | bytes 262176 | tf_op jit(solution)/shard_map/ppermute | solution.py:340
  250.7 3.8 %collective-permute-done.35 = f32[128,512]{1,0:T(8,128)S(1)} collective-permute-done((f32[128,512]{1,0:T(8,128)S(1)}, f32[128,512]{1,0:T(8,128)S(1)}, u32[]{:S(2)}, u32[]{:S(2)}) %collective-permute-start.35) | collective-permute-done | bytes 262176 | tf_op jit(solution)/shard_map/ppermute | solution.py:340
  (136 shorter events, 30.2 us)
Async XLA Ops:
  1.7 11.8 %collective-permute-start = (f32[32,2048]{1,0:T(8,128)S(1)}, f32[32,2048]{1,0:T(8,128)S(1)}, u32[]{:S(2)}, u32[]{:S(2)}) collective-permute-start(f32[32,2048]{1,0:T(8,128)S(1)} %get-tuple-element.67), channel_id=1, source_target_pairs={{0,4},{4,8},{8,12},{12,16},{16,20},{20,24},{24,28},{1,5},{5,9},{9,... | collective-permute-start | bytes 786440 | tf_op jit(solution)/shard_map/ppermute | solution.py:330
  3.6 9.9 %collective-permute-start.1 = (f32[32,2048]{1,0:T(8,128)S(1)}, f32[32,2048]{1,0:T(8,128)S(1)}, u32[]{:S(2)}, u32[]{:S(2)}) collective-permute-start(f32[32,2048]{1,0:T(8,128)S(1)} %get-tuple-element.66), channel_id=1, source_target_pairs={{4,0},{8,4},{12,8},{16,12},{20,16},{24,20},{28,24},{5,1},{9,5},{13... | collective-permute-start | bytes 786440 | tf_op jit(solution)/shard_map/ppermute | solution.py:335
  13.5 0.7 copy-start.7
  13.5 0.8 copy-start.8
  26.3 7.9 %collective-permute-start.2 = (f32[32,2048]{1,0:T(8,128)}, f32[32,2048]{1,0:T(8,128)S(1)}, u32[]{:S(2)}, u32[]{:S(2)}) collective-permute-start(f32[32,2048]{1,0:T(8,128)} %get-tuple-element.26), channel_id=1, source_target_pairs={{0,4},{4,8},{8,12},{12,16},{16,20},{20,24},{24,28},{1,5},{5,9},{9,... | collective-permute-start | bytes 786440 | tf_op jit(solution)/shard_map/ppermute | solution.py:330
  28.4 8.6 %collective-permute-start.3 = (f32[32,2048]{1,0:T(8,128)}, f32[32,2048]{1,0:T(8,128)S(1)}, u32[]{:S(2)}, u32[]{:S(2)}) collective-permute-start(f32[32,2048]{1,0:T(8,128)} %get-tuple-element.27), channel_id=1, source_target_pairs={{4,0},{8,4},{12,8},{16,12},{20,16},{24,20},{28,24},{5,1},{9,5},{13... | collective-permute-start | bytes 786440 | tf_op jit(solution)/shard_map/ppermute | solution.py:335
  38.2 2.5 copy-start.5
  38.2 2.5 copy-start.6
  38.2 7.0 %copy-start.2 = (f32[2,128,2048]{2,1,0:T(8,128)S(1)}, f32[2,128,2048]{2,1,0:T(8,128)}, u32[]{:S(2)}) copy-start(f32[2,128,2048]{2,1,0:T(8,128)} %w_hbm.1) | copy-start | bytes 6291460
  39.1 17.6 %collective-permute-start.4 = (f32[128,1024]{1,0:T(8,128)}, f32[128,1024]{1,0:T(8,128)S(1)}, u32[]{:S(2)}, u32[]{:S(2)}) collective-permute-start(f32[128,1024]{1,0:T(8,128)} %pad_maximum_fusion.7), channel_id=1, source_target_pairs={{0,1},{1,0},{2,3},{3,2},{4,5},{5,4},{6,7},{7,6},{8,9},{9,8},{10,11... | collective-permute-start | bytes 1572872 | tf_op jit(solution)/shard_map/ppermute | solution.py:340
  40.7 12.0 %collective-permute-start.10 = (f32[2,2,65]{2,1,0:T(2,128)S(1)}, f32[2,2,65]{2,1,0:T(2,128)S(1)}, u32[]{:S(2)}, u32[]{:S(2)}) collective-permute-start(f32[2,2,65]{2,1,0:T(2,128)S(1)} %pad_maximum_fusion.21), channel_id=1, source_target_pairs={{0,1},{1,0},{2,3},{3,2},{4,5},{5,4},{6,7},{7,6},{8,9},{9,8},{10,11... | collective-permute-start | bytes 3128 | tf_op jit(solution)/shard_map/ppermute | solution.py:340
  41.2 14.0 %collective-permute-start.11 = (f32[2,2,65]{2,1,0:T(2,128)S(1)}, f32[2,2,65]{2,1,0:T(2,128)S(1)}, u32[]{:S(2)}, u32[]{:S(2)}) collective-permute-start(f32[2,2,65]{2,1,0:T(2,128)S(1)} %pad_maximum_fusion.21), channel_id=1, source_target_pairs={{0,2},{1,3},{2,0},{3,1},{4,6},{5,7},{6,4},{7,5},{8,10},{9,11},{10,... | collective-permute-start | bytes 3128 | tf_op jit(solution)/shard_map/ppermute | solution.py:340
  43.8 12.8 %collective-permute-start.12 = (f32[2,2,65]{2,1,0:T(2,128)S(1)}, f32[2,2,65]{2,1,0:T(2,128)S(1)}, u32[]{:S(2)}, u32[]{:S(2)}) collective-permute-start(f32[2,2,65]{2,1,0:T(2,128)S(1)} %pad_maximum_fusion.21), channel_id=1, source_target_pairs={{0,3},{1,2},{2,1},{3,0},{4,7},{5,6},{6,5},{7,4},{8,11},{9,10},{10,... | collective-permute-start | bytes 3128 | tf_op jit(solution)/shard_map/ppermute | solution.py:340
  46.6 64.7 %copy-start = (f32[128,2048]{1,0:T(8,128)S(1)}, f32[128,2048]{1,0:T(8,128)}, u32[]{:S(2)}) copy-start(f32[128,2048]{1,0:T(8,128)} %est.1) | copy-start | bytes 3145732
  46.6 83.1 %collective-permute-start.14 = (f32[2,128,512]{2,1,0:T(8,128)}, f32[2,128,512]{2,1,0:T(8,128)}, u32[]{:S(2)}, u32[]{:S(2)}) collective-permute-start(f32[2,128,512]{2,1,0:T(8,128)} %get-tuple-element.47), channel_id=1, source_target_pairs={{0,1},{1,0},{2,3},{3,2},{4,5},{5,4},{6,7},{7,6},{8,9},{9,8},{10,11... | collective-permute-start | bytes 1572872 | tf_op jit(solution)/shard_map/ppermute | solution.py:340
  52.7 77.0 %collective-permute-start.15 = (f32[2,128,512]{2,1,0:T(8,128)}, f32[2,128,512]{2,1,0:T(8,128)}, u32[]{:S(2)}, u32[]{:S(2)}) collective-permute-start(f32[2,128,512]{2,1,0:T(8,128)} %get-tuple-element.44), channel_id=1, source_target_pairs={{0,2},{1,3},{2,0},{3,1},{4,6},{5,7},{6,4},{7,5},{8,10},{9,11},{10,... | collective-permute-start | bytes 1572872 | tf_op jit(solution)/shard_map/ppermute | solution.py:340
  55.2 82.9 %collective-permute-start.13 = (f32[2,128,512]{2,1,0:T(8,128)}, f32[2,128,512]{2,1,0:T(8,128)}, u32[]{:S(2)}, u32[]{:S(2)}) collective-permute-start(f32[2,128,512]{2,1,0:T(8,128)} %get-tuple-element.46), channel_id=1, source_target_pairs={{0,3},{1,2},{2,1},{3,0},{4,7},{5,6},{6,5},{7,4},{8,11},{9,10},{10,... | collective-permute-start | bytes 1572872 | tf_op jit(solution)/shard_map/ppermute | solution.py:340
  56.9 54.5 %collective-permute-start.5 = (f32[128,512]{1,0:T(8,128)S(1)}, f32[128,512]{1,0:T(8,128)S(1)}, u32[]{:S(2)}, u32[]{:S(2)}) collective-permute-start(f32[128,512]{1,0:T(8,128)S(1)} %constant_dynamic-slice_fusion.4), channel_id=1, source_target_pairs={{0,2},{1,3},{2,0},{3,1},{4,6},{5,7},{6,4},{7,5},{8,10},{9,11},{10,... | collective-permute-start | bytes 786440 | tf_op jit(solution)/shard_map/ppermute | solution.py:340
  111.5 6.0 %collective-permute-start.6 = (f32[32,512]{1,0:T(8,128)S(1)}, f32[32,512]{1,0:T(8,128)S(1)}, u32[]{:S(2)}, u32[]{:S(2)}) collective-permute-start(f32[32,512]{1,0:T(8,128)S(1)} %get-tuple-element.94), channel_id=1, source_target_pairs={{0,4},{4,8},{8,12},{12,16},{16,20},{20,24},{24,28},{1,5},{5,9},{9,... | collective-permute-start | bytes 196616 | tf_op jit(solution)/shard_map/ppermute | solution.py:330
  115.5 3.8 %collective-permute-start.7 = (f32[32,512]{1,0:T(8,128)S(1)}, f32[32,512]{1,0:T(8,128)S(1)}, u32[]{:S(2)}, u32[]{:S(2)}) collective-permute-start(f32[32,512]{1,0:T(8,128)S(1)} %get-tuple-element.95), channel_id=1, source_target_pairs={{4,0},{8,4},{12,8},{16,12},{20,16},{24,20},{28,24},{5,1},{9,5},{13... | collective-permute-start | bytes 196616 | tf_op jit(solution)/shard_map/ppermute | solution.py:335
  119.3 8.7 %collective-permute-start.8 = (f32[192,128]{1,0:T(8,128)S(1)}, f32[192,128]{1,0:T(8,128)S(1)}, u32[]{:S(2)}, u32[]{:S(2)}) collective-permute-start(f32[192,128]{1,0:T(8,128)S(1)} %get-tuple-element.90), channel_id=1, source_target_pairs={{0,1},{1,2},{2,3},{4,5},{5,6},{6,7},{8,9},{9,10},{10,11},{12,13},{... | collective-permute-start | bytes 294920 | tf_op jit(solution)/shard_map/ppermute | solution.py:330
  122.3 6.5 %collective-permute-start.9 = (f32[192,128]{1,0:T(8,128)S(1)}, f32[192,128]{1,0:T(8,128)S(1)}, u32[]{:S(2)}, u32[]{:S(2)}) collective-permute-start(f32[192,128]{1,0:T(8,128)S(1)} %get-tuple-element.91), channel_id=1, source_target_pairs={{1,0},{2,1},{3,2},{5,4},{6,5},{7,6},{9,8},{10,9},{11,10},{13,12},{... | collective-permute-start | bytes 294920 | tf_op jit(solution)/shard_map/ppermute | solution.py:335
  144.3 6.6 %collective-permute-start.16 = (f32[64,640]{1,0:T(8,128)S(1)}, f32[64,640]{1,0:T(8,128)S(1)}, u32[]{:S(2)}, u32[]{:S(2)}) collective-permute-start(f32[64,640]{1,0:T(8,128)S(1)} %get-tuple-element.88), channel_id=1, source_target_pairs={{0,4},{4,8},{8,12},{12,16},{16,20},{20,24},{24,28},{1,5},{5,9},{9,... | collective-permute-start | bytes 491528 | tf_op jit(solution)/shard_map/ppermute | solution.py:330
  148.6 4.9 %collective-permute-start.17 = (f32[64,640]{1,0:T(8,128)S(1)}, f32[64,640]{1,0:T(8,128)S(1)}, u32[]{:S(2)}, u32[]{:S(2)}) collective-permute-start(f32[64,640]{1,0:T(8,128)S(1)} %get-tuple-element.89), channel_id=1, source_target_pairs={{4,0},{8,4},{12,8},{16,12},{20,16},{24,20},{28,24},{5,1},{9,5},{13... | collective-permute-start | bytes 491528 | tf_op jit(solution)/shard_map/ppermute | solution.py:335
  154.8 6.3 %collective-permute-start.18 = (f32[192,128]{1,0:T(8,128)S(1)}, f32[192,128]{1,0:T(8,128)S(1)}, u32[]{:S(2)}, u32[]{:S(2)}) collective-permute-start(f32[192,128]{1,0:T(8,128)S(1)} %get-tuple-element.83), channel_id=1, source_target_pairs={{0,1},{1,2},{2,3},{4,5},{5,6},{6,7},{8,9},{9,10},{10,11},{12,13},{... | collective-permute-start | bytes 294920 | tf_op jit(solution)/shard_map/ppermute | solution.py:330
  158.9 6.7 %collective-permute-start.19 = (f32[192,128]{1,0:T(8,128)S(1)}, f32[192,128]{1,0:T(8,128)S(1)}, u32[]{:S(2)}, u32[]{:S(2)}) collective-permute-start(f32[192,128]{1,0:T(8,128)S(1)} %get-tuple-element.84), channel_id=1, source_target_pairs={{1,0},{2,1},{3,2},{5,4},{6,5},{7,6},{9,8},{10,9},{11,10},{13,12},{... | collective-permute-start | bytes 294920 | tf_op jit(solution)/shard_map/ppermute | solution.py:335
  165.8 0.8 copy-start.1
  166.6 10.3 %copy-start.4 = (f32[8,128]{1,0:T(8,128)S(1)}, f32[8,128]{1,0:T(8,128)}, u32[]{:S(2)}) copy-start(f32[8,128]{1,0:T(8,128)} %get-tuple-element.34) | copy-start | bytes 12292
  176.9 26.9 %copy-start.3 = (f32[192,640]{1,0:T(8,128)S(1)}, f32[192,640]{1,0:T(8,128)}, u32[]{:S(2)}) copy-start(f32[192,640]{1,0:T(8,128)} %get-tuple-element.39) | copy-start | bytes 1474564
  177.7 3.7 %collective-permute-start.20 = (f32[4,8,128]{2,1,0:T(8,128)S(1)}, f32[4,8,128]{2,1,0:T(8,128)S(1)}, u32[]{:S(2)}, u32[]{:S(2)}) collective-permute-start(f32[4,8,128]{2,1,0:T(8,128)S(1)} %pad_maximum_fusion.16), channel_id=1, source_target_pairs={{0,1},{1,0},{2,3},{3,2},{4,5},{5,4},{6,7},{7,6},{8,9},{9,8},{10,11... | collective-permute-start | bytes 49160 | tf_op jit(solution)/shard_map/ppermute | solution.py:340
  182.1 5.0 %collective-permute-start.21 = (f32[4,8,128]{2,1,0:T(8,128)S(1)}, f32[4,8,128]{2,1,0:T(8,128)S(1)}, u32[]{:S(2)}, u32[]{:S(2)}) collective-permute-start(f32[4,8,128]{2,1,0:T(8,128)S(1)} %fusion.4), channel_id=1, source_target_pairs={{0,2},{1,3},{2,0},{3,1},{4,6},{5,7},{6,4},{7,5},{8,10},{9,11},{10,... | collective-permute-start | bytes 49160 | tf_op jit(solution)/shard_map/ppermute | solution.py:340
  185.3 14.9 %collective-permute-start.25 = (f32[1,128,512]{2,1,0:T(8,128)S(1)}, f32[1,128,512]{2,1,0:T(8,128)S(1)}, u32[]{:S(2)}, u32[]{:S(2)}) collective-permute-start(f32[1,128,512]{2,1,0:T(8,128)S(1)} %get-tuple-element.92), channel_id=1, source_target_pairs={{0,2},{1,3},{2,0},{3,1},{4,6},{5,7},{6,4},{7,5},{8,10},{9,11},{10,... | collective-permute-start | bytes 786440 | tf_op jit(solution)/shard_map/ppermute | solution.py:340
  187.9 1.2 collective-permute-start.22
  189.0 6.6 %collective-permute-start.23 = (f32[4,8,128]{2,1,0:T(8,128)S(1)}, f32[4,8,128]{2,1,0:T(8,128)S(1)}, u32[]{:S(2)}, u32[]{:S(2)}) collective-permute-start(f32[4,8,128]{2,1,0:T(8,128)S(1)} %add.210), channel_id=1, source_target_pairs={{0,8},{4,12},{8,0},{12,4},{16,24},{20,28},{24,16},{28,20},{1,9},{5... | collective-permute-start | bytes 49160 | tf_op jit(solution)/shard_map/ppermute | solution.py:340
  190.1 13.8 %collective-permute-start.29 = (f32[64,640]{1,0:T(8,128)S(1)}, f32[64,640]{1,0:T(8,128)S(1)}, u32[]{:S(2)}, u32[]{:S(2)}) collective-permute-start(f32[64,640]{1,0:T(8,128)S(1)} %get-tuple-element.79), channel_id=1, source_target_pairs={{0,4},{4,8},{8,12},{12,16},{16,20},{20,24},{24,28},{1,5},{5,9},{9,... | collective-permute-start | bytes 491528 | tf_op jit(solution)/shard_map/ppermute | solution.py:330
  192.1 11.7 %collective-permute-start.30 = (f32[64,640]{1,0:T(8,128)S(1)}, f32[64,640]{1,0:T(8,128)S(1)}, u32[]{:S(2)}, u32[]{:S(2)}) collective-permute-start(f32[64,640]{1,0:T(8,128)S(1)} %get-tuple-element.80), channel_id=1, source_target_pairs={{4,0},{8,4},{12,8},{16,12},{20,16},{24,20},{28,24},{5,1},{9,5},{13... | collective-permute-start | bytes 491528 | tf_op jit(solution)/shard_map/ppermute | solution.py:335
  195.7 8.1 %collective-permute-start.24 = (f32[4,8,128]{2,1,0:T(8,128)S(1)}, f32[4,8,128]{2,1,0:T(8,128)S(1)}, u32[]{:S(2)}, u32[]{:S(2)}) collective-permute-start(f32[4,8,128]{2,1,0:T(8,128)S(1)} %add.211), channel_id=1, source_target_pairs={{0,16},{4,20},{8,24},{12,28},{16,0},{20,4},{24,8},{28,12},{1,17},{... | collective-permute-start | bytes 49160 | tf_op jit(solution)/shard_map/ppermute | solution.py:340
  201.0 25.8 %collective-permute-start.26 = (f32[2,128,512]{2,1,0:T(8,128)}, f32[2,128,512]{2,1,0:T(8,128)S(1)}, u32[]{:S(2)}, u32[]{:S(2)}) collective-permute-start(f32[2,128,512]{2,1,0:T(8,128)} %pad_maximum_fusion.8), channel_id=1, source_target_pairs={{0,1},{1,0},{2,3},{3,2},{4,5},{5,4},{6,7},{7,6},{8,9},{9,8},{10,11... | collective-permute-start | bytes 1572872 | tf_op jit(solution)/shard_map/ppermute | solution.py:340
  201.9 22.8 %collective-permute-start.27 = (f32[1,128,512]{2,1,0:T(8,128)S(1)}, f32[1,128,512]{2,1,0:T(8,128)S(1)}, u32[]{:S(2)}, u32[]{:S(2)}) collective-permute-start(f32[1,128,512]{2,1,0:T(8,128)S(1)} %bitcast.61), channel_id=1, source_target_pairs={{0,2},{1,3},{2,0},{3,1},{4,6},{5,7},{6,4},{7,5},{8,10},{9,11},{10,... | collective-permute-start | bytes 786440 | tf_op jit(solution)/shard_map/ppermute | solution.py:340
  204.1 16.6 %collective-permute-start.31 = (f32[192,128]{1,0:T(8,128)S(1)}, f32[192,128]{1,0:T(8,128)S(1)}, u32[]{:S(2)}, u32[]{:S(2)}) collective-permute-start(f32[192,128]{1,0:T(8,128)S(1)} %get-tuple-element.74), channel_id=1, source_target_pairs={{0,1},{1,2},{2,3},{4,5},{5,6},{6,7},{8,9},{9,10},{10,11},{12,13},{... | collective-permute-start | bytes 294920 | tf_op jit(solution)/shard_map/ppermute | solution.py:330
  207.4 15.5 %collective-permute-start.32 = (f32[192,128]{1,0:T(8,128)S(1)}, f32[192,128]{1,0:T(8,128)S(1)}, u32[]{:S(2)}, u32[]{:S(2)}) collective-permute-start(f32[192,128]{1,0:T(8,128)S(1)} %get-tuple-element.75), channel_id=1, source_target_pairs={{1,0},{2,1},{3,2},{5,4},{6,5},{7,6},{9,8},{10,9},{11,10},{13,12},{... | collective-permute-start | bytes 294920 | tf_op jit(solution)/shard_map/ppermute | solution.py:335
  224.0 13.4 %collective-permute-start.34 = (f32[128,512]{1,0:T(8,128)S(1)}, f32[128,512]{1,0:T(8,128)S(1)}, u32[]{:S(2)}, u32[]{:S(2)}) collective-permute-start(f32[128,512]{1,0:T(8,128)S(1)} %fusion.3), channel_id=1, source_target_pairs={{0,2},{1,3},{2,0},{3,1},{4,6},{5,7},{6,4},{7,5},{8,10},{9,11},{10,... | collective-permute-start | bytes 786440 | tf_op jit(solution)/shard_map/ppermute | solution.py:340
  224.7 30.0 %collective-permute-start.28 = (f32[2,128,512]{2,1,0:T(8,128)S(1)}, f32[2,128,512]{2,1,0:T(8,128)S(1)}, u32[]{:S(2)}, u32[]{:S(2)}) collective-permute-start(f32[2,128,512]{2,1,0:T(8,128)S(1)} %pad_maximum_fusion.9), channel_id=1, source_target_pairs={{0,1},{1,0},{2,3},{3,2},{4,5},{5,4},{6,7},{7,6},{8,9},{9,8},{10,11... | collective-permute-start | bytes 1572872 | tf_op jit(solution)/shard_map/ppermute | solution.py:340
  226.5 24.2 %collective-permute-start.33 = (f32[128,512]{1,0:T(8,128)S(1)}, f32[128,512]{1,0:T(8,128)S(1)}, u32[]{:S(2)}, u32[]{:S(2)}) collective-permute-start(f32[128,512]{1,0:T(8,128)S(1)} %fusion.3), channel_id=1, source_target_pairs={{0,1},{1,0},{2,3},{3,2},{4,5},{5,4},{6,7},{7,6},{8,9},{9,8},{10,11... | collective-permute-start | bytes 786440 | tf_op jit(solution)/shard_map/ppermute | solution.py:340
  237.4 17.1 %collective-permute-start.35 = (f32[128,512]{1,0:T(8,128)S(1)}, f32[128,512]{1,0:T(8,128)S(1)}, u32[]{:S(2)}, u32[]{:S(2)}) collective-permute-start(f32[128,512]{1,0:T(8,128)S(1)} %collective-permute-done.34), channel_id=1, source_target_pairs={{0,1},{1,0},{2,3},{3,2},{4,5},{5,4},{6,7},{7,6},{8,9},{9,8},{10,11... | collective-permute-start | bytes 786440 | tf_op jit(solution)/shard_map/ppermute | solution.py:340

commit v2 on v1

--- a/solution.py
+++ b/solution.py
@@ -30,62 +30,72 @@
     return [(s, min(step, width - s)) for s in range(0, width, step)]
 
 
-def kernel_bases(col_unit, row_unit):
-    count, taps = col_unit.shape
+def taps_tile(column_kernels, row_kernels, w):
+    both = jnp.concatenate([column_kernels, row_kernels], axis=0)
+    count, taps = both.shape
+    return jnp.pad(both, ((0, -count % 8), (0, w - taps)))
+
+
+def setup_kernel(frames, rows, halo, sources, *refs):
+    tiles_in = refs[: len(sources)]
+    t_ref, b_ref, bp_ref, ta_ref, taps, sem = refs[len(sources) :]
     wide = 2 * LANE
-
-    def at(values, start):
-        return jnp.pad(values, ((0, 0), (start, wide - taps - start)))
-
-    def turned(values):
-        gap = jnp.zeros((count, wide - taps), f32)
-        return jnp.concatenate([values[:, :1], gap, values[:, :0:-1]], axis=1)
-
-    return jnp.stack(
-        [at(row_unit, 0), turned(col_unit), at(col_unit, LANE), turned(row_unit)], axis=1
-    )
-
-
-def setup_kernel(per_group, rows, halo, base_ref, t_ref, b_ref, bp_ref, ta_ref):
-    frames = base_ref.shape[0]
-
-    def toeplitz(f, which, count):
-        base = jnp.broadcast_to(base_ref[f, which : which + 1, :], (count, 2 * LANE))
-        return pltpu.roll(base, 0, 1, stride=1, stride_axis=0)
-
-    ext = rows + 2 * halo
-    for f in range(frames):
-        hi, lo = split(toeplitz(f, 0, rows))
-        t_ref[f, :rows, :] = hi
-        t_ref[f, rows:, :] = lo
-        hi, lo = split(toeplitz(f, 1, 2 * LANE)[:, :LANE])
-        b_ref[f, :, :LANE] = hi
-        b_ref[f, :, LANE:] = lo
-        hi, lo = split(toeplitz(f, 2, 2 * LANE)[:, :LANE])
-        bp_ref[f, :, :LANE] = hi
-        bp_ref[f, :, LANE:] = lo
-        hi, lo = split(toeplitz(f, 3, ext)[:, :rows])
-        g, s = divmod(f, per_group)
-        ta_ref[g, :ext, s * rows : (s + 1) * rows] = hi
-        ta_ref[g, ext:, s * rows : (s + 1) * rows] = lo
-
-
-def setup_matrices(bases, per_group, rows, halo):
-    frames = bases.shape[0]
-    ext = rows + 2 * halo
+    ext = rows + 2 * halo
+
+    def copy(g):
+        start, count = sources[g]
+        return pltpu.make_async_copy(
+            tiles_in[g].at[pl.ds(start, count), pl.ds(0, wide)], taps.at[g], sem.at[g]
+        )
+
+    def toeplitz(base, count):
+        return pltpu.roll(jnp.broadcast_to(base, (count, wide)), 0, 1, stride=1, stride_axis=0)
+
+    for g in range(len(sources)):
+        copy(g).start()
+    for g in range(len(sources)):
+        copy(g).wait()
+        unit = taps[g] / jnp.sum(taps[g], axis=1, keepdims=True)
+        for s in range(frames):
+            f = g * frames + s
+            col = unit[s : s + 1]
+            row = unit[frames + s : frames + s + 1]
+            by_rows = toeplitz(row, rows)
+            hi, lo = split(by_rows)
+            t_ref[f, :rows, :] = hi
+            t_ref[f, rows:, :] = lo
+            hi, lo = split(by_rows.T[:ext])
+            ta_ref[g, :ext, s * rows : (s + 1) * rows] = hi
+            ta_ref[g, ext:, s * rows : (s + 1) * rows] = lo
+            hi, lo = split(toeplitz(col, LANE).T)
+            b_ref[f, :, :LANE] = hi
+            b_ref[f, :, LANE:] = lo
+            hi, lo = split(toeplitz(pltpu.roll(col, LANE, 1), wide)[:, :LANE])
+            bp_ref[f, :, :LANE] = hi
+            bp_ref[f, :, LANE:] = lo
+
+
+def setup_matrices(tiles_in, starts, frames, rows, halo):
+    groups = len(tiles_in)
+    ext = rows + 2 * halo
+    height = -(-2 * frames // 8) * 8
     shapes = (
-        (frames, 2 * rows, 2 * LANE),
-        (frames, 2 * LANE, 2 * LANE),
-        (frames, 2 * LANE, 2 * LANE),
-        (frames // per_group, 2 * ext, per_group * rows),
+        (groups * frames, 2 * rows, 2 * LANE),
+        (groups * frames, 2 * LANE, 2 * LANE),
+        (groups * frames, 2 * LANE, 2 * LANE),
+        (groups, 2 * ext, frames * rows),
     )
     return pl.pallas_call(
-        functools.partial(setup_kernel, per_group, rows, halo),
+        functools.partial(setup_kernel, frames, rows, halo, [(start, height) for start in starts]),
         out_shape=[jax.ShapeDtypeStruct(s, bf16) for s in shapes],
-        in_specs=[VMEM],
+        in_specs=[ANY] * groups,
         out_specs=[VMEM] * 4,
+        scratch_shapes=[
+            pltpu.VMEM((groups, height, 2 * LANE), f32),
+            pltpu.SemaphoreType.DMA((groups,)),
+        ],
         name="setup_matrices",
-    )(bases)
+    )(*tiles_in)
 
 
 def load_image(y_hi, y_lo, image, halo):
@@ -245,43 +255,79 @@
     )(est, lo, hi, *mats, weights, observed)
 
 
-def apply_kernel(frames, rows, halo, w, groups, base, has_acc, final, *refs):
-    image, t_hbm, b_hbm, bp_hbm, ta_hbm = refs[:5]
-    weights = refs[5 : 5 + groups]
-    refs = refs[5 + groups :]
-    if has_acc:
-        acc_in, stat_in = refs[:2]
-        refs = refs[2:]
-    out, stat, y_hi, y_lo, us, qs, vs_hi, vs_lo, acc, tb, bb, bpb, tab, wbuf, sem = refs
+def pack_kernel(plan, rows, w, place, weights, tile, *refs):
+    outs, sem = refs[:-1], refs[-1]
+    pending = []
+    for i, (distance, lead, count, with_taps) in enumerate(plan):
+        start = pl.multiple_of(jnp.bitwise_xor(place[0], distance) * w, LANE)
+        for k in range(count):
+            copy = pltpu.make_async_copy(
+                weights.at[lead + k, :, pl.ds(start, w)],
+                outs[i].at[pl.ds(k * rows, rows), :],
+                sem.at[i, k],
+            )
+            copy.start()
+            pending.append(copy)
+        if with_taps:
+            outs[i][count * rows :, :] = tile[...]
+    for copy in pending:
+        copy.wait()
+
+
+def pack_weights(plan, place, weights, tile):
+    frames, rows, _ = weights.shape
+    w = tile.shape[1]
+    return pl.pallas_call(
+        functools.partial(pack_kernel, plan, rows, w),
+        out_shape=[
+            jax.ShapeDtypeStruct((count * rows + (tile.shape[0] if taps else 0), w), f32)
+            for _, _, count, taps in plan
+        ],
+        in_specs=[pl.BlockSpec(memory_space=pltpu.SMEM), ANY, VMEM],
+        out_specs=[VMEM] * len(plan),
+        scratch_shapes=[pltpu.SemaphoreType.DMA((len(plan), frames))],
+        name="pack_weights",
+    )(place, weights, tile)
+
+
+def apply_kernel(frames, rows, halo, w, groups, origin, cut, count, place, image, *refs):
+    t_hbm, b_hbm, bp_hbm, ta_hbm, own = refs[:5]
+    moved = refs[5 : 5 + count]
+    top, mid, bot, stat = refs[5 + count : 9 + count]
+    y_hi, y_lo, us, qs, vs_hi, vs_lo, acc, tb, bb, bpb, tab, wbuf, sem, wsem = refs[9 + count :]
     ext = rows + 2 * halo
 
     def copies(g):
-        span = pl.ds((base + g) * frames, frames)
+        span = pl.ds(g * frames, frames)
         return [
             pltpu.make_async_copy(t_hbm.at[span], tb.at[g], sem.at[0, g]),
             pltpu.make_async_copy(b_hbm.at[span], bb.at[g], sem.at[1, g]),
             pltpu.make_async_copy(bp_hbm.at[span], bpb.at[g], sem.at[2, g]),
-            pltpu.make_async_copy(ta_hbm.at[base + g], tab.at[g], sem.at[3, g]),
+            pltpu.make_async_copy(ta_hbm.at[g], tab.at[g], sem.at[3, g]),
         ]
 
+    mine = pl.ds(pl.multiple_of(place[0] * w, LANE), w)
     for g in range(groups):
         for c in copies(g):
             c.start()
-        pltpu.make_async_copy(weights[g], wbuf.at[g], sem.at[4, g]).start()
+        for f in range(frames):
+            if g == 0:
+                source = own.at[f, :, mine]
+            else:
+                ref, start = origin[g, f]
+                source = moved[ref].at[pl.ds(start, rows), :]
+            pltpu.make_async_copy(source, wbuf.at[g, f], wsem.at[g, f]).start()
     clear_edges(y_hi, y_lo, qs, ext, rows, w)
     load_image(y_hi, y_lo, image[...], halo)
-    if has_acc:
-        acc[...] = acc_in[...]
-        stat[...] = stat_in[...]
-    else:
-        acc[...] = jnp.zeros_like(acc)
-        stat[...] = jnp.zeros_like(stat)
+    acc[...] = jnp.zeros_like(acc)
+    stat[...] = jnp.zeros_like(stat)
 
     @pl.loop(0, groups)
     def _(g):
         for c in copies(g):
             c.wait()
-        pltpu.make_async_copy(weights[0], wbuf.at[g], sem.at[4, g]).wait()
+        for f in range(frames):
+            pltpu.make_async_copy(own.at[f, :, mine], wbuf.at[g, f], wsem.at[g, f]).wait()
         group_terms(
             frames, rows, w, y_hi, y_lo,
             lambda f: tb.at[g, f], lambda f: bb.at[g, f], lambda f: bpb.at[g, f], tab.at[g],
@@ -289,27 +335,29 @@
             us, qs, vs_hi, vs_lo, acc, stat,
         )
 
-    out[...] = unshift(acc[...], halo) if final else acc[...]
-
-
-def apply_terms(image, mats, weights, base, halo, carry=None, final=True):
-    frames, rows, w = weights[0].shape
-    ext = rows + 2 * halo
-    groups = len(weights)
+    z = unshift(acc[...], halo)
+    top[...] = z[:cut]
+    mid[...] = z[cut : ext - cut]
+    bot[...] = z[ext - cut :]
+
+
+def apply_terms(place, image, mats, weights, moved, origin, cut, halo):
+    frames, rows, _ = weights.shape
+    w = image.shape[1] - 2 * LANE
+    ext = rows + 2 * halo
     t, b, bp, ta = mats
-    args = [image, t, b, bp, ta, *weights]
-    specs = [VMEM] + [ANY] * (4 + groups)
-    if carry is not None:
-        args += list(carry)
-        specs += [VMEM, VMEM]
+    groups = ta.shape[0]
+    wide = w + LANE
     return pl.pallas_call(
-        functools.partial(apply_kernel, frames, rows, halo, w, groups, base, carry is not None, final),
+        functools.partial(apply_kernel, frames, rows, halo, w, groups, origin, cut, len(moved)),
         out_shape=[
-            jax.ShapeDtypeStruct((ext, w + LANE), f32),
+            jax.ShapeDtypeStruct((cut, wide), f32),
+            jax.ShapeDtypeStruct((ext - 2 * cut, wide), f32),
+            jax.ShapeDtypeStruct((cut, wide), f32),
             jax.ShapeDtypeStruct((8, LANE), f32),
         ],
-        in_specs=specs,
-        out_specs=[VMEM, VMEM],
+        in_specs=[pl.BlockSpec(memory_space=pltpu.SMEM), VMEM] + [ANY] * (5 + len(moved)),
+        out_specs=[VMEM] * 4,
         scratch_shapes=work_scratch(frames, rows, halo, w)
         + [
             pltpu.VMEM((groups, frames) + t.shape[1:], bf16),
@@ -317,12 +365,113 @@
             pltpu.VMEM((groups, frames) + bp.shape[1:], bf16),
             pltpu.VMEM((groups,) + ta.shape[1:], bf16),
             pltpu.VMEM((groups, frames, rows, w), f32),
-            pltpu.SemaphoreType.DMA((5, groups)),
+            pltpu.SemaphoreType.DMA((4, groups)),
+            pltpu.SemaphoreType.DMA((groups, frames)),
         ],
         cost_estimate=pl.CostEstimate(
             flops=groups * 3 * 10**9, bytes_accessed=groups * 2**20, transcendentals=0
         ),
-    )(*args)
+    )(place, image, t, b, bp, ta, weights, *moved)
+
+
+def wrap_kernel(rows, halo, w, top, mid, bot, up, dn, before, sums, out):
+    keep = rows - 2 * halo
+    pieces = (
+        (0, halo, mid[:halo, :] + up[...]),
+        (halo, keep, mid[halo : rows - halo, :]),
+        (rows - halo, halo, mid[rows - halo :, :] + dn[...]),
+    )
+    edges = []
+    for start, size, value in pieces:
+        span = slice(start, start + size)
+        out[span, :] = value[:, :w] + damping * before[span, :]
+        edges.append(pltpu.roll(value[:, w:], halo, 1))
+    edge = jnp.concatenate(edges, axis=0)
+    short = rows * 2 * halo // w
+    lane = lax.broadcasted_iota(jnp.int32, (short, LANE), 1)
+    per = LANE // (2 * halo)
+    for t in range(w // LANE):
+        tile = None
+        for p in range(per):
+            k = t * per + p
+            part = edge[k * short : (k + 1) * short]
+            part = pltpu.roll(part, p * 2 * halo, 1) if p else part
+            tile = part if tile is None else jnp.where(lane >= p * 2 * halo, part, tile)
+        out[rows : rows + short, t * LANE : (t + 1) * LANE] = tile
+    out[rows + short :, :] = jnp.zeros((8, w), f32)
+    for i in range(4):
+        out[rows + short + i : rows + short + i + 1, :LANE] = jnp.sum(sums[i], axis=0, keepdims=True)
+
+
+def wrap(top, mid, bot, up, dn, before, sums, halo):
+    rows, w = before.shape
+    height = rows + rows * 2 * halo // w + 8
+    return pl.pallas_call(
+        functools.partial(wrap_kernel, rows, halo, w),
+        out_shape=jax.ShapeDtypeStruct((height, w), f32),
+        in_specs=[VMEM] * 7,
+        out_specs=VMEM,
+        name="wrap",
+    )(top, mid, bot, up, dn, before, sums)
+
+
+def final_kernel(n, rows, halo, w, place, est, *refs):
+    k0, k1, k2 = refs[:n], refs[n : 2 * n], refs[2 * n : 3 * n]
+    sol, res, full = refs[3 * n :]
+    short = rows * 2 * halo // w
+    per = LANE // (2 * halo)
+    total = k2[0][rows + short :, :LANE]
+    for i in range(1, n):
+        total = total + k2[i][rows + short :, :LANE]
+    total = jnp.sum(total, axis=1, keepdims=True)
+    k00, k11 = total[0:1], total[2:3]
+    k01 = total[1:2] + damping * k00
+    k12 = total[3:4] + damping * k11
+    alpha0 = k00 / k01
+    norm1 = k00 - 2.0 * alpha0 * k01 + alpha0 * alpha0 * k11
+    beta = norm1 / k00
+    curve1 = (1.0 + beta) * (1.0 + beta) * k01 - 2.0 * (1.0 + beta) * alpha0 * k11
+    curve1 = curve1 + alpha0 * alpha0 * k12
+    alpha1 = norm1 / curve1
+    c1 = alpha0 + alpha1 * (1.0 + beta)
+    c2 = alpha0 * alpha1
+
+    lane = lax.broadcasted_iota(jnp.int32, (rows, LANE), 1)
+    spot = [jnp.bitwise_xor(place[0], i) for i in range(n)]
+    for end in (0, LANE + n * w):
+        full[:, end : end + LANE] = jnp.zeros((rows, LANE), f32)
+    for i in range(n):
+        full[:, pl.ds(pl.multiple_of(spot[i] * w + LANE, LANE), w)] = k2[i][:rows, :]
+    for i in range(n):
+        parts = []
+        for k in range(w // (2 * halo)):
+            t, p = divmod(k, per)
+            part = k2[i][rows : rows + short, t * LANE : (t + 1) * LANE]
+            back = (LANE - halo - p * 2 * halo) % LANE
+            parts.append(pltpu.roll(part, back, 1) if back else part)
+        edge = jnp.concatenate(parts, axis=0)
+        left = pl.ds(pl.multiple_of(spot[i] * w, LANE), LANE)
+        right = pl.ds(pl.multiple_of(spot[i] * w + w + LANE, LANE), LANE)
+        full[:, left] += jnp.where(lane >= LANE - halo, edge, 0.0)
+        full[:, right] += jnp.where(lane < halo, edge, 0.0)
+    for i in range(n):
+        cols = pl.ds(pl.multiple_of(spot[i] * w, LANE), w)
+        a0, a1 = k0[i][...], k1[i][...]
+        sol[:, cols] = est[:, cols] + c1 * a0 - c2 * a1
+        res[:, cols] = a0 - c1 * a1 + c2 * full[:, pl.ds(pl.multiple_of(spot[i] * w + LANE, LANE), w)]
+
+
+def final_images(place, est, k0, k1, k2, halo):
+    n = len(k0)
+    rows, w = k0[0].shape
+    return pl.pallas_call(
+        functools.partial(final_kernel, n, rows, halo, w),
+        out_shape=[jax.ShapeDtypeStruct(est.shape, f32)] * 2,
+        in_specs=[pl.BlockSpec(memory_space=pltpu.SMEM)] + [VMEM] * (1 + 3 * n),
+        out_specs=[VMEM] * 2,
+        scratch_shapes=[pltpu.VMEM((rows, n * w + 2 * LANE), f32)],
+        name="final_images",
+    )(place, est, *k0, *k1, *k2)
 
 
 def shift_up(x, axis):
@@ -343,6 +492,7 @@
 def steps(estimate, observed, weights, column_kernels, row_kernels):
     n = lax.axis_size("frame")
     me = lax.axis_index("frame")
+    place = me.reshape(1).astype(jnp.int32)
     strips = lax.axis_size("strip")
     strip = lax.axis_index("strip")
     rows, cols = estimate.shape
@@ -352,36 +502,41 @@
     ext = rows + 2 * halo
     distances = [1 << k for k in range(n.bit_length() - 1)]
 
-    unit = lambda k: k / jnp.sum(k, axis=1, keepdims=True)
+    def block_of(x, j):
+        return lax.dynamic_slice_in_dim(x, j * w, w, axis=x.ndim - 1)
+
+    def fold(x):
+        return jnp.sum(x.reshape(rows * w // (8 * LANE), 8, LANE), axis=0)
+
     est_lo = shift_up(estimate[rows - halo :], "strip")
     est_hi = shift_down(estimate[:halo], "strip")
-    taps = jnp.stack([column_kernels, row_kernels])
-    all_taps = [taps]
-    for d in range(1, n):
-        all_taps.append(swap(taps, "frame", d))
-    bases = kernel_bases(unit(column_kernels), unit(row_kernels))
-    all_taps = jnp.concatenate(all_taps, axis=1)
-
-    def block_of(x, j):
-        return lax.dynamic_slice_in_dim(x, j * w, w, axis=x.ndim - 1)
-
-    my_weights = [block_of(weights, me)]
-    for d in range(1, n):
-        my_weights.append(swap(block_of(weights, me ^ d), "frame", d))
-
-    own_mats = setup_matrices(bases, frames, rows, halo)
+
+    early = frames // 2
+    plan = [(d, 0, frames, True) for d in range(1, n - 1)]
+    plan += [(n - 1, 0, early, True), (n - 1, early, frames - early, False)]
+    tile = taps_tile(column_kernels, row_kernels, w)
+    packed = pack_weights(plan, place, weights, tile)
+    moved = []
+    for i, (d, _, _, taps) in enumerate(plan):
+        moved.append(swap(packed[i], "frame", d))
+    origin = {}
+    starts = [0]
+    for i, (d, lead, count, taps) in enumerate(plan):
+        for k in range(count):
+            origin[d, lead + k] = (i, k * rows)
+        if taps:
+            starts.append(count * rows)
+
+    own_mats = setup_matrices([tile], [0], frames, rows, halo)
     top, mid, bot = first_terms(estimate, est_lo, est_hi, own_mats, weights, observed, w)
-
-    all_bases = kernel_bases(unit(all_taps[0]), unit(all_taps[1]))
-    mats = setup_matrices(all_bases, frames, rows, halo)
+    mats = setup_matrices([tile] + moved[: n - 1], starts, frames, rows, halo)
 
     from_up = shift_up(bot, "strip")
     from_dn = shift_down(top, "strip")
-    terms = jnp.concatenate(
+    left = jnp.concatenate(
         [mid[:halo] + from_up, mid[halo : rows - halo], mid[rows - halo :] + from_dn], axis=0
     )
 
-    left = terms
     for d in distances:
         bit = (me // d) % 2
         half = left.shape[1] // w // 2
@@ -391,8 +546,10 @@
                 [block_of(left, 2 * i + which) for i in range(half)], axis=1
             )
 
-        left = pick(bit) + swap(pick(1 - bit), "frame", d)
+        sent = swap(pick(1 - bit), "frame", d)
+        left = pick(bit) + sent
     k0 = -(left + damping * block_of(estimate, me))
+    k00_part = fold(k0 * k0)
 
     lane = lax.broadcasted_iota(jnp.int32, (ext, LANE), 1)
     row = lax.broadcasted_iota(jnp.int32, (ext, 1), 0)
@@ -412,13 +569,10 @@
         axis=1,
     )
 
-    def complete(part, before):
-        up = shift_up(part[rows:], "strip")
-        dn = shift_down(part[: 2 * halo], "strip")
-        q = jnp.concatenate(
-            [part[: 2 * halo] + up, part[2 * halo : rows], part[rows:] + dn], axis=0
-        )
-        q = jnp.where(inside, q, 0.0)
+    def complete(top, mid, bot, before):
+        up = shift_up(bot, "strip")
+        dn = shift_down(top, "strip")
+        q = jnp.where(inside, jnp.concatenate([top + up, mid, bot + dn], axis=0), 0.0)
         edge = q[:, w:]
         to_right = jnp.where(lane >= LANE - halo, q[:, w - LANE : w], edge)
         to_left = jnp.where(lane < halo, q[:, :LANE], edge)
@@ -436,64 +590,38 @@
         )
         return jnp.concatenate([left_tile, own, right_tile], axis=1) + damping * before
 
-    def own_block(x):
-        return x[halo : halo + rows, LANE : LANE + w]
-
-    def fold(x):
-        return jnp.sum(x.reshape(rows * w // (8 * LANE), 8, LANE), axis=0)
-
-    k00_part = fold(k0 * k0)
-    carry = apply_terms(k0x, mats, my_weights[: n - 1], 0, halo, final=False)
-    part1, stat1 = apply_terms(k0x, mats, my_weights[n - 1 :], n - 1, halo, carry)
-    k1x = complete(part1, k0x)
-    k1, k1x = lax.optimization_barrier((own_block(k1x), k1x))
+    top, mid, bot, stat1 = apply_terms(place, k0x, mats, weights, moved, origin, 2 * halo, halo)
+    k1x = complete(top, mid, bot, k0x)
+    k1, k1x = lax.optimization_barrier((k1x[halo : halo + rows, LANE : LANE + w], k1x))
     k11_part = fold(k1 * k1)
-    part2, stat2 = apply_terms(k1x, mats, my_weights, 0, halo)
-    k2 = own_block(complete(part2, k1x))
-
+    top, mid, bot, stat2 = apply_terms(place, k1x, mats, weights, moved, origin, halo, halo)
+    up = shift_up(bot, "strip")
+    dn = shift_down(top, "strip")
     sums = jnp.stack([k00_part, stat1, k11_part, stat2])
-    for axis, size in (("frame", n), ("strip", strips)):
-        d = 1
-        while d < size:
-            sums = sums + swap(sums, axis, d)
-            d *= 2
-    sums = jnp.sum(sums, axis=(1, 2))
-    k00, k11 = sums[0], sums[2]
-    k01 = sums[1] + damping * k00
-    k12 = sums[3] + damping * k11
-    alpha0 = k00 / k01
-    norm1 = k00 - 2.0 * alpha0 * k01 + alpha0 * alpha0 * k11
-    beta = norm1 / k00
-    curve1 = (1.0 + beta) ** 2 * k01 - 2.0 * (1.0 + beta) * alpha0 * k11 + alpha0 * alpha0 * k12
-    alpha1 = norm1 / curve1
-    c1 = alpha0 + alpha1 * (1.0 + beta)
-    c2 = alpha0 * alpha1
-
-    def ordered(parts):
-        both = jnp.stack(parts)
-        return jnp.concatenate(
-            [lax.dynamic_index_in_dim(both, me ^ j, 0, keepdims=False) for j in range(n)], axis=1
-        )
+    d = 1
+    while d < strips:
+        sums = sums + swap(sums, "strip", d)
+        d *= 2
+    k2 = wrap(top, mid, bot, up, dn, k1, sums, halo)
 
     def gathered(x):
         parts = [x] + [None] * (n - 1)
         for d in reversed(distances):
             known = [i for i in range(n) if parts[i] is not None]
-            sent = swap(jnp.stack([parts[i] for i in known]), "frame", d)
-            for s, i in enumerate(known):
-                parts[i ^ d] = sent[s]
-        return ordered(parts)
+            for i in known:
+                parts[i ^ d] = swap(parts[i], "frame", d)
+        return parts
 
     def gathered_soon(x):
         parts = [x] + [None] * (n - 1)
-        for i in range(0, n):
+        for i in range(n):
             for d in reversed(distances):
                 if i % (2 * d) == 0:
                     parts[i + d] = swap(parts[i], "frame", d)
-        return ordered(parts)
+        return parts
 
     g0, g1, g2 = gathered(k0), gathered(k1), gathered_soon(k2)
-    return estimate + c1 * g0 - c2 * g1, g0 - c1 * g1 + c2 * g2
+    return tuple(final_images(place, estimate, g0, g1, g2, halo))
 
 
 def solution(mesh):

time: 259 us -> 244 us (0.942)
  Pallas kernels: 41.5 us -> 49.1 us
  starting transfers between devices: 69.9 us -> 62.7 us
  other arithmetic: 16.3 us -> 10.4 us
  between operations: 6.85 us -> 1.21 us
  waiting for transfers between devices: 114 us -> 110 us
    pallas_call x2 -> x5, Pallas kernels: 5.7 us -> 15.8 us  [the longest x2 6.49 us: setup_matrices(): pl.pallas_call(functools.partial(setup_kernel, frames, rows, halo, [(star...]
    ppermute x8 -> x7, waiting for transfers between devices: 8.01 us -> 2.57 us  [shift_up(): return lax.ppermute(x, axis, [(i, i + 1) for i in range(n - 1)])]
    ppermute x8 -> x7, starting transfers between devices: 24.8 us -> 20.2 us  [shift_up(): return lax.ppermute(x, axis, [(i, i + 1) for i in range(n - 1)])]
    unnamed x18 -> x44, local copies, waits for them, and re-layouts: 1.44 us -> 4.92 us
    slice x10 -> x1, local copies, waits for them, and re-layouts: 3.07 us -> 0.02 us  [steps(): k1x[halo:halo + rows, LANE:LANE + w]]
    pallas_call x3 -> x2, Pallas kernels: 23.9 us -> 21.4 us  [apply_terms(): pl.pallas_call(functools.partial(apply_kernel, frames, rows, halo, w, gro...]
    ppermute x8 -> x7, starting transfers between devices: 18.5 us -> 17 us  [shift_down(): return lax.ppermute(x, axis, [(i + 1, i) for i in range(n - 1)])]
    ppermute x20 -> x18, starting transfers between devices: 26.7 us -> 25.5 us  [swap(): return lax.ppermute(x, axis, [(i, i ^ distance) for i in range(n)])]
  transfers between devices with their start and end apart: 36 -> 32, of which waited for: 19 -> 20; matrix products, arithmetic and copies ran while one was open for 6% -> 3% of each run, Pallas kernels for 5% -> 4%
where the time goes in v2:
time: 244 us; the launch traced here: 240 us
  waiting for transfers between devices  110 us (45%)
  starting transfers between devices  62.7 us (26%)
  Pallas kernels  49.1 us (20%)
  other arithmetic  10.4 us (4%)
  local copies, waits for them, and re-layouts  7.25 us (3%)
    ppermute x18, waiting for transfers between devices, swap(): return lax.ppermute(x, axis, [(i, i ^ distance) for i in range(n)])  91.1 us
    ppermute x18, starting transfers between devices, swap(): return lax.ppermute(x, axis, [(i, i ^ distance) for i in range(n)])  25.5 us
    pallas_call x2, Pallas kernels, apply_terms(): pl.pallas_call(functools.partial(apply_kernel, frames, rows, halo, w, gro...  21.4 us
    ppermute x7, starting transfers between devices, shift_up(): return lax.ppermute(x, axis, [(i, i + 1) for i in range(n - 1)])  20.2 us
    ppermute x7, starting transfers between devices, shift_down(): return lax.ppermute(x, axis, [(i + 1, i) for i in range(n - 1)])  17 us
    ppermute x7, waiting for transfers between devices, shift_down(): return lax.ppermute(x, axis, [(i + 1, i) for i in range(n - 1)])  15.9 us
    pallas_call x1, Pallas kernels, first_terms(): pl.pallas_call(functools.partial(first_kernel, frames, rows, halo, w), ou...  12 us
    pallas_call x2, Pallas kernels, setup_matrices(): pl.pallas_call(functools.partial(setup_kernel, frames, rows, halo, [(star...  6.49 us
  transfers between devices with their start and end apart: 32, of which 20 were waited for; matrix products, arithmetic and copies ran while one was open for 3% of the time, Pallas kernels for 4%

profile of v2, /device:TPU:2, one launch (start us, length us, event | category | flops | bytes accessed | tf_op | source)
XLA Modules:
  0.0 240.2 jit_solution(7761300758490776109)
XLA Ops:
  1.7 1.9 collective-permute-start
  3.6 3.6 %collective-permute-start.1 = (f32[32,2048]{1,0:T(8,128)S(1)}, f32[32,2048]{1,0:T(8,128)S(1)}, u32[]{:S(2)}, u32[]{:S(2)}) collective-permute-start(f32[32,2048]{1,0:T(8,128)S(1)} %get-tuple-element.60), channel_id=1, source_target_pairs={{4,0},{8,4},{12,8},{16,12},{20,16},{24,20},{28,24},{5,1},{9,5},{13... | collective-permute-start | bytes 786440 | tf_op jit(solution)/shard_map/ppermute | solution.py:484
  7.3 1.3 select_maximum_fusion.refs_0_.tile
  8.6 2.0 setup_matrices.2
  11.9 12.0 %first_terms.1 = (f32[32,2048]{1,0:T(8,128)}, f32[128,2048]{1,0:T(8,128)}, f32[32,2048]{1,0:T(8,128)}) custom-call(f32[128,2048]{1,0:T(8,128)} %est.3, f32[32,2048]{1,0:T(8,128)} %copy-done.20, f32[32,2048]{1,0:T(8,128)} %copy-done.21, bf16[2,256,256]{2,1,0:T(8,128)(2,1)} %get-tuple-element.27.t_ref, bf16[2,256,256]{2,1,0:T(8,128)(2,1)} %get-tuple-element.28.b_ref, ...), custom_call_target="tpu_custom_call" | custom-call | flops 8000000000 | bytes 8388608 | tf_op jit(solution)/shard_map/first_terms/pallas_call | solution.py:236
  23.9 4.5 %collective-permute-start.2 = (f32[32,2048]{1,0:T(8,128)}, f32[32,2048]{1,0:T(8,128)S(1)}, u32[]{:S(2)}, u32[]{:S(2)}) collective-permute-start(f32[32,2048]{1,0:T(8,128)} %get-tuple-element.32), channel_id=1, source_target_pairs={{0,4},{4,8},{8,12},{12,16},{16,20},{20,24},{24,28},{1,5},{5,9},{9,... | collective-permute-start | bytes 786440 | tf_op jit(solution)/shard_map/ppermute | solution.py:479
  28.4 1.9 collective-permute-start.3
  32.0 2.7 %collective-permute-done.3 = f32[32,2048]{1,0:T(8,128)S(1)} collective-permute-done((f32[32,2048]{1,0:T(8,128)}, f32[32,2048]{1,0:T(8,128)S(1)}, u32[]{:S(2)}, u32[]{:S(2)}) %collective-permute-start.3) | collective-permute-done | bytes 262176 | tf_op jit(solution)/shard_map/ppermute | solution.py:484
  36.1 1.6 collective-permute-start.4
  37.7 11.7 %collective-permute-done.4 = f32[128,1024]{1,0:T(8,128)S(1)} collective-permute-done((f32[128,1024]{1,0:T(8,128)S(1)}, f32[128,1024]{1,0:T(8,128)S(1)}, u32[]{:S(2)}, u32[]{:S(2)}) %collective-permute-start.4) | collective-permute-done | bytes 524320 | tf_op jit(solution)/shard_map/ppermute | solution.py:489
  49.5 2.6 %collective-permute-start.5 = (f32[128,512]{1,0:T(8,128)S(1)}, f32[128,512]{1,0:T(8,128)S(1)}, u32[]{:S(2)}, u32[]{:S(2)}) collective-permute-start(f32[128,512]{1,0:T(8,128)S(1)} %constant_dynamic-slice_fusion), channel_id=1, source_target_pairs={{0,2},{1,3},{2,0},{3,1},{4,6},{5,7},{6,4},{7,5},{8,10},{9,11},{10,... | collective-permute-start | bytes 786440 | tf_op jit(solution)/shard_map/ppermute | solution.py:489
  52.1 3.3 %pack_weights.1 = (f32[264,512]{1,0:T(8,128)}, f32[264,512]{1,0:T(8,128)}, f32[136,512]{1,0:T(8,128)}, f32[128,512]{1,0:T(8,128)}) custom-call(s32[1]{0:T(128)} %bitcast.place, f32[2,128,2048]{2,1,0:T(8,128)} %refs_4_.3, f32[8,512]{1,0:T(8,128)} %select_maximum_fusion.refs_0_.tile), custom_call_target="tpu_custom_call" | custom-call | tf_op jit(solution)/shard_map/pack_weights/pallas_call | solution.py:280
  55.5 1.6 collective-permute-start.13
  57.4 2.5 %collective-permute-start.15 = (f32[136,512]{1,0:T(8,128)}, f32[136,512]{1,0:T(8,128)S(1)}, u32[]{:S(2)}, u32[]{:S(2)}) collective-permute-start(f32[136,512]{1,0:T(8,128)} %get-tuple-element.36), channel_id=1, source_target_pairs={{0,3},{1,2},{2,1},{3,0},{4,7},{5,6},{6,5},{7,4},{8,11},{9,10},{10,... | collective-permute-start | bytes 835592 | tf_op jit(solution)/shard_map/ppermute | solution.py:489
  59.9 5.1 %collective-permute-done.5 = f32[128,512]{1,0:T(8,128)S(1)} collective-permute-done((f32[128,512]{1,0:T(8,128)S(1)}, f32[128,512]{1,0:T(8,128)S(1)}, u32[]{:S(2)}, u32[]{:S(2)}) %collective-permute-start.5) | collective-permute-done | bytes 262176 | tf_op jit(solution)/shard_map/ppermute | solution.py:489
  66.0 1.9 collective-permute-start.10
  68.0 2.7 %collective-permute-start.9 = (f32[32,512]{1,0:T(8,128)S(1)}, f32[32,512]{1,0:T(8,128)S(1)}, u32[]{:S(2)}, u32[]{:S(2)}) collective-permute-start(f32[32,512]{1,0:T(8,128)S(1)} %get-tuple-element.68), channel_id=1, source_target_pairs={{0,4},{4,8},{8,12},{12,16},{16,20},{20,24},{24,28},{1,5},{5,9},{9,... | collective-permute-start | bytes 196616 | tf_op jit(solution)/shard_map/ppermute | solution.py:479
  70.7 3.6 %collective-permute-start.16 = (f32[128,512]{1,0:T(8,128)S(1)}, f32[128,512]{1,0:T(8,128)S(1)}, u32[]{:S(2)}, u32[]{:S(2)}) collective-permute-start(f32[128,512]{1,0:T(8,128)S(1)} %copy-done.19), channel_id=1, source_target_pairs={{0,3},{1,2},{2,1},{3,0},{4,7},{5,6},{6,5},{7,4},{8,11},{9,10},{10,... | collective-permute-start | bytes 786440 | tf_op jit(solution)/shard_map/ppermute | solution.py:489
  74.3 2.1 collective-permute-start.11
  76.5 13.1 %collective-permute-done.15.refs_3_.refs_7_ = f32[136,512]{1,0:T(8,128)S(1)} collective-permute-done((f32[136,512]{1,0:T(8,128)}, f32[136,512]{1,0:T(8,128)S(1)}, u32[]{:S(2)}, u32[]{:S(2)}) %collective-permute-start.15) | collective-permute-done | bytes 278560 | tf_op jit(solution)/shard_map/ppermute | solution.py:489
  89.5 1.3 collective-permute-start.12
  90.9 8.8 %collective-permute-done.14.refs_2_.refs_6_ = f32[264,512]{1,0:T(8,128)S(1)} collective-permute-done((f32[264,512]{1,0:T(8,128)}, f32[264,512]{1,0:T(8,128)S(1)}, u32[]{:S(2)}, u32[]{:S(2)}) %collective-permute-start.14) | collective-permute-done | bytes 540704 | tf_op jit(solution)/shard_map/ppermute | solution.py:489
  100.5 4.5 %setup_matrices.3 = (bf16[8,256,256]{2,1,0:T(8,128)(2,1)}, bf16[8,256,256]{2,1,0:T(8,128)(2,1)}, bf16[8,256,256]{2,1,0:T(8,128)(2,1)}, bf16[4,384,256]{2,1,0:T(8,128)(2,1)}) custom-call(f32[8,512]{1,0:T(8,128)} %select_maximum_fusion.refs_0_.tile, f32[264,512]{1,0:T(8,128)} %copy-done.3, f32[264,512]{1,0:T(8,128)} %copy-done.4, f32[136,512]{1,0:T(8,128)} %copy-done.8), custom_call_target="tpu_custom_call" | custom-call | tf_op jit(solution)/shard_map/setup_matrices/pallas_call | solution.py:88
  105.0 7.0 %collective-permute-done.12 = f32[192,128]{1,0:T(8,128)S(1)} collective-permute-done((f32[192,128]{1,0:T(8,128)S(1)}, f32[192,128]{1,0:T(8,128)S(1)}, u32[]{:S(2)}, u32[]{:S(2)}) %collective-permute-start.12) | collective-permute-done | bytes 98336 | tf_op jit(solution)/shard_map/ppermute | solution.py:484
  113.5 10.7 %shard_map.68 = (f32[64,640]{1,0:T(8,128)}, f32[64,640]{1,0:T(8,128)}, f32[64,640]{1,0:T(8,128)}, f32[8,128]{1,0:T(8,128)}) custom-call(s32[1]{0:T(128)} %bitcast.place, f32[192,768]{1,0:T(8,128)} %pad_maximum_fusion.1.image, bf16[8,256,256]{2,1,0:T(8,128)(2,1)} %get-tuple-element.37.refs_0_, bf16[8,256,256]{2,1,0:T(8,128)(2,1)} %get-tuple-element.38.refs_1_, ...), custom_call_target="tpu_custom_call" | custom-call | flops 12000000000 | bytes 4194304 | tf_op jit(solution)/shard_map/pallas_call | solution.py:351
  124.2 1.9 collective-permute-start.17
  126.1 3.6 %collective-permute-start.18 = (f32[64,640]{1,0:T(8,128)}, f32[64,640]{1,0:T(8,128)S(1)}, u32[]{:S(2)}, u32[]{:S(2)}) collective-permute-start(f32[64,640]{1,0:T(8,128)} %get-tuple-element.42), channel_id=1, source_target_pairs={{4,0},{8,4},{12,8},{16,12},{20,16},{24,20},{28,24},{5,1},{9,5},{13... | collective-permute-start | bytes 491528 | tf_op jit(solution)/shard_map/ppermute | solution.py:484
  134.9 4.8 %collective-permute-start.19 = (f32[192,128]{1,0:T(8,128)S(1)}, f32[192,128]{1,0:T(8,128)S(1)}, u32[]{:S(2)}, u32[]{:S(2)}) collective-permute-start(f32[192,128]{1,0:T(8,128)S(1)} %get-tuple-element.64), channel_id=1, source_target_pairs={{0,1},{1,2},{2,3},{4,5},{5,6},{6,7},{8,9},{9,10},{10,11},{12,13},{... | collective-permute-start | bytes 294920 | tf_op jit(solution)/shard_map/ppermute | solution.py:479
  139.7 1.3 collective-permute-start.20
  141.9 4.7 %collective-permute-done.20 = f32[192,128]{1,0:T(8,128)S(1)} collective-permute-done((f32[192,128]{1,0:T(8,128)S(1)}, f32[192,128]{1,0:T(8,128)S(1)}, u32[]{:S(2)}, u32[]{:S(2)}) %collective-permute-start.20) | collective-permute-done | bytes 98336 | tf_op jit(solution)/shard_map/ppermute | solution.py:484
  147.5 10.7 %shard_map.69 = (f32[32,640]{1,0:T(8,128)}, f32[128,640]{1,0:T(8,128)}, f32[32,640]{1,0:T(8,128)}, f32[8,128]{1,0:T(8,128)}) custom-call(s32[1]{0:T(128)} %bitcast.place, f32[192,768]{1,0:T(8,128)} %copy-done.2, bf16[8,256,256]{2,1,0:T(8,128)(2,1)} %get-tuple-element.37.refs_0_, bf16[8,256,256]{2,1,0:T(8,128)(2,1)} %get-tuple-element.38.refs_1_, ...), custom_call_target="tpu_custom_call" | custom-call | flops 12000000000 | bytes 4194304 | tf_op jit(solution)/shard_map/pallas_call | solution.py:351
  158.9 1.3 collective-permute-start.26
  161.7 2.2 collective-permute-start.24
  164.0 3.3 %collective-permute-start.25 = (f32[32,640]{1,0:T(8,128)}, f32[32,640]{1,0:T(8,128)S(1)}, u32[]{:S(2)}, u32[]{:S(2)}) collective-permute-start(f32[32,640]{1,0:T(8,128)} %get-tuple-element.47.top), channel_id=1, source_target_pairs={{4,0},{8,4},{12,8},{16,12},{20,16},{24,20},{28,24},{5,1},{9,5},{13... | collective-permute-start | bytes 245768 | tf_op jit(solution)/shard_map/ppermute | solution.py:484
  168.0 1.9 collective-permute-start.28
  169.9 2.4 %collective-permute-done.28 = f32[4,8,128]{2,1,0:T(8,128)S(1)} collective-permute-done((f32[4,8,128]{2,1,0:T(8,128)S(1)}, f32[4,8,128]{2,1,0:T(8,128)S(1)}, u32[]{:S(2)}, u32[]{:S(2)}) %collective-permute-start.28) | collective-permute-done | bytes 16416 | tf_op jit(solution)/shard_map/ppermute | solution.py:489
  173.6 2.0 wrap.1.refs_8_
  175.6 3.0 %collective-permute-start.30 = (f32[152,512]{1,0:T(8,128)}, f32[152,512]{1,0:T(8,128)S(1)}, u32[]{:S(2)}, u32[]{:S(2)}) collective-permute-start(f32[152,512]{1,0:T(8,128)} %wrap.1.refs_8_), channel_id=1, source_target_pairs={{0,2},{1,3},{2,0},{3,1},{4,6},{5,7},{6,4},{7,5},{8,10},{9,11},{10,... | collective-permute-start | bytes 933896 | tf_op jit(solution)/shard_map/ppermute | solution.py:489
  178.7 1.9 collective-permute-start.6
  181.6 2.0 collective-permute-start.29
  183.6 20.2 %collective-permute-done.30.refs_10_ = f32[152,512]{1,0:T(8,128)S(1)} collective-permute-done((f32[152,512]{1,0:T(8,128)}, f32[152,512]{1,0:T(8,128)S(1)}, u32[]{:S(2)}, u32[]{:S(2)}) %collective-permute-start.30) | collective-permute-done | bytes 311328 | tf_op jit(solution)/shard_map/ppermute | solution.py:489
  203.8 6.5 %collective-permute-done.7.refs_2_ = f32[128,512]{1,0:T(8,128)S(1)} collective-permute-done((f32[128,512]{1,0:T(8,128)S(1)}, f32[128,512]{1,0:T(8,128)S(1)}, u32[]{:S(2)}, u32[]{:S(2)}) %collective-permute-start.7) | collective-permute-done | bytes 262176 | tf_op jit(solution)/shard_map/ppermute | solution.py:489
  210.3 2.0 collective-permute-start.21
  212.3 2.4 collective-permute-done.22.refs_6_
  214.7 12.1 %collective-permute-done.8.refs_3_ = f32[128,512]{1,0:T(8,128)S(1)} collective-permute-done((f32[128,512]{1,0:T(8,128)S(1)}, f32[128,512]{1,0:T(8,128)S(1)}, u32[]{:S(2)}, u32[]{:S(2)}) %collective-permute-start.8) | collective-permute-done | bytes 262176 | tf_op jit(solution)/shard_map/ppermute | solution.py:489
  226.8 5.2 %collective-permute-done.21.refs_5_ = f32[128,512]{1,0:T(8,128)S(1)} collective-permute-done((f32[128,512]{1,0:T(8,128)}, f32[128,512]{1,0:T(8,128)S(1)}, u32[]{:S(2)}, u32[]{:S(2)}) %collective-permute-start.21) | collective-permute-done | bytes 262176 | tf_op jit(solution)/shard_map/ppermute | solution.py:489
  232.0 2.8 %collective-permute-done.23.refs_7_ = f32[128,512]{1,0:T(8,128)S(1)} collective-permute-done((f32[128,512]{1,0:T(8,128)S(1)}, f32[128,512]{1,0:T(8,128)S(1)}, u32[]{:S(2)}, u32[]{:S(2)}) %collective-permute-start.23) | collective-permute-done | bytes 262176 | tf_op jit(solution)/shard_map/ppermute | solution.py:489
  236.3 4.0 %final_images.1 = (f32[128,2048]{1,0:T(8,128)}, f32[128,2048]{1,0:T(8,128)}) custom-call(s32[1]{0:T(128)} %bitcast.place, f32[128,2048]{1,0:T(8,128)} %est.3, f32[128,512]{1,0:T(8,128)} %copy-done, f32[128,512]{1,0:T(8,128)} %copy-done.10, f32[128,512]{1,0:T(8,128)} %copy-done.9, f32[128,512]{1,0:T(8,128)} %copy-done.12, f32[128,512]{1,0:T(8,128)} %copy-done.1, ...), custom_call_target="tpu_custom_call" | custom-call | tf_op jit(solution)/shard_map/final_images/pallas_call | solution.py:467
  (101 shorter events, 22.7 us)
Async XLA Ops:
  1.7 8.9 %collective-permute-start = (f32[32,2048]{1,0:T(8,128)S(1)}, f32[32,2048]{1,0:T(8,128)S(1)}, u32[]{:S(2)}, u32[]{:S(2)}) collective-permute-start(f32[32,2048]{1,0:T(8,128)S(1)} %get-tuple-element.61), channel_id=1, source_target_pairs={{0,4},{4,8},{8,12},{12,16},{16,20},{20,24},{24,28},{1,5},{5,9},{9,... | collective-permute-start | bytes 786440 | tf_op jit(solution)/shard_map/ppermute | solution.py:479
  3.6 7.6 %collective-permute-start.1 = (f32[32,2048]{1,0:T(8,128)S(1)}, f32[32,2048]{1,0:T(8,128)S(1)}, u32[]{:S(2)}, u32[]{:S(2)}) collective-permute-start(f32[32,2048]{1,0:T(8,128)S(1)} %get-tuple-element.60), channel_id=1, source_target_pairs={{4,0},{8,4},{12,8},{16,12},{20,16},{24,20},{28,24},{5,1},{9,5},{13... | collective-permute-start | bytes 786440 | tf_op jit(solution)/shard_map/ppermute | solution.py:484
  23.9 8.1 %collective-permute-start.2 = (f32[32,2048]{1,0:T(8,128)}, f32[32,2048]{1,0:T(8,128)S(1)}, u32[]{:S(2)}, u32[]{:S(2)}) collective-permute-start(f32[32,2048]{1,0:T(8,128)} %get-tuple-element.32), channel_id=1, source_target_pairs={{0,4},{4,8},{8,12},{12,16},{16,20},{20,24},{24,28},{1,5},{5,9},{9,... | collective-permute-start | bytes 786440 | tf_op jit(solution)/shard_map/ppermute | solution.py:479
  28.4 6.3 %collective-permute-start.3 = (f32[32,2048]{1,0:T(8,128)}, f32[32,2048]{1,0:T(8,128)S(1)}, u32[]{:S(2)}, u32[]{:S(2)}) collective-permute-start(f32[32,2048]{1,0:T(8,128)} %get-tuple-element.33), channel_id=1, source_target_pairs={{4,0},{8,4},{12,8},{16,12},{20,16},{24,20},{28,24},{5,1},{9,5},{13... | collective-permute-start | bytes 786440 | tf_op jit(solution)/shard_map/ppermute | solution.py:484
  36.1 13.3 %collective-permute-start.4 = (f32[128,1024]{1,0:T(8,128)S(1)}, f32[128,1024]{1,0:T(8,128)S(1)}, u32[]{:S(2)}, u32[]{:S(2)}) collective-permute-start(f32[128,1024]{1,0:T(8,128)S(1)} %pad_maximum_fusion.2), channel_id=1, source_target_pairs={{0,1},{1,0},{2,3},{3,2},{4,5},{5,4},{6,7},{7,6},{8,9},{9,8},{10,11... | collective-permute-start | bytes 1572872 | tf_op jit(solution)/shard_map/ppermute | solution.py:489
  49.5 15.5 %collective-permute-start.5 = (f32[128,512]{1,0:T(8,128)S(1)}, f32[128,512]{1,0:T(8,128)S(1)}, u32[]{:S(2)}, u32[]{:S(2)}) collective-permute-start(f32[128,512]{1,0:T(8,128)S(1)} %constant_dynamic-slice_fusion), channel_id=1, source_target_pairs={{0,2},{1,3},{2,0},{3,1},{4,6},{5,7},{6,4},{7,5},{8,10},{9,11},{10,... | collective-permute-start | bytes 786440 | tf_op jit(solution)/shard_map/ppermute | solution.py:489
  55.4 15.3 %copy-start.19 = (f32[128,512]{1,0:T(8,128)S(1)}, f32[128,512]{1,0:T(8,128)}, u32[]{:S(2)}) copy-start(f32[128,512]{1,0:T(8,128)} %get-tuple-element.41) | copy-start | bytes 786436
  55.5 35.4 %collective-permute-start.13 = (f32[264,512]{1,0:T(8,128)}, f32[264,512]{1,0:T(8,128)S(1)}, u32[]{:S(2)}, u32[]{:S(2)}) collective-permute-start(f32[264,512]{1,0:T(8,128)} %get-tuple-element.34), channel_id=1, source_target_pairs={{0,1},{1,0},{2,3},{3,2},{4,5},{5,4},{6,7},{7,6},{8,9},{9,8},{10,11... | collective-permute-start | bytes 1622024 | tf_op jit(solution)/shard_map/ppermute | solution.py:489
  57.1 42.6 %collective-permute-start.14 = (f32[264,512]{1,0:T(8,128)}, f32[264,512]{1,0:T(8,128)S(1)}, u32[]{:S(2)}, u32[]{:S(2)}) collective-permute-start(f32[264,512]{1,0:T(8,128)} %get-tuple-element.35), channel_id=1, source_target_pairs={{0,2},{1,3},{2,0},{3,1},{4,6},{5,7},{6,4},{7,5},{8,10},{9,11},{10,... | collective-permute-start | bytes 1622024 | tf_op jit(solution)/shard_map/ppermute | solution.py:489
  57.4 32.1 %collective-permute-start.15 = (f32[136,512]{1,0:T(8,128)}, f32[136,512]{1,0:T(8,128)S(1)}, u32[]{:S(2)}, u32[]{:S(2)}) collective-permute-start(f32[136,512]{1,0:T(8,128)} %get-tuple-element.36), channel_id=1, source_target_pairs={{0,3},{1,2},{2,1},{3,0},{4,7},{5,6},{6,5},{7,4},{8,11},{9,10},{10,... | collective-permute-start | bytes 835592 | tf_op jit(solution)/shard_map/ppermute | solution.py:489
  66.0 112.7 %copy-start = (f32[128,512]{1,0:T(8,128)}, f32[128,512]{1,0:T(8,128)S(1)}, u32[]{:S(2)}) copy-start(f32[128,512]{1,0:T(8,128)S(1)} %neg.3.refs_0_) | copy-start | bytes 786436
  66.0 4.7 %collective-permute-start.10 = (f32[32,512]{1,0:T(8,128)S(1)}, f32[32,512]{1,0:T(8,128)S(1)}, u32[]{:S(2)}, u32[]{:S(2)}) collective-permute-start(f32[32,512]{1,0:T(8,128)S(1)} %get-tuple-element.69), channel_id=1, source_target_pairs={{4,0},{8,4},{12,8},{16,12},{20,16},{24,20},{28,24},{5,1},{9,5},{13... | collective-permute-start | bytes 196616 | tf_op jit(solution)/shard_map/ppermute | solution.py:484
  68.0 6.3 %collective-permute-start.9 = (f32[32,512]{1,0:T(8,128)S(1)}, f32[32,512]{1,0:T(8,128)S(1)}, u32[]{:S(2)}, u32[]{:S(2)}) collective-permute-start(f32[32,512]{1,0:T(8,128)S(1)} %get-tuple-element.68), channel_id=1, source_target_pairs={{0,4},{4,8},{8,12},{12,16},{16,20},{20,24},{24,28},{1,5},{5,9},{9,... | collective-permute-start | bytes 196616 | tf_op jit(solution)/shard_map/ppermute | solution.py:479
  70.7 42.1 %collective-permute-start.16 = (f32[128,512]{1,0:T(8,128)S(1)}, f32[128,512]{1,0:T(8,128)S(1)}, u32[]{:S(2)}, u32[]{:S(2)}) collective-permute-start(f32[128,512]{1,0:T(8,128)S(1)} %copy-done.19), channel_id=1, source_target_pairs={{0,3},{1,2},{2,1},{3,0},{4,7},{5,6},{6,5},{7,4},{8,11},{9,10},{10,... | collective-permute-start | bytes 786440 | tf_op jit(solution)/shard_map/ppermute | solution.py:489
  74.3 30.6 %collective-permute-start.11 = (f32[192,128]{1,0:T(8,128)S(1)}, f32[192,128]{1,0:T(8,128)S(1)}, u32[]{:S(2)}, u32[]{:S(2)}) collective-permute-start(f32[192,128]{1,0:T(8,128)S(1)} %get-tuple-element.66), channel_id=1, source_target_pairs={{0,1},{1,2},{2,3},{4,5},{5,6},{6,7},{8,9},{9,10},{10,11},{12,13},{... | collective-permute-start | bytes 294920 | tf_op jit(solution)/shard_map/ppermute | solution.py:479
  89.5 10.1 %copy-start.8 = (f32[136,512]{1,0:T(8,128)}, f32[136,512]{1,0:T(8,128)S(1)}, u32[]{:S(2)}) copy-start(f32[136,512]{1,0:T(8,128)S(1)} %collective-permute-done.15.refs_3_.refs_7_) | copy-start | bytes 835588
  89.5 22.4 %collective-permute-start.12 = (f32[192,128]{1,0:T(8,128)S(1)}, f32[192,128]{1,0:T(8,128)S(1)}, u32[]{:S(2)}, u32[]{:S(2)}) collective-permute-start(f32[192,128]{1,0:T(8,128)S(1)} %get-tuple-element.67), channel_id=1, source_target_pairs={{1,0},{2,1},{3,2},{5,4},{6,5},{7,6},{9,8},{10,9},{11,10},{13,12},{... | collective-permute-start | bytes 294920 | tf_op jit(solution)/shard_map/ppermute | solution.py:484
  90.9 8.8 %copy-start.3 = (f32[264,512]{1,0:T(8,128)}, f32[264,512]{1,0:T(8,128)S(1)}, u32[]{:S(2)}) copy-start(f32[264,512]{1,0:T(8,128)S(1)} %collective-permute-done.13.refs_1_.refs_5_) | copy-start | bytes 1622020
  99.7 0.8 copy-start.4
  124.2 6.8 %collective-permute-start.17 = (f32[64,640]{1,0:T(8,128)}, f32[64,640]{1,0:T(8,128)S(1)}, u32[]{:S(2)}, u32[]{:S(2)}) collective-permute-start(f32[64,640]{1,0:T(8,128)} %get-tuple-element.43), channel_id=1, source_target_pairs={{0,4},{4,8},{8,12},{12,16},{16,20},{20,24},{24,28},{1,5},{5,9},{9,... | collective-permute-start | bytes 491528 | tf_op jit(solution)/shard_map/ppermute | solution.py:479
  126.1 6.8 %collective-permute-start.18 = (f32[64,640]{1,0:T(8,128)}, f32[64,640]{1,0:T(8,128)S(1)}, u32[]{:S(2)}, u32[]{:S(2)}) collective-permute-start(f32[64,640]{1,0:T(8,128)} %get-tuple-element.42), channel_id=1, source_target_pairs={{4,0},{8,4},{12,8},{16,12},{20,16},{24,20},{28,24},{5,1},{9,5},{13... | collective-permute-start | bytes 491528 | tf_op jit(solution)/shard_map/ppermute | solution.py:484
  134.9 7.0 %collective-permute-start.19 = (f32[192,128]{1,0:T(8,128)S(1)}, f32[192,128]{1,0:T(8,128)S(1)}, u32[]{:S(2)}, u32[]{:S(2)}) collective-permute-start(f32[192,128]{1,0:T(8,128)S(1)} %get-tuple-element.64), channel_id=1, source_target_pairs={{0,1},{1,2},{2,3},{4,5},{5,6},{6,7},{8,9},{9,10},{10,11},{12,13},{... | collective-permute-start | bytes 294920 | tf_op jit(solution)/shard_map/ppermute | solution.py:479
  139.7 6.9 %collective-permute-start.20 = (f32[192,128]{1,0:T(8,128)S(1)}, f32[192,128]{1,0:T(8,128)S(1)}, u32[]{:S(2)}, u32[]{:S(2)}) collective-permute-start(f32[192,128]{1,0:T(8,128)S(1)} %get-tuple-element.65), channel_id=1, source_target_pairs={{1,0},{2,1},{3,2},{5,4},{6,5},{7,6},{9,8},{10,9},{11,10},{13,12},{... | collective-permute-start | bytes 294920 | tf_op jit(solution)/shard_map/ppermute | solution.py:484
  146.7 0.8 copy-start.2
  146.8 11.5 %copy-start.1 = (f32[128,512]{1,0:T(8,128)}, f32[128,512]{1,0:T(8,128)S(1)}, u32[]{:S(2)}) copy-start(f32[128,512]{1,0:T(8,128)S(1)} %slice.62.before.refs_4_) | copy-start | bytes 786436
  147.5 10.7 %copy-start.17 = (f32[8,128]{1,0:T(8,128)S(1)}, f32[8,128]{1,0:T(8,128)}, u32[]{:S(2)}) copy-start(f32[8,128]{1,0:T(8,128)} %get-tuple-element.50) | copy-start | bytes 12292
  158.9 2.1 collective-permute-start.26
  161.7 5.6 %collective-permute-start.27 = (f32[4,8,128]{2,1,0:T(8,128)S(1)}, f32[4,8,128]{2,1,0:T(8,128)S(1)}, u32[]{:S(2)}, u32[]{:S(2)}) collective-permute-start(f32[4,8,128]{2,1,0:T(8,128)S(1)} %fusion.1), channel_id=1, source_target_pairs={{0,8},{4,12},{8,0},{12,4},{16,24},{20,28},{24,16},{28,20},{1,9},{5... | collective-permute-start | bytes 49160 | tf_op jit(solution)/shard_map/ppermute | solution.py:489
  161.7 11.2 %collective-permute-start.24 = (f32[32,640]{1,0:T(8,128)}, f32[32,640]{1,0:T(8,128)S(1)}, u32[]{:S(2)}, u32[]{:S(2)}) collective-permute-start(f32[32,640]{1,0:T(8,128)} %get-tuple-element.49.bot), channel_id=1, source_target_pairs={{0,4},{4,8},{8,12},{12,16},{16,20},{20,24},{24,28},{1,5},{5,9},{9,... | collective-permute-start | bytes 245768 | tf_op jit(solution)/shard_map/ppermute | solution.py:479
  164.0 8.9 %collective-permute-start.25 = (f32[32,640]{1,0:T(8,128)}, f32[32,640]{1,0:T(8,128)S(1)}, u32[]{:S(2)}, u32[]{:S(2)}) collective-permute-start(f32[32,640]{1,0:T(8,128)} %get-tuple-element.47.top), channel_id=1, source_target_pairs={{4,0},{8,4},{12,8},{16,12},{20,16},{24,20},{28,24},{5,1},{9,5},{13... | collective-permute-start | bytes 245768 | tf_op jit(solution)/shard_map/ppermute | solution.py:484
  168.0 4.3 %collective-permute-start.28 = (f32[4,8,128]{2,1,0:T(8,128)S(1)}, f32[4,8,128]{2,1,0:T(8,128)S(1)}, u32[]{:S(2)}, u32[]{:S(2)}) collective-permute-start(f32[4,8,128]{2,1,0:T(8,128)S(1)} %fusion.5), channel_id=1, source_target_pairs={{0,16},{4,20},{8,24},{12,28},{16,0},{20,4},{24,8},{28,12},{1,17},{... | collective-permute-start | bytes 49160 | tf_op jit(solution)/shard_map/ppermute | solution.py:489
  175.6 28.2 %collective-permute-start.30 = (f32[152,512]{1,0:T(8,128)}, f32[152,512]{1,0:T(8,128)S(1)}, u32[]{:S(2)}, u32[]{:S(2)}) collective-permute-start(f32[152,512]{1,0:T(8,128)} %wrap.1.refs_8_), channel_id=1, source_target_pairs={{0,2},{1,3},{2,0},{3,1},{4,6},{5,7},{6,4},{7,5},{8,10},{9,11},{10,... | collective-permute-start | bytes 933896 | tf_op jit(solution)/shard_map/ppermute | solution.py:489
  178.6 31.6 %collective-permute-start.7 = (f32[128,512]{1,0:T(8,128)S(1)}, f32[128,512]{1,0:T(8,128)S(1)}, u32[]{:S(2)}, u32[]{:S(2)}) collective-permute-start(f32[128,512]{1,0:T(8,128)S(1)} %neg.3.refs_0_), channel_id=1, source_target_pairs={{0,2},{1,3},{2,0},{3,1},{4,6},{5,7},{6,4},{7,5},{8,10},{9,11},{10,... | collective-permute-start | bytes 786440 | tf_op jit(solution)/shard_map/ppermute | solution.py:489
  178.7 31.6 %collective-permute-start.6 = (f32[128,512]{1,0:T(8,128)S(1)}, f32[128,512]{1,0:T(8,128)S(1)}, u32[]{:S(2)}, u32[]{:S(2)}) collective-permute-start(f32[128,512]{1,0:T(8,128)S(1)} %neg.3.refs_0_), channel_id=1, source_target_pairs={{0,1},{1,0},{2,3},{3,2},{4,5},{5,4},{6,7},{7,6},{8,9},{9,8},{10,11... | collective-permute-start | bytes 786440 | tf_op jit(solution)/shard_map/ppermute | solution.py:489
  180.6 34.1 %collective-permute-start.22 = (f32[128,512]{1,0:T(8,128)}, f32[128,512]{1,0:T(8,128)S(1)}, u32[]{:S(2)}, u32[]{:S(2)}) collective-permute-start(f32[128,512]{1,0:T(8,128)} %copy-done.1), channel_id=1, source_target_pairs={{0,2},{1,3},{2,0},{3,1},{4,6},{5,7},{6,4},{7,5},{8,10},{9,11},{10,... | collective-permute-start | bytes 786440 | tf_op jit(solution)/shard_map/ppermute | solution.py:489
  181.6 50.4 %collective-permute-start.29 = (f32[152,512]{1,0:T(8,128)}, f32[152,512]{1,0:T(8,128)S(1)}, u32[]{:S(2)}, u32[]{:S(2)}) collective-permute-start(f32[152,512]{1,0:T(8,128)} %wrap.1.refs_8_), channel_id=1, source_target_pairs={{0,1},{1,0},{2,3},{3,2},{4,5},{5,4},{6,7},{7,6},{8,9},{9,8},{10,11... | collective-permute-start | bytes 933896 | tf_op jit(solution)/shard_map/ppermute | solution.py:489
  203.8 31.0 %copy-start.5 = (f32[152,512]{1,0:T(8,128)}, f32[152,512]{1,0:T(8,128)S(1)}, u32[]{:S(2)}) copy-start(f32[152,512]{1,0:T(8,128)S(1)} %collective-permute-done.30.refs_10_) | copy-start | bytes 933892
  203.8 31.0 %collective-permute-start.31 = (f32[152,512]{1,0:T(8,128)S(1)}, f32[152,512]{1,0:T(8,128)S(1)}, u32[]{:S(2)}, u32[]{:S(2)}) collective-permute-start(f32[152,512]{1,0:T(8,128)S(1)} %collective-permute-done.30.refs_10_), channel_id=1, source_target_pairs={{0,1},{1,0},{2,3},{3,2},{4,5},{5,4},{6,7},{7,6},{8,9},{9,8},{10,11... | collective-permute-start | bytes 933896 | tf_op jit(solution)/shard_map/ppermute | solution.py:489
  210.3 24.5 %copy-start.9 = (f32[128,512]{1,0:T(8,128)}, f32[128,512]{1,0:T(8,128)S(1)}, u32[]{:S(2)}) copy-start(f32[128,512]{1,0:T(8,128)S(1)} %collective-permute-done.7.refs_2_) | copy-start | bytes 786436
  210.3 16.5 %collective-permute-start.8 = (f32[128,512]{1,0:T(8,128)S(1)}, f32[128,512]{1,0:T(8,128)S(1)}, u32[]{:S(2)}, u32[]{:S(2)}) collective-permute-start(f32[128,512]{1,0:T(8,128)S(1)} %collective-permute-done.7.refs_2_), channel_id=1, source_target_pairs={{0,1},{1,0},{2,3},{3,2},{4,5},{5,4},{6,7},{7,6},{8,9},{9,8},{10,11... | collective-permute-start | bytes 786440 | tf_op jit(solution)/shard_map/ppermute | solution.py:489
  210.3 24.5 %copy-start.10 = (f32[128,512]{1,0:T(8,128)}, f32[128,512]{1,0:T(8,128)S(1)}, u32[]{:S(2)}) copy-start(f32[128,512]{1,0:T(8,128)S(1)} %collective-permute-done.6.refs_1_) | copy-start | bytes 786436
  210.3 21.7 %collective-permute-start.21 = (f32[128,512]{1,0:T(8,128)}, f32[128,512]{1,0:T(8,128)S(1)}, u32[]{:S(2)}, u32[]{:S(2)}) collective-permute-start(f32[128,512]{1,0:T(8,128)} %copy-done.1), channel_id=1, source_target_pairs={{0,1},{1,0},{2,3},{3,2},{4,5},{5,4},{6,7},{7,6},{8,9},{9,8},{10,11... | collective-permute-start | bytes 786440 | tf_op jit(solution)/shard_map/ppermute | solution.py:489
  214.7 20.1 %copy-start.11 = (f32[128,512]{1,0:T(8,128)}, f32[128,512]{1,0:T(8,128)S(1)}, u32[]{:S(2)}) copy-start(f32[128,512]{1,0:T(8,128)S(1)} %collective-permute-done.22.refs_6_) | copy-start | bytes 786436
  214.7 20.1 %collective-permute-start.23 = (f32[128,512]{1,0:T(8,128)S(1)}, f32[128,512]{1,0:T(8,128)S(1)}, u32[]{:S(2)}, u32[]{:S(2)}) collective-permute-start(f32[128,512]{1,0:T(8,128)S(1)} %collective-permute-done.22.refs_6_), channel_id=1, source_target_pairs={{0,1},{1,0},{2,3},{3,2},{4,5},{5,4},{6,7},{7,6},{8,9},{9,8},{10,11... | collective-permute-start | bytes 786440 | tf_op jit(solution)/shard_map/ppermute | solution.py:489
  226.8 8.0 %copy-start.12 = (f32[128,512]{1,0:T(8,128)}, f32[128,512]{1,0:T(8,128)S(1)}, u32[]{:S(2)}) copy-start(f32[128,512]{1,0:T(8,128)S(1)} %collective-permute-done.8.refs_3_) | copy-start | bytes 786436
  232.0 2.9 %copy-start.13 = (f32[128,512]{1,0:T(8,128)}, f32[128,512]{1,0:T(8,128)S(1)}, u32[]{:S(2)}) copy-start(f32[128,512]{1,0:T(8,128)S(1)} %collective-permute-done.21.refs_5_) | copy-start | bytes 786436
  232.0 2.9 %copy-start.6 = (f32[152,512]{1,0:T(8,128)}, f32[152,512]{1,0:T(8,128)S(1)}, u32[]{:S(2)}) copy-start(f32[152,512]{1,0:T(8,128)S(1)} %collective-permute-done.29.refs_9_) | copy-start | bytes 933892
  235.5 0.7 copy-start.7
  (6 other events, 4.1 us)

commit v3 on v2

--- a/solution.py
+++ b/solution.py
@@ -94,7 +94,6 @@
             pltpu.VMEM((groups, height, 2 * LANE), f32),
             pltpu.SemaphoreType.DMA((groups,)),
         ],
-        name="setup_matrices",
     )(*tiles_in)
 
 
@@ -374,7 +373,7 @@
     )(place, image, t, b, bp, ta, weights, *moved)
 
 
-def wrap_kernel(rows, halo, w, top, mid, bot, up, dn, before, sums, out):
+def wrap_kernel(rows, halo, w, top, mid, bot, up, dn, before, out):
     keep = rows - 2 * halo
     pieces = (
         (0, halo, mid[:halo, :] + up[...]),
@@ -398,35 +397,29 @@
             part = pltpu.roll(part, p * 2 * halo, 1) if p else part
             tile = part if tile is None else jnp.where(lane >= p * 2 * halo, part, tile)
         out[rows : rows + short, t * LANE : (t + 1) * LANE] = tile
-    out[rows + short :, :] = jnp.zeros((8, w), f32)
-    for i in range(4):
-        out[rows + short + i : rows + short + i + 1, :LANE] = jnp.sum(sums[i], axis=0, keepdims=True)
-
-
-def wrap(top, mid, bot, up, dn, before, sums, halo):
+
+
+def wrap(top, mid, bot, up, dn, before, halo):
     rows, w = before.shape
-    height = rows + rows * 2 * halo // w + 8
+    height = rows + rows * 2 * halo // w
     return pl.pallas_call(
         functools.partial(wrap_kernel, rows, halo, w),
         out_shape=jax.ShapeDtypeStruct((height, w), f32),
-        in_specs=[VMEM] * 7,
+        in_specs=[VMEM] * 6,
         out_specs=VMEM,
         name="wrap",
-    )(top, mid, bot, up, dn, before, sums)
-
-
-def final_kernel(n, rows, halo, w, place, est, *refs):
+    )(top, mid, bot, up, dn, before)
+
+
+def final_kernel(n, rows, halo, w, place, est, sums, *refs):
     k0, k1, k2 = refs[:n], refs[n : 2 * n], refs[2 * n : 3 * n]
     sol, res, full = refs[3 * n :]
     short = rows * 2 * halo // w
     per = LANE // (2 * halo)
-    total = k2[0][rows + short :, :LANE]
-    for i in range(1, n):
-        total = total + k2[i][rows + short :, :LANE]
-    total = jnp.sum(total, axis=1, keepdims=True)
-    k00, k11 = total[0:1], total[2:3]
-    k01 = total[1:2] + damping * k00
-    k12 = total[3:4] + damping * k11
+    total = [jnp.sum(jnp.sum(sums[i], axis=0, keepdims=True), axis=1, keepdims=True) for i in range(4)]
+    k00, k11 = total[0], total[2]
+    k01 = total[1] + damping * k00
+    k12 = total[3] + damping * k11
     alpha0 = k00 / k01
     norm1 = k00 - 2.0 * alpha0 * k01 + alpha0 * alpha0 * k11
     beta = norm1 / k00
@@ -461,17 +454,17 @@
         res[:, cols] = a0 - c1 * a1 + c2 * full[:, pl.ds(pl.multiple_of(spot[i] * w + LANE, LANE), w)]
 
 
-def final_images(place, est, k0, k1, k2, halo):
+def final_images(place, est, sums, k0, k1, k2, halo):
     n = len(k0)
     rows, w = k0[0].shape
     return pl.pallas_call(
         functools.partial(final_kernel, n, rows, halo, w),
         out_shape=[jax.ShapeDtypeStruct(est.shape, f32)] * 2,
-        in_specs=[pl.BlockSpec(memory_space=pltpu.SMEM)] + [VMEM] * (1 + 3 * n),
+        in_specs=[pl.BlockSpec(memory_space=pltpu.SMEM)] + [VMEM] * (2 + 3 * n),
         out_specs=[VMEM] * 2,
         scratch_shapes=[pltpu.VMEM((rows, n * w + 2 * LANE), f32)],
         name="final_images",
-    )(place, est, *k0, *k1, *k2)
+    )(place, est, sums, *k0, *k1, *k2)
 
 
 def shift_up(x, axis):
@@ -537,18 +530,11 @@
         [mid[:halo] + from_up, mid[halo : rows - halo], mid[rows - halo :] + from_dn], axis=0
     )
 
-    for d in distances:
-        bit = (me // d) % 2
-        half = left.shape[1] // w // 2
-
-        def pick(which, left=left, half=half):
-            return jnp.concatenate(
-                [block_of(left, 2 * i + which) for i in range(half)], axis=1
-            )
-
-        sent = swap(pick(1 - bit), "frame", d)
-        left = pick(bit) + sent
-    k0 = -(left + damping * block_of(estimate, me))
+    part = [block_of(left, me ^ i) for i in range(n)]
+    for i in range(n - 1, 0, -1):
+        d = i & -i
+        part[i ^ d] = part[i ^ d] + swap(part[i], "frame", d)
+    k0 = -(part[0] + damping * block_of(estimate, me))
     k00_part = fold(k0 * k0)
 
     lane = lax.broadcasted_iota(jnp.int32, (ext, LANE), 1)
@@ -598,21 +584,14 @@
     up = shift_up(bot, "strip")
     dn = shift_down(top, "strip")
     sums = jnp.stack([k00_part, stat1, k11_part, stat2])
-    d = 1
-    while d < strips:
-        sums = sums + swap(sums, "strip", d)
-        d *= 2
-    k2 = wrap(top, mid, bot, up, dn, k1, sums, halo)
+    for axis, size in (("frame", n), ("strip", strips)):
+        d = 1
+        while d < size:
+            sums = sums + swap(sums, axis, d)
+            d *= 2
+    k2 = wrap(top, mid, bot, up, dn, k1, halo)
 
     def gathered(x):
-        parts = [x] + [None] * (n - 1)
-        for d in reversed(distances):
-            known = [i for i in range(n) if parts[i] is not None]
-            for i in known:
-                parts[i ^ d] = swap(parts[i], "frame", d)
-        return parts
-
-    def gathered_soon(x):
         parts = [x] + [None] * (n - 1)
         for i in range(n):
             for d in reversed(distances):
@@ -620,8 +599,8 @@
                     parts[i + d] = swap(parts[i], "frame", d)
         return parts
 
-    g0, g1, g2 = gathered(k0), gathered(k1), gathered_soon(k2)
-    return tuple(final_images(place, estimate, g0, g1, g2, halo))
+    g0, g1, g2 = gathered(k0), gathered(k1), gathered(k2)
+    return tuple(final_images(place, estimate, sums, g0, g1, g2, halo))
 
 
 def solution(mesh):

time: 244 us -> 242 us (level); the launches traced: 240 us -> 241 us
  starting transfers between devices: 62.7 us -> 69.9 us
  waiting for transfers between devices: 110 us -> 103 us
    ppermute x7, starting transfers between devices: 20.2 us -> 30.7 us  [shift_up(): return lax.ppermute(x, axis, [(i, i + 1) for i in range(n - 1)])]
    ppermute x18 -> x21, starting transfers between devices: 25.5 us -> 20.9 us  [swap(): return lax.ppermute(x, axis, [(i, i ^ distance) for i in range(n)])]
    ppermute x7, waiting for transfers between devices: 15.9 us -> 12.2 us  [shift_down(): return lax.ppermute(x, axis, [(i + 1, i) for i in range(n - 1)])]
    ppermute x18 -> x21, waiting for transfers between devices: 91.1 us -> 88.6 us  [swap(): return lax.ppermute(x, axis, [(i, i ^ distance) for i in range(n)])]
    unnamed x44 -> x46, local copies, waits for them, and re-layouts: 4.92 us -> 5.82 us
  transfers between devices with their start and end apart: 32 -> 35, of which waited for: 20 -> 21; matrix products, arithmetic and copies ran while one was open for 3% -> 3% of each run, Pallas kernels for 4% -> 5%
where the time goes in v3:
time: 242 us; the launch traced here: 241 us
  waiting for transfers between devices  103 us (43%)
  starting transfers between devices  69.9 us (29%)
  Pallas kernels  49.2 us (20%)
  other arithmetic  9.13 us (4%)
  local copies, waits for them, and re-layouts  8.06 us (3%)
    ppermute x21, waiting for transfers between devices, swap(): return lax.ppermute(x, axis, [(i, i ^ distance) for i in range(n)])  88.6 us
    ppermute x7, starting transfers between devices, shift_up(): return lax.ppermute(x, axis, [(i, i + 1) for i in range(n - 1)])  30.7 us
    pallas_call x2, Pallas kernels, apply_terms(): pl.pallas_call(functools.partial(apply_kernel, frames, rows, halo, w, gro...  21.4 us
    ppermute x21, starting transfers between devices, swap(): return lax.ppermute(x, axis, [(i, i ^ distance) for i in range(n)])  20.9 us
    ppermute x7, starting transfers between devices, shift_down(): return lax.ppermute(x, axis, [(i + 1, i) for i in range(n - 1)])  18.3 us
    ppermute x7, waiting for transfers between devices, shift_down(): return lax.ppermute(x, axis, [(i + 1, i) for i in range(n - 1)])  12.2 us
    pallas_call x1, Pallas kernels, first_terms(): pl.pallas_call(functools.partial(first_kernel, frames, rows, halo, w), ou...  12 us
    pallas_call x2, Pallas kernels, setup_matrices(): pl.pallas_call(functools.partial(setup_kernel, frames, rows, halo, [(star...  6.46 us
  transfers between devices with their start and end apart: 35, of which 21 were waited for; matrix products, arithmetic and copies ran while one was open for 3% of the time, Pallas kernels for 5%

profile of v3, /device:TPU:2, one launch (start us, length us, event | category | flops | bytes accessed | tf_op | source)
XLA Modules:
  0.0 240.9 jit_solution(9699454442413485922)
XLA Ops:
  1.7 1.9 collective-permute-start
  3.6 3.6 %collective-permute-start.1 = (f32[32,2048]{1,0:T(8,128)S(1)}, f32[32,2048]{1,0:T(8,128)S(1)}, u32[]{:S(2)}, u32[]{:S(2)}) collective-permute-start(f32[32,2048]{1,0:T(8,128)S(1)} %get-tuple-element.58), channel_id=1, source_target_pairs={{4,0},{8,4},{12,8},{16,12},{20,16},{24,20},{28,24},{5,1},{9,5},{13... | collective-permute-start | bytes 786440 | tf_op jit(solution)/shard_map/ppermute | solution.py:477
  7.3 1.3 select_maximum_fusion.refs_0_.tile
  8.6 2.0 shard_map.68
  11.9 12.0 %first_terms.1 = (f32[32,2048]{1,0:T(8,128)}, f32[128,2048]{1,0:T(8,128)}, f32[32,2048]{1,0:T(8,128)}) custom-call(f32[128,2048]{1,0:T(8,128)} %est.3, f32[32,2048]{1,0:T(8,128)} %copy-done.21, f32[32,2048]{1,0:T(8,128)} %copy-done.22, bf16[2,256,256]{2,1,0:T(8,128)(2,1)} %get-tuple-element.27.t_ref, bf16[2,256,256]{2,1,0:T(8,128)(2,1)} %get-tuple-element.28.b_ref, ...), custom_call_target="tpu_custom_call" | custom-call | flops 8000000000 | bytes 8388608 | tf_op jit(solution)/shard_map/first_terms/pallas_call | solution.py:235
  23.9 4.5 %collective-permute-start.2 = (f32[32,2048]{1,0:T(8,128)}, f32[32,2048]{1,0:T(8,128)S(1)}, u32[]{:S(2)}, u32[]{:S(2)}) collective-permute-start(f32[32,2048]{1,0:T(8,128)} %get-tuple-element.32), channel_id=1, source_target_pairs={{0,4},{4,8},{8,12},{12,16},{16,20},{20,24},{24,28},{1,5},{5,9},{9,... | collective-permute-start | bytes 786440 | tf_op jit(solution)/shard_map/ppermute | solution.py:472
  28.4 1.9 collective-permute-start.3
  32.0 2.8 %collective-permute-done.3 = f32[32,2048]{1,0:T(8,128)S(1)} collective-permute-done((f32[32,2048]{1,0:T(8,128)}, f32[32,2048]{1,0:T(8,128)S(1)}, u32[]{:S(2)}, u32[]{:S(2)}) %collective-permute-start.3) | collective-permute-done | bytes 262176 | tf_op jit(solution)/shard_map/ppermute | solution.py:477
  34.7 1.1 slice_add_fusion.2
  36.0 1.6 collective-permute-start.4
  37.6 6.1 %collective-permute-done.4 = f32[128,512]{1,0:T(8,128)S(1)} collective-permute-done((f32[128,512]{1,0:T(8,128)S(1)}, f32[128,512]{1,0:T(8,128)S(1)}, u32[]{:S(2)}, u32[]{:S(2)}) %collective-permute-start.4) | collective-permute-done | bytes 262176 | tf_op jit(solution)/shard_map/ppermute | solution.py:482
  43.7 2.6 %collective-permute-start.5 = (f32[128,512]{1,0:T(8,128)S(1)}, f32[128,512]{1,0:T(8,128)S(1)}, u32[]{:S(2)}, u32[]{:S(2)}) collective-permute-start(f32[128,512]{1,0:T(8,128)S(1)} %get-tuple-element.54), channel_id=1, source_target_pairs={{0,2},{1,3},{2,0},{3,1},{4,6},{5,7},{6,4},{7,5},{8,10},{9,11},{10,... | collective-permute-start | bytes 786440 | tf_op jit(solution)/shard_map/ppermute | solution.py:482
  46.4 1.6 collective-permute-start.6
  48.0 3.3 %pack_weights.1 = (f32[264,512]{1,0:T(8,128)}, f32[264,512]{1,0:T(8,128)}, f32[136,512]{1,0:T(8,128)}, f32[128,512]{1,0:T(8,128)}) custom-call(s32[1]{0:T(128)} %bitcast.place, f32[2,128,2048]{2,1,0:T(8,128)} %refs_4_.3, f32[8,512]{1,0:T(8,128)} %select_maximum_fusion.refs_0_.tile), custom_call_target="tpu_custom_call" | custom-call | tf_op jit(solution)/shard_map/pack_weights/pallas_call | solution.py:279
  52.1 3.6 %collective-permute-start.13 = (f32[136,512]{1,0:T(8,128)}, f32[136,512]{1,0:T(8,128)S(1)}, u32[]{:S(2)}, u32[]{:S(2)}) collective-permute-start(f32[136,512]{1,0:T(8,128)} %get-tuple-element.36), channel_id=1, source_target_pairs={{0,3},{1,2},{2,1},{3,0},{4,7},{5,6},{6,5},{7,4},{8,11},{9,10},{10,... | collective-permute-start | bytes 835592 | tf_op jit(solution)/shard_map/ppermute | solution.py:482
  55.7 3.5 %collective-permute-done.5 = f32[128,512]{1,0:T(8,128)S(1)} collective-permute-done((f32[128,512]{1,0:T(8,128)S(1)}, f32[128,512]{1,0:T(8,128)S(1)}, u32[]{:S(2)}, u32[]{:S(2)}) %collective-permute-start.5) | collective-permute-done | bytes 262176 | tf_op jit(solution)/shard_map/ppermute | solution.py:482
  59.2 12.4 %collective-permute-done.6 = f32[128,512]{1,0:T(8,128)} collective-permute-done((f32[128,512]{1,0:T(8,128)S(1)}, f32[128,512]{1,0:T(8,128)}, u32[]{:S(2)}, u32[]{:S(2)}) %collective-permute-start.6) | collective-permute-done | bytes 262176 | tf_op jit(solution)/shard_map/ppermute | solution.py:482
  71.7 1.1 fusion.2
  72.9 2.1 collective-permute-start.7
  75.0 3.4 %collective-permute-start.8 = (f32[32,512]{1,0:T(8,128)S(1)}, f32[32,512]{1,0:T(8,128)S(1)}, u32[]{:S(2)}, u32[]{:S(2)}) collective-permute-start(f32[32,512]{1,0:T(8,128)S(1)} %get-tuple-element.67), channel_id=1, source_target_pairs={{4,0},{8,4},{12,8},{16,12},{20,16},{24,20},{28,24},{5,1},{9,5},{13... | collective-permute-start | bytes 196616 | tf_op jit(solution)/shard_map/ppermute | solution.py:477
  78.5 1.8 collective-permute-done.8
  80.3 1.3 collective-permute-start.10
  81.6 7.9 %collective-permute-done.13.refs_3_.refs_7_ = f32[136,512]{1,0:T(8,128)S(1)} collective-permute-done((f32[136,512]{1,0:T(8,128)}, f32[136,512]{1,0:T(8,128)S(1)}, u32[]{:S(2)}, u32[]{:S(2)}) %collective-permute-start.13) | collective-permute-done | bytes 278560 | tf_op jit(solution)/shard_map/ppermute | solution.py:482
  89.5 13.4 %collective-permute-start.9 = (f32[192,128]{1,0:T(8,128)S(1)}, f32[192,128]{1,0:T(8,128)S(1)}, u32[]{:S(2)}, u32[]{:S(2)}) collective-permute-start(f32[192,128]{1,0:T(8,128)S(1)} %get-tuple-element.64), channel_id=1, source_target_pairs={{0,1},{1,2},{2,3},{4,5},{5,6},{6,7},{8,9},{9,10},{10,11},{12,13},{... | collective-permute-start | bytes 294920 | tf_op jit(solution)/shard_map/ppermute | solution.py:472
  104.5 4.5 %shard_map.69 = (bf16[8,256,256]{2,1,0:T(8,128)(2,1)}, bf16[8,256,256]{2,1,0:T(8,128)(2,1)}, bf16[8,256,256]{2,1,0:T(8,128)(2,1)}, bf16[4,384,256]{2,1,0:T(8,128)(2,1)}) custom-call(f32[8,512]{1,0:T(8,128)} %select_maximum_fusion.refs_0_.tile, f32[264,512]{1,0:T(8,128)} %copy-done.4, f32[264,512]{1,0:T(8,128)} %copy-done.5, f32[136,512]{1,0:T(8,128)} %copy-done.9), custom_call_target="tpu_custom_call" | custom-call | tf_op jit(solution)/shard_map/pallas_call | solution.py:88
  110.6 10.7 %shard_map.70 = (f32[64,640]{1,0:T(8,128)}, f32[64,640]{1,0:T(8,128)}, f32[64,640]{1,0:T(8,128)}, f32[8,128]{1,0:T(8,128)}) custom-call(s32[1]{0:T(128)} %bitcast.place, f32[192,768]{1,0:T(8,128)} %pad_maximum_fusion.1.image, bf16[8,256,256]{2,1,0:T(8,128)(2,1)} %get-tuple-element.37.refs_0_, bf16[8,256,256]{2,1,0:T(8,128)(2,1)} %get-tuple-element.38.refs_1_, ...), custom_call_target="tpu_custom_call" | custom-call | flops 12000000000 | bytes 4194304 | tf_op jit(solution)/shard_map/pallas_call | solution.py:350
  121.3 2.0 collective-permute-start.15
  123.2 3.6 %collective-permute-start.16 = (f32[64,640]{1,0:T(8,128)}, f32[64,640]{1,0:T(8,128)S(1)}, u32[]{:S(2)}, u32[]{:S(2)}) collective-permute-start(f32[64,640]{1,0:T(8,128)} %get-tuple-element.43), channel_id=1, source_target_pairs={{4,0},{8,4},{12,8},{16,12},{20,16},{24,20},{28,24},{5,1},{9,5},{13... | collective-permute-start | bytes 491528 | tf_op jit(solution)/shard_map/ppermute | solution.py:477
  126.9 1.2 collective-permute-done.15
  132.0 4.3 %collective-permute-start.17 = (f32[192,128]{1,0:T(8,128)S(1)}, f32[192,128]{1,0:T(8,128)S(1)}, u32[]{:S(2)}, u32[]{:S(2)}) collective-permute-start(f32[192,128]{1,0:T(8,128)S(1)} %get-tuple-element.62), channel_id=1, source_target_pairs={{0,1},{1,2},{2,3},{4,5},{5,6},{6,7},{8,9},{9,10},{10,11},{12,13},{... | collective-permute-start | bytes 294920 | tf_op jit(solution)/shard_map/ppermute | solution.py:472
  136.3 1.3 collective-permute-start.18
  138.4 4.6 %collective-permute-done.18 = f32[192,128]{1,0:T(8,128)S(1)} collective-permute-done((f32[192,128]{1,0:T(8,128)S(1)}, f32[192,128]{1,0:T(8,128)S(1)}, u32[]{:S(2)}, u32[]{:S(2)}) %collective-permute-start.18) | collective-permute-done | bytes 98336 | tf_op jit(solution)/shard_map/ppermute | solution.py:477
  144.1 10.8 %shard_map.71 = (f32[32,640]{1,0:T(8,128)}, f32[128,640]{1,0:T(8,128)}, f32[32,640]{1,0:T(8,128)}, f32[8,128]{1,0:T(8,128)}) custom-call(s32[1]{0:T(128)} %bitcast.place, f32[192,768]{1,0:T(8,128)} %copy-done.3, bf16[8,256,256]{2,1,0:T(8,128)(2,1)} %get-tuple-element.37.refs_0_, bf16[8,256,256]{2,1,0:T(8,128)(2,1)} %get-tuple-element.38.refs_1_, ...), custom_call_target="tpu_custom_call" | custom-call | flops 12000000000 | bytes 4194304 | tf_op jit(solution)/shard_map/pallas_call | solution.py:350
  154.9 2.5 %collective-permute-start.30 = (f32[32,640]{1,0:T(8,128)}, f32[32,640]{1,0:T(8,128)S(1)}, u32[]{:S(2)}, u32[]{:S(2)}) collective-permute-start(f32[32,640]{1,0:T(8,128)} %get-tuple-element.51.bot), channel_id=1, source_target_pairs={{0,4},{4,8},{8,12},{12,16},{16,20},{20,24},{24,28},{1,5},{5,9},{9,... | collective-permute-start | bytes 245768 | tf_op jit(solution)/shard_map/ppermute | solution.py:472
  157.3 3.1 %collective-permute-start.31 = (f32[32,640]{1,0:T(8,128)}, f32[32,640]{1,0:T(8,128)S(1)}, u32[]{:S(2)}, u32[]{:S(2)}) collective-permute-start(f32[32,640]{1,0:T(8,128)} %get-tuple-element.49.top), channel_id=1, source_target_pairs={{4,0},{8,4},{12,8},{16,12},{20,16},{24,20},{28,24},{5,1},{9,5},{13... | collective-permute-start | bytes 245768 | tf_op jit(solution)/shard_map/ppermute | solution.py:477
  161.3 1.5 collective-permute-done.31.dn
  163.4 2.0 wrap.1.refs_8_
  165.5 3.0 %collective-permute-start.20 = (f32[4,8,128]{2,1,0:T(8,128)S(1)}, f32[4,8,128]{2,1,0:T(8,128)S(1)}, u32[]{:S(2)}, u32[]{:S(2)}) collective-permute-start(f32[4,8,128]{2,1,0:T(8,128)S(1)} %fusion.1), channel_id=1, source_target_pairs={{0,2},{1,3},{2,0},{3,1},{4,6},{5,7},{6,4},{7,5},{8,10},{9,11},{10,... | collective-permute-start | bytes 49160 | tf_op jit(solution)/shard_map/ppermute | solution.py:482
  169.1 2.8 %collective-permute-start.28 = (f32[128,512]{1,0:T(8,128)S(1)}, f32[128,512]{1,0:T(8,128)S(1)}, u32[]{:S(2)}, u32[]{:S(2)}) collective-permute-start(f32[128,512]{1,0:T(8,128)S(1)} %copy-done.2), channel_id=1, source_target_pairs={{0,2},{1,3},{2,0},{3,1},{4,6},{5,7},{6,4},{7,5},{8,10},{9,11},{10,... | collective-permute-start | bytes 786440 | tf_op jit(solution)/shard_map/ppermute | solution.py:482
  171.9 22.7 %collective-permute-done.20 = f32[4,8,128]{2,1,0:T(8,128)S(1)} collective-permute-done((f32[4,8,128]{2,1,0:T(8,128)S(1)}, f32[4,8,128]{2,1,0:T(8,128)S(1)}, u32[]{:S(2)}, u32[]{:S(2)}) %collective-permute-start.20) | collective-permute-done | bytes 16416 | tf_op jit(solution)/shard_map/ppermute | solution.py:482
  195.8 3.7 %collective-permute-done.22 = f32[4,8,128]{2,1,0:T(8,128)S(1)} collective-permute-done((f32[4,8,128]{2,1,0:T(8,128)S(1)}, f32[4,8,128]{2,1,0:T(8,128)S(1)}, u32[]{:S(2)}, u32[]{:S(2)}) %collective-permute-start.22) | collective-permute-done | bytes 16416 | tf_op jit(solution)/shard_map/ppermute | solution.py:482
  199.5 2.0 collective-permute-start.34
  201.8 3.6 %collective-permute-done.23 = f32[4,8,128]{2,1,0:T(8,128)S(1)} collective-permute-done((f32[4,8,128]{2,1,0:T(8,128)S(1)}, f32[4,8,128]{2,1,0:T(8,128)S(1)}, u32[]{:S(2)}, u32[]{:S(2)}) %collective-permute-start.23) | collective-permute-done | bytes 16416 | tf_op jit(solution)/shard_map/ppermute | solution.py:482
  205.9 1.5 collective-permute-start.29
  208.0 16.3 %collective-permute-done.26.refs_3_ = f32[128,512]{1,0:T(8,128)S(1)} collective-permute-done((f32[128,512]{1,0:T(8,128)S(1)}, f32[128,512]{1,0:T(8,128)S(1)}, u32[]{:S(2)}, u32[]{:S(2)}) %collective-permute-start.26) | collective-permute-done | bytes 262176 | tf_op jit(solution)/shard_map/ppermute | solution.py:482
  224.3 5.6 %collective-permute-done.27.refs_5_ = f32[128,512]{1,0:T(8,128)S(1)} collective-permute-done((f32[128,512]{1,0:T(8,128)S(1)}, f32[128,512]{1,0:T(8,128)S(1)}, u32[]{:S(2)}, u32[]{:S(2)}) %collective-permute-start.27) | collective-permute-done | bytes 262176 | tf_op jit(solution)/shard_map/ppermute | solution.py:482
  229.9 5.5 %collective-permute-done.29.refs_7_ = f32[128,512]{1,0:T(8,128)S(1)} collective-permute-done((f32[128,512]{1,0:T(8,128)S(1)}, f32[128,512]{1,0:T(8,128)S(1)}, u32[]{:S(2)}, u32[]{:S(2)}) %collective-permute-start.29) | collective-permute-done | bytes 262176 | tf_op jit(solution)/shard_map/ppermute | solution.py:482
  236.9 4.0 %final_images.1 = (f32[128,2048]{1,0:T(8,128)}, f32[128,2048]{1,0:T(8,128)}) custom-call(s32[1]{0:T(128)} %bitcast.place, f32[128,2048]{1,0:T(8,128)} %est.3, f32[4,8,128]{2,1,0:T(8,128)} %add.94.sums, f32[128,512]{1,0:T(8,128)} %copy-done, f32[128,512]{1,0:T(8,128)} %copy-done.11, f32[128,512]{1,0:T(8,128)} %copy-done.10, f32[128,512]{1,0:T(8,128)} %copy-done.13, ...), custom_call_target="tpu_custom_call" | custom-call | tf_op jit(solution)/shard_map/final_images/pallas_call | solution.py:460
  (109 shorter events, 20.1 us)
Async XLA Ops:
  1.7 8.9 %collective-permute-start = (f32[32,2048]{1,0:T(8,128)S(1)}, f32[32,2048]{1,0:T(8,128)S(1)}, u32[]{:S(2)}, u32[]{:S(2)}) collective-permute-start(f32[32,2048]{1,0:T(8,128)S(1)} %get-tuple-element.59), channel_id=1, source_target_pairs={{0,4},{4,8},{8,12},{12,16},{16,20},{20,24},{24,28},{1,5},{5,9},{9,... | collective-permute-start | bytes 786440 | tf_op jit(solution)/shard_map/ppermute | solution.py:472
  3.6 7.6 %collective-permute-start.1 = (f32[32,2048]{1,0:T(8,128)S(1)}, f32[32,2048]{1,0:T(8,128)S(1)}, u32[]{:S(2)}, u32[]{:S(2)}) collective-permute-start(f32[32,2048]{1,0:T(8,128)S(1)} %get-tuple-element.58), channel_id=1, source_target_pairs={{4,0},{8,4},{12,8},{16,12},{20,16},{24,20},{28,24},{5,1},{9,5},{13... | collective-permute-start | bytes 786440 | tf_op jit(solution)/shard_map/ppermute | solution.py:477
  23.9 8.1 %collective-permute-start.2 = (f32[32,2048]{1,0:T(8,128)}, f32[32,2048]{1,0:T(8,128)S(1)}, u32[]{:S(2)}, u32[]{:S(2)}) collective-permute-start(f32[32,2048]{1,0:T(8,128)} %get-tuple-element.32), channel_id=1, source_target_pairs={{0,4},{4,8},{8,12},{12,16},{16,20},{20,24},{24,28},{1,5},{5,9},{9,... | collective-permute-start | bytes 786440 | tf_op jit(solution)/shard_map/ppermute | solution.py:472
  28.4 6.3 %collective-permute-start.3 = (f32[32,2048]{1,0:T(8,128)}, f32[32,2048]{1,0:T(8,128)S(1)}, u32[]{:S(2)}, u32[]{:S(2)}) collective-permute-start(f32[32,2048]{1,0:T(8,128)} %get-tuple-element.33), channel_id=1, source_target_pairs={{4,0},{8,4},{12,8},{16,12},{20,16},{24,20},{28,24},{5,1},{9,5},{13... | collective-permute-start | bytes 786440 | tf_op jit(solution)/shard_map/ppermute | solution.py:477
  36.0 7.7 %collective-permute-start.4 = (f32[128,512]{1,0:T(8,128)S(1)}, f32[128,512]{1,0:T(8,128)S(1)}, u32[]{:S(2)}, u32[]{:S(2)}) collective-permute-start(f32[128,512]{1,0:T(8,128)S(1)} %constant_dynamic-slice_fusion.1), channel_id=1, source_target_pairs={{0,1},{1,0},{2,3},{3,2},{4,5},{5,4},{6,7},{7,6},{8,9},{9,8},{10,11... | collective-permute-start | bytes 786440 | tf_op jit(solution)/shard_map/ppermute | solution.py:482
  43.7 15.5 %collective-permute-start.5 = (f32[128,512]{1,0:T(8,128)S(1)}, f32[128,512]{1,0:T(8,128)S(1)}, u32[]{:S(2)}, u32[]{:S(2)}) collective-permute-start(f32[128,512]{1,0:T(8,128)S(1)} %get-tuple-element.54), channel_id=1, source_target_pairs={{0,2},{1,3},{2,0},{3,1},{4,6},{5,7},{6,4},{7,5},{8,10},{9,11},{10,... | collective-permute-start | bytes 786440 | tf_op jit(solution)/shard_map/ppermute | solution.py:482
  46.4 25.3 %collective-permute-start.6 = (f32[128,512]{1,0:T(8,128)S(1)}, f32[128,512]{1,0:T(8,128)}, u32[]{:S(2)}, u32[]{:S(2)}) collective-permute-start(f32[128,512]{1,0:T(8,128)S(1)} %get-tuple-element.55), channel_id=1, source_target_pairs={{0,1},{1,0},{2,3},{3,2},{4,5},{5,4},{6,7},{7,6},{8,9},{9,8},{10,11... | collective-permute-start | bytes 786440 | tf_op jit(solution)/shard_map/ppermute | solution.py:482
  51.3 51.6 %collective-permute-start.11 = (f32[264,512]{1,0:T(8,128)}, f32[264,512]{1,0:T(8,128)S(1)}, u32[]{:S(2)}, u32[]{:S(2)}) collective-permute-start(f32[264,512]{1,0:T(8,128)} %get-tuple-element.34), channel_id=1, source_target_pairs={{0,1},{1,0},{2,3},{3,2},{4,5},{5,4},{6,7},{7,6},{8,9},{9,8},{10,11... | collective-permute-start | bytes 1622024 | tf_op jit(solution)/shard_map/ppermute | solution.py:482
  51.8 51.2 %collective-permute-start.12 = (f32[264,512]{1,0:T(8,128)}, f32[264,512]{1,0:T(8,128)S(1)}, u32[]{:S(2)}, u32[]{:S(2)}) collective-permute-start(f32[264,512]{1,0:T(8,128)} %get-tuple-element.35), channel_id=1, source_target_pairs={{0,2},{1,3},{2,0},{3,1},{4,6},{5,7},{6,4},{7,5},{8,10},{9,11},{10,... | collective-permute-start | bytes 1622024 | tf_op jit(solution)/shard_map/ppermute | solution.py:482
  52.1 37.4 %collective-permute-start.13 = (f32[136,512]{1,0:T(8,128)}, f32[136,512]{1,0:T(8,128)S(1)}, u32[]{:S(2)}, u32[]{:S(2)}) collective-permute-start(f32[136,512]{1,0:T(8,128)} %get-tuple-element.36), channel_id=1, source_target_pairs={{0,3},{1,2},{2,1},{3,0},{4,7},{5,6},{6,5},{7,4},{8,11},{9,10},{10,... | collective-permute-start | bytes 835592 | tf_op jit(solution)/shard_map/ppermute | solution.py:482
  72.8 95.7 %copy-start = (f32[128,512]{1,0:T(8,128)}, f32[128,512]{1,0:T(8,128)S(1)}, u32[]{:S(2)}) copy-start(f32[128,512]{1,0:T(8,128)S(1)} %neg.3.refs_0_) | copy-start | bytes 786436
  72.9 5.6 %collective-permute-start.7 = (f32[32,512]{1,0:T(8,128)S(1)}, f32[32,512]{1,0:T(8,128)S(1)}, u32[]{:S(2)}, u32[]{:S(2)}) collective-permute-start(f32[32,512]{1,0:T(8,128)S(1)} %get-tuple-element.66), channel_id=1, source_target_pairs={{0,4},{4,8},{8,12},{12,16},{16,20},{20,24},{24,28},{1,5},{5,9},{9,... | collective-permute-start | bytes 196616 | tf_op jit(solution)/shard_map/ppermute | solution.py:472
  75.0 5.3 %collective-permute-start.8 = (f32[32,512]{1,0:T(8,128)S(1)}, f32[32,512]{1,0:T(8,128)S(1)}, u32[]{:S(2)}, u32[]{:S(2)}) collective-permute-start(f32[32,512]{1,0:T(8,128)S(1)} %get-tuple-element.67), channel_id=1, source_target_pairs={{4,0},{8,4},{12,8},{16,12},{20,16},{24,20},{28,24},{5,1},{9,5},{13... | collective-permute-start | bytes 196616 | tf_op jit(solution)/shard_map/ppermute | solution.py:477
  78.4 31.4 %collective-permute-start.14 = (f32[128,512]{1,0:T(8,128)}, f32[128,512]{1,0:T(8,128)S(1)}, u32[]{:S(2)}, u32[]{:S(2)}) collective-permute-start(f32[128,512]{1,0:T(8,128)} %get-tuple-element.41), channel_id=1, source_target_pairs={{0,3},{1,2},{2,1},{3,0},{4,7},{5,6},{6,5},{7,4},{8,11},{9,10},{10,... | collective-permute-start | bytes 786440 | tf_op jit(solution)/shard_map/ppermute | solution.py:482
  80.3 28.7 %collective-permute-start.10 = (f32[192,128]{1,0:T(8,128)S(1)}, f32[192,128]{1,0:T(8,128)S(1)}, u32[]{:S(2)}, u32[]{:S(2)}) collective-permute-start(f32[192,128]{1,0:T(8,128)S(1)} %get-tuple-element.65), channel_id=1, source_target_pairs={{1,0},{2,1},{3,2},{5,4},{6,5},{7,6},{9,8},{10,9},{11,10},{13,12},{... | collective-permute-start | bytes 294920 | tf_op jit(solution)/shard_map/ppermute | solution.py:477
  89.5 13.5 %copy-start.9 = (f32[136,512]{1,0:T(8,128)}, f32[136,512]{1,0:T(8,128)S(1)}, u32[]{:S(2)}) copy-start(f32[136,512]{1,0:T(8,128)S(1)} %collective-permute-done.13.refs_3_.refs_7_) | copy-start | bytes 835588
  89.5 19.5 %collective-permute-start.9 = (f32[192,128]{1,0:T(8,128)S(1)}, f32[192,128]{1,0:T(8,128)S(1)}, u32[]{:S(2)}, u32[]{:S(2)}) collective-permute-start(f32[192,128]{1,0:T(8,128)S(1)} %get-tuple-element.64), channel_id=1, source_target_pairs={{0,1},{1,2},{2,3},{4,5},{5,6},{6,7},{8,9},{9,10},{10,11},{12,13},{... | collective-permute-start | bytes 294920 | tf_op jit(solution)/shard_map/ppermute | solution.py:472
  121.3 6.8 %collective-permute-start.15 = (f32[64,640]{1,0:T(8,128)}, f32[64,640]{1,0:T(8,128)S(1)}, u32[]{:S(2)}, u32[]{:S(2)}) collective-permute-start(f32[64,640]{1,0:T(8,128)} %get-tuple-element.44), channel_id=1, source_target_pairs={{0,4},{4,8},{8,12},{12,16},{16,20},{20,24},{24,28},{1,5},{5,9},{9,... | collective-permute-start | bytes 491528 | tf_op jit(solution)/shard_map/ppermute | solution.py:472
  123.2 6.7 %collective-permute-start.16 = (f32[64,640]{1,0:T(8,128)}, f32[64,640]{1,0:T(8,128)S(1)}, u32[]{:S(2)}, u32[]{:S(2)}) collective-permute-start(f32[64,640]{1,0:T(8,128)} %get-tuple-element.43), channel_id=1, source_target_pairs={{4,0},{8,4},{12,8},{16,12},{20,16},{24,20},{28,24},{5,1},{9,5},{13... | collective-permute-start | bytes 491528 | tf_op jit(solution)/shard_map/ppermute | solution.py:477
  132.0 6.5 %collective-permute-start.17 = (f32[192,128]{1,0:T(8,128)S(1)}, f32[192,128]{1,0:T(8,128)S(1)}, u32[]{:S(2)}, u32[]{:S(2)}) collective-permute-start(f32[192,128]{1,0:T(8,128)S(1)} %get-tuple-element.62), channel_id=1, source_target_pairs={{0,1},{1,2},{2,3},{4,5},{5,6},{6,7},{8,9},{9,10},{10,11},{12,13},{... | collective-permute-start | bytes 294920 | tf_op jit(solution)/shard_map/ppermute | solution.py:472
  136.3 6.8 %collective-permute-start.18 = (f32[192,128]{1,0:T(8,128)S(1)}, f32[192,128]{1,0:T(8,128)S(1)}, u32[]{:S(2)}, u32[]{:S(2)}) collective-permute-start(f32[192,128]{1,0:T(8,128)S(1)} %get-tuple-element.63), channel_id=1, source_target_pairs={{1,0},{2,1},{3,2},{5,4},{6,5},{7,6},{9,8},{10,9},{11,10},{13,12},{... | collective-permute-start | bytes 294920 | tf_op jit(solution)/shard_map/ppermute | solution.py:477
  144.1 16.4 %copy-start.1 = (f32[128,512]{1,0:T(8,128)}, f32[128,512]{1,0:T(8,128)S(1)}, u32[]{:S(2)}) copy-start(f32[128,512]{1,0:T(8,128)S(1)} %slice.62.before.refs_4_) | copy-start | bytes 786436
  144.1 16.5 %copy-start.18 = (f32[8,128]{1,0:T(8,128)S(1)}, f32[8,128]{1,0:T(8,128)}, u32[]{:S(2)}) copy-start(f32[8,128]{1,0:T(8,128)} %get-tuple-element.42) | copy-start | bytes 12292
  154.8 10.6 %copy-start.19 = (f32[8,128]{1,0:T(8,128)S(1)}, f32[8,128]{1,0:T(8,128)}, u32[]{:S(2)}) copy-start(f32[8,128]{1,0:T(8,128)} %get-tuple-element.48) | copy-start | bytes 12292
  154.9 6.4 %collective-permute-start.30 = (f32[32,640]{1,0:T(8,128)}, f32[32,640]{1,0:T(8,128)S(1)}, u32[]{:S(2)}, u32[]{:S(2)}) collective-permute-start(f32[32,640]{1,0:T(8,128)} %get-tuple-element.51.bot), channel_id=1, source_target_pairs={{0,4},{4,8},{8,12},{12,16},{16,20},{20,24},{24,28},{1,5},{5,9},{9,... | collective-permute-start | bytes 245768 | tf_op jit(solution)/shard_map/ppermute | solution.py:472
  157.3 5.5 %collective-permute-start.31 = (f32[32,640]{1,0:T(8,128)}, f32[32,640]{1,0:T(8,128)S(1)}, u32[]{:S(2)}, u32[]{:S(2)}) collective-permute-start(f32[32,640]{1,0:T(8,128)} %get-tuple-element.49.top), channel_id=1, source_target_pairs={{4,0},{8,4},{12,8},{16,12},{20,16},{24,20},{28,24},{5,1},{9,5},{13... | collective-permute-start | bytes 245768 | tf_op jit(solution)/shard_map/ppermute | solution.py:477
  160.5 8.6 %copy-start.2 = (f32[128,512]{1,0:T(8,128)S(1)}, f32[128,512]{1,0:T(8,128)}, u32[]{:S(2)}) copy-start(f32[128,512]{1,0:T(8,128)} %copy-done.1) | copy-start | bytes 786436
  161.3 4.2 %collective-permute-start.19 = (f32[4,8,128]{2,1,0:T(8,128)S(1)}, f32[4,8,128]{2,1,0:T(8,128)S(1)}, u32[]{:S(2)}, u32[]{:S(2)}) collective-permute-start(f32[4,8,128]{2,1,0:T(8,128)S(1)} %pad_maximum_fusion.5), channel_id=1, source_target_pairs={{0,1},{1,0},{2,3},{3,2},{4,5},{5,4},{6,7},{7,6},{8,9},{9,8},{10,11... | collective-permute-start | bytes 49160 | tf_op jit(solution)/shard_map/ppermute | solution.py:482
  165.5 34.1 %collective-permute-start.33 = (f32[144,512]{1,0:T(8,128)}, f32[144,512]{1,0:T(8,128)S(1)}, u32[]{:S(2)}, u32[]{:S(2)}) collective-permute-start(f32[144,512]{1,0:T(8,128)} %wrap.1.refs_8_), channel_id=1, source_target_pairs={{0,2},{1,3},{2,0},{3,1},{4,6},{5,7},{6,4},{7,5},{8,10},{9,11},{10,... | collective-permute-start | bytes 884744 | tf_op jit(solution)/shard_map/ppermute | solution.py:482
  165.5 29.1 %collective-permute-start.20 = (f32[4,8,128]{2,1,0:T(8,128)S(1)}, f32[4,8,128]{2,1,0:T(8,128)S(1)}, u32[]{:S(2)}, u32[]{:S(2)}) collective-permute-start(f32[4,8,128]{2,1,0:T(8,128)S(1)} %fusion.1), channel_id=1, source_target_pairs={{0,2},{1,3},{2,0},{3,1},{4,6},{5,7},{6,4},{7,5},{8,10},{9,11},{10,... | collective-permute-start | bytes 49160 | tf_op jit(solution)/shard_map/ppermute | solution.py:482
  168.5 33.1 %collective-permute-start.25 = (f32[128,512]{1,0:T(8,128)S(1)}, f32[128,512]{1,0:T(8,128)S(1)}, u32[]{:S(2)}, u32[]{:S(2)}) collective-permute-start(f32[128,512]{1,0:T(8,128)S(1)} %neg.3.refs_0_), channel_id=1, source_target_pairs={{0,2},{1,3},{2,0},{3,1},{4,6},{5,7},{6,4},{7,5},{8,10},{9,11},{10,... | collective-permute-start | bytes 786440 | tf_op jit(solution)/shard_map/ppermute | solution.py:482
  168.5 33.1 %collective-permute-start.24 = (f32[128,512]{1,0:T(8,128)S(1)}, f32[128,512]{1,0:T(8,128)S(1)}, u32[]{:S(2)}, u32[]{:S(2)}) collective-permute-start(f32[128,512]{1,0:T(8,128)S(1)} %neg.3.refs_0_), channel_id=1, source_target_pairs={{0,1},{1,0},{2,3},{3,2},{4,5},{5,4},{6,7},{7,6},{8,9},{9,8},{10,11... | collective-permute-start | bytes 786440 | tf_op jit(solution)/shard_map/ppermute | solution.py:482
  169.1 36.8 %collective-permute-start.28 = (f32[128,512]{1,0:T(8,128)S(1)}, f32[128,512]{1,0:T(8,128)S(1)}, u32[]{:S(2)}, u32[]{:S(2)}) collective-permute-start(f32[128,512]{1,0:T(8,128)S(1)} %copy-done.2), channel_id=1, source_target_pairs={{0,2},{1,3},{2,0},{3,1},{4,6},{5,7},{6,4},{7,5},{8,10},{9,11},{10,... | collective-permute-start | bytes 786440 | tf_op jit(solution)/shard_map/ppermute | solution.py:482
  194.6 1.2 collective-permute-start.21
  195.8 3.7 %collective-permute-start.22 = (f32[4,8,128]{2,1,0:T(8,128)S(1)}, f32[4,8,128]{2,1,0:T(8,128)S(1)}, u32[]{:S(2)}, u32[]{:S(2)}) collective-permute-start(f32[4,8,128]{2,1,0:T(8,128)S(1)} %add.92), channel_id=1, source_target_pairs={{0,8},{4,12},{8,0},{12,4},{16,24},{20,28},{24,16},{28,20},{1,9},{5... | collective-permute-start | bytes 49160 | tf_op jit(solution)/shard_map/ppermute | solution.py:482
  199.5 30.4 %collective-permute-start.32 = (f32[144,512]{1,0:T(8,128)}, f32[144,512]{1,0:T(8,128)S(1)}, u32[]{:S(2)}, u32[]{:S(2)}) collective-permute-start(f32[144,512]{1,0:T(8,128)} %wrap.1.refs_8_), channel_id=1, source_target_pairs={{0,1},{1,0},{2,3},{3,2},{4,5},{5,4},{6,7},{7,6},{8,9},{9,8},{10,11... | collective-permute-start | bytes 884744 | tf_op jit(solution)/shard_map/ppermute | solution.py:482
  199.5 35.9 %copy-start.6 = (f32[144,512]{1,0:T(8,128)}, f32[144,512]{1,0:T(8,128)S(1)}, u32[]{:S(2)}) copy-start(f32[144,512]{1,0:T(8,128)S(1)} %collective-permute-done.33.refs_10_) | copy-start | bytes 884740
  199.5 35.9 %collective-permute-start.34 = (f32[144,512]{1,0:T(8,128)S(1)}, f32[144,512]{1,0:T(8,128)S(1)}, u32[]{:S(2)}, u32[]{:S(2)}) collective-permute-start(f32[144,512]{1,0:T(8,128)S(1)} %collective-permute-done.33.refs_10_), channel_id=1, source_target_pairs={{0,1},{1,0},{2,3},{3,2},{4,5},{5,4},{6,7},{7,6},{8,9},{9,8},{10,11... | collective-permute-start | bytes 884744 | tf_op jit(solution)/shard_map/ppermute | solution.py:482
  201.6 33.9 %copy-start.10 = (f32[128,512]{1,0:T(8,128)}, f32[128,512]{1,0:T(8,128)S(1)}, u32[]{:S(2)}) copy-start(f32[128,512]{1,0:T(8,128)S(1)} %collective-permute-done.25.refs_2_) | copy-start | bytes 786436
  201.6 3.8 %collective-permute-start.23 = (f32[4,8,128]{2,1,0:T(8,128)S(1)}, f32[4,8,128]{2,1,0:T(8,128)S(1)}, u32[]{:S(2)}, u32[]{:S(2)}) collective-permute-start(f32[4,8,128]{2,1,0:T(8,128)S(1)} %add.93), channel_id=1, source_target_pairs={{0,16},{4,20},{8,24},{12,28},{16,0},{20,4},{24,8},{28,12},{1,17},{... | collective-permute-start | bytes 49160 | tf_op jit(solution)/shard_map/ppermute | solution.py:482
  201.7 33.8 %copy-start.11 = (f32[128,512]{1,0:T(8,128)}, f32[128,512]{1,0:T(8,128)S(1)}, u32[]{:S(2)}) copy-start(f32[128,512]{1,0:T(8,128)S(1)} %collective-permute-done.24.refs_1_) | copy-start | bytes 786436
  201.7 22.6 %collective-permute-start.26 = (f32[128,512]{1,0:T(8,128)S(1)}, f32[128,512]{1,0:T(8,128)S(1)}, u32[]{:S(2)}, u32[]{:S(2)}) collective-permute-start(f32[128,512]{1,0:T(8,128)S(1)} %collective-permute-done.25.refs_2_), channel_id=1, source_target_pairs={{0,1},{1,0},{2,3},{3,2},{4,5},{5,4},{6,7},{7,6},{8,9},{9,8},{10,11... | collective-permute-start | bytes 786440 | tf_op jit(solution)/shard_map/ppermute | solution.py:482
  205.4 24.5 %collective-permute-start.27 = (f32[128,512]{1,0:T(8,128)S(1)}, f32[128,512]{1,0:T(8,128)S(1)}, u32[]{:S(2)}, u32[]{:S(2)}) collective-permute-start(f32[128,512]{1,0:T(8,128)S(1)} %copy-done.2), channel_id=1, source_target_pairs={{0,1},{1,0},{2,3},{3,2},{4,5},{5,4},{6,7},{7,6},{8,9},{9,8},{10,11... | collective-permute-start | bytes 786440 | tf_op jit(solution)/shard_map/ppermute | solution.py:482
  205.9 29.5 %copy-start.12 = (f32[128,512]{1,0:T(8,128)}, f32[128,512]{1,0:T(8,128)S(1)}, u32[]{:S(2)}) copy-start(f32[128,512]{1,0:T(8,128)S(1)} %collective-permute-done.28.refs_6_) | copy-start | bytes 786436
  205.9 29.5 %collective-permute-start.29 = (f32[128,512]{1,0:T(8,128)S(1)}, f32[128,512]{1,0:T(8,128)S(1)}, u32[]{:S(2)}, u32[]{:S(2)}) collective-permute-start(f32[128,512]{1,0:T(8,128)S(1)} %collective-permute-done.28.refs_6_), channel_id=1, source_target_pairs={{0,1},{1,0},{2,3},{3,2},{4,5},{5,4},{6,7},{7,6},{8,9},{9,8},{10,11... | collective-permute-start | bytes 786440 | tf_op jit(solution)/shard_map/ppermute | solution.py:482
  224.3 11.2 %copy-start.13 = (f32[128,512]{1,0:T(8,128)}, f32[128,512]{1,0:T(8,128)S(1)}, u32[]{:S(2)}) copy-start(f32[128,512]{1,0:T(8,128)S(1)} %collective-permute-done.26.refs_3_) | copy-start | bytes 786436
  229.9 5.6 %copy-start.14 = (f32[128,512]{1,0:T(8,128)}, f32[128,512]{1,0:T(8,128)S(1)}, u32[]{:S(2)}) copy-start(f32[128,512]{1,0:T(8,128)S(1)} %collective-permute-done.27.refs_5_) | copy-start | bytes 786436
  229.9 5.6 %copy-start.7 = (f32[144,512]{1,0:T(8,128)}, f32[144,512]{1,0:T(8,128)S(1)}, u32[]{:S(2)}) copy-start(f32[144,512]{1,0:T(8,128)S(1)} %collective-permute-done.32.refs_9_) | copy-start | bytes 884740
  (10 other events, 8.1 us)

commit v4 on v3

v4 whole, which is shorter than its diff:
```python
import functools

import jax
import jax.numpy as jnp
from jax import lax
from jax.experimental import pallas as pl
from jax.experimental.pallas import tpu as pltpu
from jax.sharding import PartitionSpec as P


damping = 0.05
f32 = jnp.float32
bf16 = jnp.bfloat16
LANE = 128
VMEM = pl.BlockSpec(memory_space=pltpu.VMEM)
ANY = pl.BlockSpec(memory_space=pl.ANY)
SMEM = pl.BlockSpec(memory_space=pltpu.SMEM)


def split(x):
    hi = x.astype(bf16)
    lo = (x - hi.astype(f32)).astype(bf16)
    return hi, lo


def dot(a, b):
    return jnp.dot(a, b, preferred_element_type=f32)


def choose(flag, a, b):
    return jnp.where(jnp.full(a.shape, flag, jnp.int32) == 1, a, b)


def pack_edge(edge, halo, w):
    rows = edge.shape[0]
    per = LANE // (2 * halo)
    short = rows * 2 * halo // w
    edge = pltpu.roll(edge, halo, 1)
    lane = lax.broadcasted_iota(jnp.int32, (short, LANE), 1)
    out = []
    for t in range(w // LANE):
        tile = None
        for p in range(per):
            k = t * per + p
            part = edge[k * short : (k + 1) * short]
            part = pltpu.roll(part, p * 2 * halo, 1) if p else part
            tile = part if tile is None else jnp.where(lane >= p * 2 * halo, part, tile)
        out.append(tile)
    return jnp.concatenate(out, axis=1)


def unpack_edge(packed, halo):
    _, w = packed.shape
    per = LANE // (2 * halo)
    parts = []
    for k in range(w // (2 * halo)):
        t, p = divmod(k, per)
        part = packed[:, t * LANE : (t + 1) * LANE]
        back = (LANE - halo - p * 2 * halo) % LANE
        parts.append(pltpu.roll(part, back, 1) if back else part)
    return jnp.concatenate(parts, axis=0)


def tiles(width, step=256):
    return [(s, min(step, width - s)) for s in range(0, width, step)]


def toeplitz(base, count):
    wide = base.shape[1]
    return pltpu.roll(jnp.broadcast_to(base, (count, wide)), 0, 1, stride=1, stride_axis=0)


def build_group(taps, g, frames, rows, halo, t_ref, b_ref, bp_ref, ta_ref):
    ext = rows + 2 * halo
    unit = taps / jnp.sum(taps, axis=1, keepdims=True)
    for s in range(frames):
        f = g * frames + s
        col = unit[s : s + 1]
        row = unit[frames + s : frames + s + 1]
        by_rows = toeplitz(row, rows)
        hi, lo = split(by_rows)
        t_ref[f, :rows, :] = hi
        t_ref[f, rows:, :] = lo
        hi, lo = split(by_rows.T[:ext])
        ta_ref[g, :ext, s * rows : (s + 1) * rows] = hi
        ta_ref[g, ext:, s * rows : (s + 1) * rows] = lo
        hi, lo = split(toeplitz(col, LANE).T)
        b_ref[f, :, :LANE] = hi
        b_ref[f, :, LANE:] = lo
        hi, lo = split(toeplitz(pltpu.roll(col, LANE, 1), 2 * LANE)[:, :LANE])
        bp_ref[f, :, :LANE] = hi
        bp_ref[f, :, LANE:] = lo


def matrix_shapes(groups, frames, rows, halo):
    ext = rows + 2 * halo
    return [
        jax.ShapeDtypeStruct(s, bf16)
        for s in (
            (groups * frames, 2 * rows, 2 * LANE),
            (groups * frames, 2 * LANE, 2 * LANE),
            (groups * frames, 2 * LANE, 2 * LANE),
            (groups, 2 * ext, frames * rows),
        )
    ]


def tile_height(frames):
    return -(-2 * frames // 8) * 8


def setup_kernel(frames, rows, halo, starts, *refs):
    tiles_in = refs[: len(starts)]
    mats, taps, sem = refs[len(starts) : -2], refs[-2], refs[-1]
    height = tile_height(frames)

    def copy(g):
        source = tiles_in[g].at[pl.ds(starts[g], height), pl.ds(0, 2 * LANE)]
        return pltpu.make_async_copy(source, taps.at[g], sem.at[g])

    for g in range(len(starts)):
        copy(g).start()
    for g in range(len(starts)):
        copy(g).wait()
        build_group(taps[g], g, frames, rows, halo, *mats)


def setup_matrices(tiles_in, starts, frames, rows, halo):
    groups = len(tiles_in)
    return pl.pallas_call(
        functools.partial(setup_kernel, frames, rows, halo, starts),
        out_shape=matrix_shapes(groups, frames, rows, halo),
        in_specs=[ANY] * groups,
        out_specs=[VMEM] * 4,
        scratch_shapes=[
            pltpu.VMEM((groups, tile_height(frames), 2 * LANE), f32),
            pltpu.SemaphoreType.DMA((groups,)),
        ],
        name="setup_all",
    )(*tiles_in)


def load_image(y_hi, y_lo, image, halo):
    ext, full = image.shape
    shift = LANE - halo
    y = pltpu.roll(image, full - shift, 1)[:, : full - LANE]
    hi, lo = split(y)
    y_hi[:ext, :] = hi
    y_lo[:ext, :] = lo


def group_terms(frames, rows, w, y_hi, y_lo, t, b, bp, ta, weight, data, us, qs, vs_hi, vs_lo, acc, stat):
    total = None
    for f in range(frames):
        for c, size in tiles(w + LANE):
            r1 = dot(t(f)[...], y_hi[:, c : c + size])
            r2 = dot(t(f)[:rows, :], y_lo[:, c : c + size])
            hi, lo = split(r1[:rows] + r1[rows:] + r2)
            us[:rows, c : c + size] = hi
            us[rows:, c : c + size] = lo
        for k in range(w // LANE):
            c = k * LANE
            r = dot(us[:, c : c + 2 * LANE], b(f)[...])
            a = r[:rows, :LANE] + r[:rows, LANE:] + r[rows:, :LANE]
            if data is not None:
                a = a - data(f)[:, c : c + LANE]
            q = weight(f)[:, c : c + LANE] * a
            if stat is not None:
                part = jnp.sum((a * q).reshape(rows // 8, 8, LANE), axis=0)
                total = part if total is None else total + part
            hi, lo = split(q)
            qs[:rows, c + LANE : c + 2 * LANE] = hi
            qs[rows:, c + LANE : c + 2 * LANE] = lo
        for k in range(w // LANE + 1):
            c = k * LANE
            r = dot(qs[:, c : c + 2 * LANE], bp(f)[...])
            hi, lo = split(r[:rows, :LANE] + r[:rows, LANE:] + r[rows:, :LANE])
            vs_hi[f * rows : (f + 1) * rows, c : c + LANE] = hi
            vs_lo[f * rows : (f + 1) * rows, c : c + LANE] = lo
    ext = acc.shape[0]
    for c, size in tiles(w + LANE):
        r1 = dot(ta[...], vs_hi[:, c : c + size])
        r2 = dot(ta[:ext, :], vs_lo[:, c : c + size])
        acc[:, c : c + size] += r1[:ext] + r1[ext:] + r2
    if stat is not None:
        stat[...] += total


def work_scratch(frames, rows, halo, w):
    ext = rows + 2 * halo
    return [
        pltpu.VMEM((2 * LANE, w + LANE), bf16),
        pltpu.VMEM((2 * LANE, w + LANE), bf16),
        pltpu.VMEM((2 * rows, w + LANE), bf16),
        pltpu.VMEM((2 * rows, w + 2 * LANE), bf16),
        pltpu.VMEM((frames * rows, w + LANE), bf16),
        pltpu.VMEM((frames * rows, w + LANE), bf16),
        pltpu.VMEM((ext, w + LANE), f32),
    ]


def clear_edges(y_hi, y_lo, qs, ext, rows, w):
    zero = jnp.zeros((y_hi.shape[0] - ext, y_hi.shape[1]), bf16)
    y_hi[ext:, :] = zero
    y_lo[ext:, :] = zero
    qs[:, :LANE] = jnp.zeros((2 * rows, LANE), bf16)
    qs[:, w + LANE :] = jnp.zeros((2 * rows, LANE), bf16)


def unshift(acc, halo):
    return pltpu.roll(acc, acc.shape[1] - halo, 1)


def first_kernel(
    frames, rows, halo, w,
    place, est, recv_a, recv_b, t_ref, b_ref, bp_ref, ta_ref, w_hbm, d_hbm,
    send_a, mid, send_b,
    y_hi, y_lo, us, qs, vs_hi, vs_lo, acc, estp, outp, wbuf, dbuf, sem,
):
    ext = rows + 2 * halo
    cols = est.shape[1]
    blocks = cols // w

    def copies(j, slot):
        window = pl.ds(pl.multiple_of(j * w, LANE), w)
        return (
            pltpu.make_async_copy(w_hbm.at[:, :, window], wbuf.at[slot], sem.at[0, slot]),
            pltpu.make_async_copy(d_hbm.at[:, :, window], dbuf.at[slot], sem.at[1, slot]),
        )

    for c in copies(0, 0):
        c.start()
    clear_edges(y_hi, y_lo, qs, ext, rows, w)
    for edge in (0, LANE + cols):
        estp[:, edge : edge + LANE] = jnp.zeros((ext, LANE), f32)
    inner = slice(LANE, LANE + cols)
    odd = lax.rem(place[1], 2)
    estp[:halo, inner] = choose(odd, recv_a[...], recv_b[...])
    estp[halo : halo + rows, inner] = est[...]
    estp[halo + rows :, inner] = choose(odd, recv_b[...], recv_a[...])
    outp[...] = jnp.zeros_like(outp)
    lane = lax.broadcasted_iota(jnp.int32, (ext, LANE), 1)

    @pl.loop(0, blocks)
    def _(j):
        slot = lax.rem(j, 2)

        @pl.when(j + 1 < blocks)
        def _():
            for c in copies(j + 1, 1 - slot):
                c.start()

        start = pl.multiple_of(j * w, LANE)
        load_image(y_hi, y_lo, estp[:, pl.ds(start, w + 2 * LANE)], halo)
        acc[...] = jnp.zeros_like(acc)
        for c in copies(j, slot):
            c.wait()
        group_terms(
            frames, rows, w, y_hi, y_lo,
            lambda f: t_ref.at[f], lambda f: b_ref.at[f], lambda f: bp_ref.at[f], ta_ref.at[0],
            lambda f: wbuf.at[slot, f], lambda f: dbuf.at[slot, f],
            us, qs, vs_hi, vs_lo, acc, None,
        )
        z = unshift(acc[...], halo)
        edge = z[:, w:]
        outp[:, pl.ds(start, LANE)] += jnp.where(lane >= LANE - halo, edge, 0.0)
        outp[:, pl.ds(pl.multiple_of(start + LANE, LANE), w)] += z[:, :w]
        outp[:, pl.ds(pl.multiple_of(start + LANE + w, LANE), LANE)] += jnp.where(lane < halo, edge, 0.0)

    send_a[...] = choose(odd, outp[:halo, inner], outp[halo + rows :, inner])
    send_b[...] = choose(odd, outp[halo + rows :, inner], outp[:halo, inner])
    mid[...] = outp[halo : halo + rows, inner]


def first_terms(place, est, recv_a, recv_b, mats, weights, observed, w):
    frames, rows, cols = weights.shape
    halo = recv_a.shape[0]
    ext = rows + 2 * halo
    return pl.pallas_call(
        functools.partial(first_kernel, frames, rows, halo, w),
        out_shape=[
            jax.ShapeDtypeStruct((halo, cols), f32),
            jax.ShapeDtypeStruct((rows, cols), f32),
            jax.ShapeDtypeStruct((halo, cols), f32),
        ],
        in_specs=[SMEM] + [VMEM] * 7 + [ANY, ANY],
        out_specs=[VMEM] * 3,
        scratch_shapes=work_scratch(frames, rows, halo, w)
        + [
            pltpu.VMEM((ext, cols + 2 * LANE), f32),
            pltpu.VMEM((ext, cols + 2 * LANE), f32),
            pltpu.VMEM((2, frames, rows, w), f32),
            pltpu.VMEM((2, frames, rows, w), f32),
            pltpu.SemaphoreType.DMA((2, 2)),
        ],
        cost_estimate=pl.CostEstimate(flops=8 * 10**9, bytes_accessed=8 * 2**20, transcendentals=0),
        name="first_terms",
    )(place, est, recv_a, recv_b, *mats, weights, observed)


def prepare_kernel(plan, frames, rows, halo, w, place, cols_in, rows_in, weights, *refs):
    outs, tile, mats, sem = refs[: len(plan)], refs[len(plan)], refs[len(plan) + 1 : -1], refs[-1]
    taps = cols_in.shape[1]
    pending = []
    for i, (distance, lead, count, _) in enumerate(plan):
        start = pl.multiple_of(jnp.bitwise_xor(place[0], distance) * w, LANE)
        for k in range(count):
            copy = pltpu.make_async_copy(
                weights.at[lead + k, :, pl.ds(start, w)],
                outs[i].at[pl.ds(k * rows, rows), :],
                sem.at[i, k],
            )
            copy.start()
            pending.append(copy)
    tile[...] = jnp.zeros_like(tile)
    tile[:frames, :taps] = cols_in[...]
    tile[frames : 2 * frames, :taps] = rows_in[...]
    for i, (_, _, count, with_taps) in enumerate(plan):
        if with_taps:
            outs[i][count * rows :, :] = tile[...]
    build_group(tile[:, : 2 * LANE], 0, frames, rows, halo, *mats)
    for copy in pending:
        copy.wait()


def prepare(plan, place, column_kernels, row_kernels, weights, w, halo):
    frames, rows, _ = weights.shape
    height = tile_height(frames)
    out = pl.pallas_call(
        functools.partial(prepare_kernel, plan, frames, rows, halo, w),
        out_shape=[
            jax.ShapeDtypeStruct((count * rows + (height if taps else 0), w), f32)
            for _, _, count, taps in plan
        ]
        + [jax.ShapeDtypeStruct((height, w), f32)]
        + matrix_shapes(1, frames, rows, halo),
        in_specs=[SMEM, VMEM, VMEM, ANY],
        out_specs=[VMEM] * (len(plan) + 5),
        scratch_shapes=[pltpu.SemaphoreType.DMA((len(plan), frames))],
        name="prepare",
    )(place, column_kernels, row_kernels, weights)
    return out[: len(plan)], out[len(plan)], out[len(plan) + 1 :]


def blocks_kernel(n, halo, w, place, send_a, mid, send_b, recv_a, recv_b, *refs):
    outs, full = refs[:-1], refs[-1]
    rows, cols = mid.shape
    odd = lax.rem(place[1], 2)
    inner = slice(LANE, LANE + cols)
    for end in (0, LANE + cols):
        full[:, end : end + LANE] = jnp.zeros((rows, LANE), f32)
    full[:halo, inner] = mid[:halo, :] + choose(odd, recv_a[...], recv_b[...])
    full[halo : rows - halo, inner] = mid[halo : rows - halo, :]
    full[rows - halo :, inner] = mid[rows - halo :, :] + choose(odd, recv_b[...], recv_a[...])
    lane = lax.broadcasted_iota(jnp.int32, (rows, LANE), 1)
    for i in range(n):
        start = jnp.bitwise_xor(place[0], i) * w
        outs[i][:rows, :] = full[:, pl.ds(pl.multiple_of(start + LANE, LANE), w)]
        before = full[:, pl.ds(pl.multiple_of(start, LANE), LANE)]
        after = full[:, pl.ds(pl.multiple_of(start + LANE + w, LANE), LANE)]
        outs[i][rows:, :] = pack_edge(jnp.where(lane >= LANE - halo, before, after), halo, w)


def column_blocks(n, place, send_a, mid, send_b, recv_a, recv_b, w):
    rows, cols = mid.shape
    halo = send_a.shape[0]
    height = rows + rows * 2 * halo // w
    return pl.pallas_call(
        functools.partial(blocks_kernel, n, halo, w),
        out_shape=[jax.ShapeDtypeStruct((height, w), f32)] * n,
        in_specs=[SMEM] + [VMEM] * 5,
        out_specs=[VMEM] * n,
        scratch_shapes=[pltpu.VMEM((rows, cols + 2 * LANE), f32)],
        name="column_blocks",
    )(place, send_a, mid, send_b, recv_a, recv_b)


def start_kernel(n, rows, halo, w, place, est, *refs):
    parts = refs[:-5]
    k0, wide, send_a, send_b, stat = refs[-5:]
    total = parts[0][...]
    for p in parts[1:]:
        total = total + p[...]
    me = place[0]
    odd = lax.rem(place[1], 2)
    at = lambda start, size: est[:, pl.ds(pl.multiple_of(start, LANE), size)]
    own = -(total[:rows] + damping * at(me * w, w))
    edge = unpack_edge(total[rows:], halo)
    before = at(jnp.maximum(me * w - LANE, 0), LANE)
    after = at(jnp.minimum(me * w + w, (n * w) - LANE), LANE)
    none = jnp.zeros((rows, LANE), f32)
    left = choose((me > 0).astype(jnp.int32), -(edge + damping * before), none)
    right = choose((me < n - 1).astype(jnp.int32), -(edge + damping * after), none)
    k0[...] = own
    wide[:, :LANE] = left
    wide[:, LANE : LANE + w] = own
    wide[:, LANE + w :] = right
    low, high = wide[:halo, :], wide[rows - halo :, :]
    send_a[...] = choose(odd, low, high)
    send_b[...] = choose(odd, high, low)
    square = own * own
    acc = square[:, :LANE]
    for c in range(LANE, w, LANE):
        acc = acc + square[:, c : c + LANE]
    stat[...] = jnp.sum(acc.reshape(rows // 8, 8, LANE), axis=0)


def start_image(n, place, est, parts, halo):
    rows, cols = est.shape
    w = cols // n
    return pl.pallas_call(
        functools.partial(start_kernel, n, rows, halo, w),
        out_shape=[
            jax.ShapeDtypeStruct((rows, w), f32),
            jax.ShapeDtypeStruct((rows, w + 2 * LANE), f32),
            jax.ShapeDtypeStruct((halo, w + 2 * LANE), f32),
            jax.ShapeDtypeStruct((halo, w + 2 * LANE), f32),
            jax.ShapeDtypeStruct((8, LANE), f32),
        ],
        in_specs=[SMEM] + [VMEM] * (1 + len(parts)),
        out_specs=[VMEM] * 5,
        name="start_image",
    )(place, est, *parts)


def apply_kernel(frames, rows, halo, w, groups, origin, cut, count, pieces, place, *refs):
    image, refs = refs[:pieces], refs[pieces:]
    t_hbm, b_hbm, bp_hbm, ta_hbm, own = refs[:5]
    moved = refs[5 : 5 + count]
    send_a, mid, send_b, stat = refs[5 + count : 9 + count]
    refs = refs[9 + count :]
    if pieces > 1:
        whole, refs = refs[0], refs[1:]
    y_hi, y_lo, us, qs, vs_hi, vs_lo, acc, tb, bb, bpb, tab, wbuf, sem, wsem = refs
    odd = lax.rem(place[1], 2)
    ext = rows + 2 * halo

    def copies(g):
        span = pl.ds(g * frames, frames)
        return [
            pltpu.make_async_copy(t_hbm.at[span], tb.at[g], sem.at[0, g]),
            pltpu.make_async_copy(b_hbm.at[span], bb.at[g], sem.at[1, g]),
            pltpu.make_async_copy(bp_hbm.at[span], bpb.at[g], sem.at[2, g]),
            pltpu.make_async_copy(ta_hbm.at[g], tab.at[g], sem.at[3, g]),
        ]

    mine = pl.ds(pl.multiple_of(place[0] * w, LANE), w)
    for g in range(groups):
        for c in copies(g):
            c.start()
        for f in range(frames):
            if g == 0:
                source = own.at[f, :, mine]
            else:
                ref, start = origin[g, f]
                source = moved[ref].at[pl.ds(start, rows), :]
            pltpu.make_async_copy(source, wbuf.at[g, f], wsem.at[g, f]).start()
    clear_edges(y_hi, y_lo, qs, ext, rows, w)
    if pieces > 1:
        wide, recv_a, recv_b = image
        whole[:halo, :] = choose(odd, recv_a[...], recv_b[...])
        whole[halo : halo + rows, :] = wide[...]
        whole[halo + rows :, :] = choose(odd, recv_b[...], recv_a[...])
        load_image(y_hi, y_lo, whole[...], halo)
    else:
        load_image(y_hi, y_lo, image[0][...], halo)
    acc[...] = jnp.zeros_like(acc)
    stat[...] = jnp.zeros_like(stat)

    @pl.loop(0, groups)
    def _(g):
        for c in copies(g):
            c.wait()
        for f in range(frames):
            pltpu.make_async_copy(own.at[f, :, mine], wbuf.at[g, f], wsem.at[g, f]).wait()
        group_terms(
            frames, rows, w, y_hi, y_lo,
            lambda f: tb.at[g, f], lambda f: bb.at[g, f], lambda f: bpb.at[g, f], tab.at[g],
            lambda f: wbuf.at[g, f], None,
            us, qs, vs_hi, vs_lo, acc, stat,
        )

    z = unshift(acc[...], halo)
    send_a[...] = choose(odd, z[:cut], z[ext - cut :])
    send_b[...] = choose(odd, z[ext - cut :], z[:cut])
    mid[...] = z[cut : ext - cut]


def apply_terms(place, image, mats, weights, moved, origin, cut, halo):
    frames, rows, _ = weights.shape
    w = image[0].shape[1] - 2 * LANE
    ext = rows + 2 * halo
    t, b, bp, ta = mats
    groups = ta.shape[0]
    wide = w + LANE
    return pl.pallas_call(
        functools.partial(apply_kernel, frames, rows, halo, w, groups, origin, cut, len(moved), len(image)),
        out_shape=[
            jax.ShapeDtypeStruct((cut, wide), f32),
            jax.ShapeDtypeStruct((ext - 2 * cut, wide), f32),
            jax.ShapeDtypeStruct((cut, wide), f32),
            jax.ShapeDtypeStruct((8, LANE), f32),
        ]
        + [jax.ShapeDtypeStruct((ext, w + 2 * LANE), f32)] * (len(image) > 1),
        in_specs=[SMEM] + [VMEM] * len(image) + [ANY] * (5 + len(moved)),
        out_specs=[VMEM] * (4 + (len(image) > 1)),
        scratch_shapes=work_scratch(frames, rows, halo, w)
        + [
            pltpu.VMEM((groups, frames) + t.shape[1:], bf16),
            pltpu.VMEM((groups, frames) + b.shape[1:], bf16),
            pltpu.VMEM((groups, frames) + bp.shape[1:], bf16),
            pltpu.VMEM((groups,) + ta.shape[1:], bf16),
            pltpu.VMEM((groups, frames, rows, w), f32),
            pltpu.SemaphoreType.DMA((4, groups)),
            pltpu.SemaphoreType.DMA((groups, frames)),
        ],
        cost_estimate=pl.CostEstimate(
            flops=groups * 3 * 10**9, bytes_accessed=groups * 2**20, transcendentals=0
        ),
    )(place, *image, t, b, bp, ta, weights, *moved)


def rows_kernel(strips, halo, w, place, send_a, mid, send_b, recv_a, recv_b, q, col_a, col_b):
    odd = lax.rem(place[1], 2)
    odd_col = lax.rem(place[0], 2)
    edge_rows, wide = send_a.shape
    ext = q.shape[0]
    row = lax.broadcasted_iota(jnp.int32, (edge_rows, wide), 0)
    strip = jnp.full((edge_rows, wide), place[1], jnp.int32)
    low = choose(odd, send_a[...], send_b[...]) + choose(odd, recv_a[...], recv_b[...])
    high = choose(odd, send_b[...], send_a[...]) + choose(odd, recv_b[...], recv_a[...])
    q[:edge_rows, :] = jnp.where((row >= halo) | (strip > 0), low, 0.0)
    q[edge_rows : ext - edge_rows, :] = mid[...]
    q[ext - edge_rows :, :] = jnp.where((row < edge_rows - halo) | (strip < strips - 1), high, 0.0)
    lane = lax.broadcasted_iota(jnp.int32, (ext, LANE), 1)
    edge = q[:, w:]
    to_left = jnp.where(lane < halo, q[:, :LANE], edge)
    to_right = jnp.where(lane >= LANE - halo, q[:, w - LANE : w], edge)
    col_a[...] = choose(odd_col, to_left, to_right)
    col_b[...] = choose(odd_col, to_right, to_left)


def merge_rows(strips, place, send_a, mid, send_b, recv_a, recv_b, halo):
    ext = mid.shape[0] + 2 * send_a.shape[0]
    wide = mid.shape[1]
    return pl.pallas_call(
        functools.partial(rows_kernel, strips, halo, wide - LANE),
        out_shape=[
            jax.ShapeDtypeStruct((ext, wide), f32),
            jax.ShapeDtypeStruct((ext, LANE), f32),
            jax.ShapeDtypeStruct((ext, LANE), f32),
        ],
        in_specs=[SMEM] + [VMEM] * 5,
        out_specs=[VMEM] * 3,
        name="merge_rows",
    )(place, send_a, mid, send_b, recv_a, recv_b)


def wrap_kernel(rows, halo, w, place, send_a, mid, send_b, recv_a, recv_b, before, out):
    odd = lax.rem(place[1], 2)
    keep = rows - 2 * halo
    pieces = (
        (0, halo, mid[:halo, :] + choose(odd, recv_a[...], recv_b[...])),
        (halo, keep, mid[halo : rows - halo, :]),
        (rows - halo, halo, mid[rows - halo :, :] + choose(odd, recv_b[...], recv_a[...])),
    )
    edges = []
    for start, size, value in pieces:
        span = slice(start, start + size)
        out[span, :] = value[:, :w] + damping * before[span, :]
        edges.append(value[:, w:])
    out[rows:, :] = pack_edge(jnp.concatenate(edges, axis=0), halo, w)


def wrap(place, send_a, mid, send_b, recv_a, recv_b, before, halo):
    rows, w = before.shape
    height = rows + rows * 2 * halo // w
    return pl.pallas_call(
        functools.partial(wrap_kernel, rows, halo, w),
        out_shape=jax.ShapeDtypeStruct((height, w), f32),
        in_specs=[SMEM] + [VMEM] * 6,
        out_specs=VMEM,
        name="wrap",
    )(place, send_a, mid, send_b, recv_a, recv_b, before)


def final_kernel(n, rows, halo, w, place, est, sums, *refs):
    k0, k1, k2 = refs[:n], refs[n : 2 * n], refs[2 * n : 3 * n]
    sol, res, full = refs[3 * n :]
    total = [jnp.sum(jnp.sum(sums[i], axis=0, keepdims=True), axis=1, keepdims=True) for i in range(4)]
    k00, k11 = total[0], total[2]
    k01 = total[1] + damping * k00
    k12 = total[3] + damping * k11
    alpha0 = k00 / k01
    norm1 = k00 - 2.0 * alpha0 * k01 + alpha0 * alpha0 * k11
    beta = norm1 / k00
    curve1 = (1.0 + beta) * (1.0 + beta) * k01 - 2.0 * (1.0 + beta) * alpha0 * k11
    curve1 = curve1 + alpha0 * alpha0 * k12
    alpha1 = norm1 / curve1
    c1 = alpha0 + alpha1 * (1.0 + beta)
    c2 = alpha0 * alpha1

    lane = lax.broadcasted_iota(jnp.int32, (rows, LANE), 1)
    spot = [jnp.bitwise_xor(place[0], i) for i in range(n)]
    for end in (0, LANE + n * w):
        full[:, end : end + LANE] = jnp.zeros((rows, LANE), f32)
    for i in range(n):
        full[:, pl.ds(pl.multiple_of(spot[i] * w + LANE, LANE), w)] = k2[i][:rows, :]
    for i in range(n):
        edge = unpack_edge(k2[i][rows:, :], halo)
        left = pl.ds(pl.multiple_of(spot[i] * w, LANE), LANE)
        right = pl.ds(pl.multiple_of(spot[i] * w + w + LANE, LANE), LANE)
        full[:, left] += jnp.where(lane >= LANE - halo, edge, 0.0)
        full[:, right] += jnp.where(lane < halo, edge, 0.0)
    for i in range(n):
        cols = pl.ds(pl.multiple_of(spot[i] * w, LANE), w)
        a0, a1 = k0[i][...], k1[i][...]
        sol[:, cols] = est[:, cols] + c1 * a0 - c2 * a1
        res[:, cols] = a0 - c1 * a1 + c2 * full[:, pl.ds(pl.multiple_of(spot[i] * w + LANE, LANE), w)]


def final_images(place, est, sums, k0, k1, k2, halo):
    n = len(k0)
    rows, w = k0[0].shape
    return pl.pallas_call(
        functools.partial(final_kernel, n, rows, halo, w),
        out_shape=[jax.ShapeDtypeStruct(est.shape, f32)] * 2,
        in_specs=[SMEM] + [VMEM] * (2 + 3 * n),
        out_specs=[VMEM] * 2,
        scratch_shapes=[pltpu.VMEM((rows, n * w + 2 * LANE), f32)],
        name="final_images",
    )(place, est, sums, *k0, *k1, *k2)


def neighbours(send_a, send_b, axis):
    n = lax.axis_size(axis)
    out = []
    for lead, x in ((0, send_a), (1, send_b)):
        pairs = [(i, i + 1) for i in range(lead, n - 1, 2)]
        out.append(lax.ppermute(x, axis, pairs + [(b, a) for a, b in pairs]))
    return out


def swap(x, axis, distance):
    n = lax.axis_size(axis)
    return lax.ppermute(x, axis, [(i, i ^ distance) for i in range(n)])


def steps(estimate, observed, weights, column_kernels, row_kernels):
    n = lax.axis_size("frame")
    me = lax.axis_index("frame")
    strips = lax.axis_size("strip")
    strip = lax.axis_index("strip")
    place = jnp.stack([me, strip]).astype(jnp.int32)
    rows, cols = estimate.shape
    frames = weights.shape[0]
    halo = column_kernels.shape[1] // 2
    w = cols // n
    ext = rows + 2 * halo
    distances = [1 << k for k in range(n.bit_length() - 1)]

    def fold(x):
        return jnp.sum(x.reshape(rows * w // (8 * LANE), 8, LANE), axis=0)

    low, high = estimate[:halo], estimate[rows - halo :]
    odd = strip % 2 == 1
    est_a, est_b = neighbours(
        jnp.where(odd, low, high), jnp.where(odd, high, low), "strip"
    )

    early = frames // 2
    plan = [(d, 0, frames, True) for d in range(1, n - 1)]
    plan += [(n - 1, 0, early, True), (n - 1, early, frames - early, False)]
    packed, tile, own_mats = prepare(plan, place, column_kernels, row_kernels, weights, w, halo)
    moved = []
    for i, (d, _, _, taps) in enumerate(plan):
        moved.append(swap(packed[i], "frame", d))
    origin = {}
    starts = [0]
    for i, (d, lead, count, taps) in enumerate(plan):
        for k in range(count):
            origin[d, lead + k] = (i, k * rows)
        if taps:
            starts.append(count * rows)

    send_a, mid, send_b = first_terms(
        place, estimate, est_a, est_b, own_mats, weights, observed, w
    )
    mats = setup_matrices([tile] + moved[: n - 1], starts, frames, rows, halo)
    recv_a, recv_b = neighbours(send_a, send_b, "strip")

    part = list(column_blocks(n, place, send_a, mid, send_b, recv_a, recv_b, w))
    mine = [part[0]]
    for i in range(n - 1, 0, -1):
        d = i & -i
        got = swap(part[i], "frame", d)
        if i == d:
            mine.append(got)
        else:
            part[i ^ d] = part[i ^ d] + got
    k0, wide, send_a, send_b, k00_part = start_image(n, place, estimate, mine, halo)
    recv_a, recv_b = neighbours(send_a, send_b, "strip")

    send_a, mid, send_b, stat1, k0x = apply_terms(
        place, (wide, recv_a, recv_b), mats, weights, moved, origin, 2 * halo, halo
    )
    recv_a, recv_b = neighbours(send_a, send_b, "strip")
    q, col_a, col_b = merge_rows(strips, place, send_a, mid, send_b, recv_a, recv_b, halo)
    recv_a, recv_b = neighbours(col_a, col_b, "frame")
    odd = me % 2 == 1
    from_left = jnp.where(odd, recv_a, recv_b)
    from_right = jnp.where(odd, recv_b, recv_a)
    lane = lax.broadcasted_iota(jnp.int32, (ext, LANE), 1)
    left_tile = jnp.where(me == 0, 0.0, q[:, w:] + from_left)
    right_tile = jnp.where(me == n - 1, 0.0, q[:, w:] + from_right)
    own_left = jnp.where(lane < halo, from_left, 0.0)
    own_right = jnp.where(lane >= LANE - halo, from_right, 0.0)
    pad = jnp.zeros((ext, w - LANE), f32)
    own = (
        q[:, :w]
        + jnp.concatenate([own_left, pad], axis=1)
        + jnp.concatenate([pad, own_right], axis=1)
    )
    k1x = jnp.concatenate([left_tile, own, right_tile], axis=1) + damping * k0x
    k1, k1x = lax.optimization_barrier((k1x[halo : halo + rows, LANE : LANE + w], k1x))
    k11_part = fold(k1 * k1)

    send_a, mid, send_b, stat2 = apply_terms(
        place, (k1x,), mats, weights, moved, origin, halo, halo
    )
    recv_a, recv_b = neighbours(send_a, send_b, "strip")
    sums = jnp.stack([k00_part, stat1, k11_part, stat2])
    for axis, size in (("frame", n), ("strip", strips)):
        d = 1
        while d < size:
            sums = sums + swap(sums, axis, d)
            d *= 2
    k2 = wrap(place, send_a, mid, send_b, recv_a, recv_b, k1, halo)

    def gathered(x):
        parts = [x] + [None] * (n - 1)
        for i in range(n):
            for d in reversed(distances):
                if i % (2 * d) == 0:
                    parts[i + d] = swap(parts[i], "frame", d)
        return parts

    g0, g1, g2 = gathered(k0), gathered(k1), gathered(k2)
    return tuple(final_images(place, estimate, sums, g0, g1, g2, halo))


def solution(mesh):
    return jax.shard_map(
        steps,
        mesh=mesh,
        in_specs=(
            P("strip", None),
            P("frame", "strip", None),
            P("frame", "strip", None),
            P("frame", None),
            P("frame", None),
        ),
        out_specs=(P("strip", None), P("strip", None)),
        check_vma=False,
    )
```

time: 242 us -> 235 us (0.971)
  starting transfers between devices: 69.9 us -> 61.4 us
  Pallas kernels: 49.2 us -> 55.7 us
  other arithmetic: 9.13 us -> 6.13 us
    ppermute x14 -> x12, starting transfers between devices: 49 us -> 27.3 us  [neighbours(): out.append(lax.ppermute(x, axis, pairs + [(b, a) for a, b in pairs]))]
    ppermute x21, starting transfers between devices: 20.9 us -> 34.1 us  [swap(): return lax.ppermute(x, axis, [(i, i ^ distance) for i in range(n)])]
    pallas_call x3 -> x5, Pallas kernels: 9.76 us -> 16.2 us  [the longest x1 4.46 us: setup_matrices(): pl.pallas_call(functools.partial(setup_kernel, frames, rows, halo, starts...]
    ppermute x21, waiting for transfers between devices: 88.6 us -> 85.9 us  [swap(): return lax.ppermute(x, axis, [(i, i ^ distance) for i in range(n)])]
    unnamed x46 -> x70, local copies, waits for them, and re-layouts: 5.82 us -> 7.25 us
    ppermute x14 -> x12, waiting for transfers between devices: 14.8 us -> 15.5 us  [neighbours(): out.append(lax.ppermute(x, axis, pairs + [(b, a) for a, b in pairs]))]
  transfers between devices with their start and end apart: 35 -> 33, of which waited for: 21 -> 15; matrix products, arithmetic and copies ran while one was open for 3% -> 1% of each run, Pallas kernels for 5% -> 6%
where the time goes in v4:
time: 235 us; the launch traced here: 233 us
  waiting for transfers between devices  101 us (43%)
  starting transfers between devices  61.4 us (26%)
  Pallas kernels  55.7 us (24%)
  local copies, waits for them, and re-layouts  7.29 us (3%)
  other arithmetic  6.13 us (3%)
    ppermute x21, waiting for transfers between devices, swap(): return lax.ppermute(x, axis, [(i, i ^ distance) for i in range(n)])  85.9 us
    ppermute x21, starting transfers between devices, swap(): return lax.ppermute(x, axis, [(i, i ^ distance) for i in range(n)])  34.1 us
    ppermute x12, starting transfers between devices, neighbours(): out.append(lax.ppermute(x, axis, pairs + [(b, a) for a, b in pairs]))  27.3 us
    pallas_call x2, Pallas kernels, apply_terms(): pl.pallas_call(functools.partial(apply_kernel, frames, rows, halo, w, gro...  21.5 us
    ppermute x12, waiting for transfers between devices, neighbours(): out.append(lax.ppermute(x, axis, pairs + [(b, a) for a, b in pairs]))  15.5 us
    pallas_call x1, Pallas kernels, first_terms(): pl.pallas_call(functools.partial(first_kernel, frames, rows, halo, w), ou...  12 us
    unnamed x70, local copies, waits for them, and re-layouts  7.25 us
  transfers between devices with their start and end apart: 33, of which 15 were waited for; matrix products, arithmetic and copies ran while one was open for 1% of the time, Pallas kernels for 6%

profile of v4, /device:TPU:2, one launch (start us, length us, event | category | flops | bytes accessed | tf_op | source)
XLA Modules:
  0.0 233.1 jit_solution(16888566797223164558)
XLA Ops:
  0.6 1.1 slice_select_fusion
  1.8 1.9 collective-permute-start.1
  4.3 4.0 %prepare.1 = (f32[264,512]{1,0:T(8,128)}, f32[264,512]{1,0:T(8,128)}, f32[136,512]{1,0:T(8,128)}, f32[128,512]{1,0:T(8,128)}, f32[8,512]{1,0:T(8,128)}, /*index=...) custom-call(s32[2]{0:T(128)} %pad_add_fusion.1.place, ...), custom_call_target="tpu_custom_call" | custom-call | tf_op jit(solution)/shard_map/prepare/pallas_call | solution.py:329
  8.4 1.1 collective-permute-done.1.recv_b
  10.2 12.0 %first_terms.1 = (f32[32,2048]{1,0:T(8,128)}, f32[128,2048]{1,0:T(8,128)}, f32[32,2048]{1,0:T(8,128)}) custom-call(s32[2]{0:T(128)} %pad_add_fusion.1.place, f32[128,2048]{1,0:T(8,128)} %est.5, f32[32,2048]{1,0:T(8,128)} %copy-done.31, f32[32,2048]{1,0:T(8,128)} %copy-done.32, bf16[2,256,256]{2,1,0:T(8,128)(2,1)} %get-tuple-element.41.t_ref, ...), custom_call_target="tpu_custom_call" | custom-call | flops 8000000000 | bytes 8388608 | tf_op jit(solution)/shard_map/first_terms/pallas_call | solution.py:279
  22.2 3.6 %collective-permute-start.2 = (f32[32,2048]{1,0:T(8,128)}, f32[32,2048]{1,0:T(8,128)S(1)}, u32[]{:S(2)}, u32[]{:S(2)}) collective-permute-start(f32[32,2048]{1,0:T(8,128)} %get-tuple-element.45.send_a), channel_id=1, source_target_pairs={{0,4},{8,12},{16,20},{24,28},{4,0},{12,8},{20,16},{28,24},{1,5},{9... | collective-permute-start | bytes 786440 | tf_op jit(solution)/shard_map/ppermute | solution.py:640
  25.8 1.9 collective-permute-start.3
  27.8 6.7 %collective-permute-done.3.recv_b = f32[32,2048]{1,0:T(8,128)S(1)} collective-permute-done((f32[32,2048]{1,0:T(8,128)}, f32[32,2048]{1,0:T(8,128)S(1)}, u32[]{:S(2)}, u32[]{:S(2)}) %collective-permute-start.3) | collective-permute-done | bytes 262176 | tf_op jit(solution)/shard_map/ppermute | solution.py:640
  35.2 2.8 %column_blocks.1 = (f32[144,512]{1,0:T(8,128)}, f32[144,512]{1,0:T(8,128)}, f32[144,512]{1,0:T(8,128)}, f32[144,512]{1,0:T(8,128)}) custom-call(s32[2]{0:T(128)} %pad_add_fusion.1.place, f32[32,2048]{1,0:T(8,128)} %get-tuple-element.45.send_a, f32[128,2048]{1,0:T(8,128)} %get-tuple-element.46.mid, f32[32,2048]{1,0:T(8,128)} %get-tuple-element.47.send_b, ...), custom_call_target="tpu_custom_call" | custom-call | tf_op jit(solution)/shard_map/column_blocks/pallas_call | solution.py:368
  39.0 1.0 collective-permute-start.6
  40.0 2.0 collective-permute-start.10
  42.0 1.5 collective-permute-start.9
  43.6 15.3 %collective-permute-done.4 = f32[144,512]{1,0:T(8,128)S(1)} collective-permute-done((f32[144,512]{1,0:T(8,128)}, f32[144,512]{1,0:T(8,128)S(1)}, u32[]{:S(2)}, u32[]{:S(2)}) %collective-permute-start.4) | collective-permute-done | bytes 294944 | tf_op jit(solution)/shard_map/ppermute | solution.py:646
  58.8 1.0 add.45
  59.9 2.0 collective-permute-start.11
  61.9 3.2 %collective-permute-done.6.refs_2_ = f32[144,512]{1,0:T(8,128)S(1)} collective-permute-done((f32[144,512]{1,0:T(8,128)}, f32[144,512]{1,0:T(8,128)S(1)}, u32[]{:S(2)}, u32[]{:S(2)}) %collective-permute-start.6) | collective-permute-done | bytes 294944 | tf_op jit(solution)/shard_map/ppermute | solution.py:646
  65.9 15.4 %collective-permute-done.5.refs_1_ = f32[144,512]{1,0:T(8,128)S(1)} collective-permute-done((f32[144,512]{1,0:T(8,128)S(1)}, f32[144,512]{1,0:T(8,128)S(1)}, u32[]{:S(2)}, u32[]{:S(2)}) %collective-permute-start.5) | collective-permute-done | bytes 294944 | tf_op jit(solution)/shard_map/ppermute | solution.py:646
  82.0 2.6 %start_image.1 = (f32[128,512]{1,0:T(8,128)}, f32[128,768]{1,0:T(8,128)}, f32[32,768]{1,0:T(8,128)}, f32[32,768]{1,0:T(8,128)}, f32[8,128]{1,0:T(8,128)}) custom-call(s32[2]{0:T(128)} %pad_add_fusion.1.place, f32[128,2048]{1,0:T(8,128)} %est.5, f32[144,512]{1,0:T(8,128)} %get-tuple-element.48.refs_0_, f32[144,512]{1,0:T(8,128)} %copy-done.10, ...), custom_call_target="tpu_custom_call" | custom-call | tf_op jit(solution)/shard_map/start_image/pallas_call | solution.py:411
  84.6 2.6 %collective-permute-start.7 = (f32[32,768]{1,0:T(8,128)}, f32[32,768]{1,0:T(8,128)S(1)}, u32[]{:S(2)}, u32[]{:S(2)}) collective-permute-start(f32[32,768]{1,0:T(8,128)} %get-tuple-element.54), channel_id=1, source_target_pairs={{0,4},{8,12},{16,20},{24,28},{4,0},{12,8},{20,16},{28,24},{1,5},{9... | collective-permute-start | bytes 294920 | tf_op jit(solution)/shard_map/ppermute | solution.py:640
  87.2 3.0 %collective-permute-done.11.refs_3_.refs_10_.refs_8_ = f32[136,512]{1,0:T(8,128)S(1)} collective-permute-done((f32[136,512]{1,0:T(8,128)S(1)}, f32[136,512]{1,0:T(8,128)S(1)}, u32[]{:S(2)}, u32[]{:S(2)}) %collective-permute-start.11) | collective-permute-done | bytes 278560 | tf_op jit(solution)/shard_map/ppermute | solution.py:646
  90.2 1.9 collective-permute-start.8
  93.1 4.5 %setup_all.1 = (bf16[8,256,256]{2,1,0:T(8,128)(2,1)}, bf16[8,256,256]{2,1,0:T(8,128)(2,1)}, bf16[8,256,256]{2,1,0:T(8,128)(2,1)}, bf16[4,384,256]{2,1,0:T(8,128)(2,1)}) custom-call(f32[8,512]{1,0:T(8,128)} %get-tuple-element.56.refs_0_, f32[264,512]{1,0:T(8,128)} %copy-done.5, f32[264,512]{1,0:T(8,128)} %copy-done.4, f32[136,512]{1,0:T(8,128)} %copy-done.11), custom_call_target="tpu_custom_call" | custom-call | tf_op jit(solution)/shard_map/setup_all/pallas_call | solution.py:130
  98.3 10.7 %shard_map.68 = (f32[64,640]{1,0:T(8,128)}, f32[64,640]{1,0:T(8,128)}, f32[64,640]{1,0:T(8,128)}, f32[8,128]{1,0:T(8,128)}, f32[192,768]{1,0:T(8,128)}) custom-call(s32[2]{0:T(128)} %pad_add_fusion.1.place, f32[128,768]{1,0:T(8,128)} %get-tuple-element.53.refs_0_, f32[32,768]{1,0:T(8,128)} %copy-done.33, f32[32,768]{1,0:T(8,128)} %copy-done.34, ...), custom_call_target="tpu_custom_call" | custom-call | flops 12000000000 | bytes 4194304 | tf_op jit(solution)/shard_map/pallas_call | solution.py:496
  109.0 5.2 %collective-permute-start.13 = (f32[64,640]{1,0:T(8,128)}, f32[64,640]{1,0:T(8,128)S(1)}, u32[]{:S(2)}, u32[]{:S(2)}) collective-permute-start(f32[64,640]{1,0:T(8,128)} %get-tuple-element.66.send_a), channel_id=1, source_target_pairs={{0,4},{8,12},{16,20},{24,28},{4,0},{12,8},{20,16},{28,24},{1,5},{9... | collective-permute-start | bytes 491528 | tf_op jit(solution)/shard_map/ppermute | solution.py:640
  114.2 1.9 collective-permute-start.14
  116.2 4.9 %collective-permute-done.14.recv_b = f32[64,640]{1,0:T(8,128)S(1)} collective-permute-done((f32[64,640]{1,0:T(8,128)}, f32[64,640]{1,0:T(8,128)S(1)}, u32[]{:S(2)}, u32[]{:S(2)}) %collective-permute-start.14) | collective-permute-done | bytes 163872 | tf_op jit(solution)/shard_map/ppermute | solution.py:640
  121.7 2.2 merge_rows.1
  124.0 5.3 %collective-permute-start.15 = (f32[192,128]{1,0:T(8,128)}, f32[192,128]{1,0:T(8,128)S(1)}, u32[]{:S(2)}, u32[]{:S(2)}) collective-permute-start(f32[192,128]{1,0:T(8,128)} %get-tuple-element.70), channel_id=1, source_target_pairs={{0,1},{2,3},{1,0},{3,2},{4,5},{6,7},{5,4},{7,6},{8,9},{10,11},{9,8... | collective-permute-start | bytes 294920 | tf_op jit(solution)/shard_map/ppermute | solution.py:640
  130.0 2.8 %collective-permute-done.15 = f32[192,128]{1,0:T(8,128)S(1)} collective-permute-done((f32[192,128]{1,0:T(8,128)}, f32[192,128]{1,0:T(8,128)S(1)}, u32[]{:S(2)}, u32[]{:S(2)}) %collective-permute-start.15) | collective-permute-done | bytes 98336 | tf_op jit(solution)/shard_map/ppermute | solution.py:640
  133.7 1.0 pad_add_fusion
  135.7 10.8 %shard_map.69 = (f32[32,640]{1,0:T(8,128)}, f32[128,640]{1,0:T(8,128)}, f32[32,640]{1,0:T(8,128)}, f32[8,128]{1,0:T(8,128)}) custom-call(s32[2]{0:T(128)} %pad_add_fusion.1.place, f32[192,768]{1,0:T(8,128)} %copy-done.2, bf16[8,256,256]{2,1,0:T(8,128)(2,1)} %get-tuple-element.60.refs_3_.refs_1_, bf16[8,256,256]{2,1,0:T(8,128)(2,1)} %get-tuple-element.61.refs_4_.refs_2_, ...), custom_call_target="tpu_custom_call" | custom-call | flops 12000000000 | bytes 4194304 | tf_op jit(solution)/shard_map/pallas_call | solution.py:496
  146.8 1.9 collective-permute-start.29
  149.5 3.9 %collective-permute-start.17 = (f32[4,8,128]{2,1,0:T(8,128)S(1)}, f32[4,8,128]{2,1,0:T(8,128)S(1)}, u32[]{:S(2)}, u32[]{:S(2)}) collective-permute-start(f32[4,8,128]{2,1,0:T(8,128)S(1)} %pad_maximum_fusion), channel_id=1, source_target_pairs={{0,1},{1,0},{2,3},{3,2},{4,5},{5,4},{6,7},{7,6},{8,9},{9,8},{10,11... | collective-permute-start | bytes 49160 | tf_op jit(solution)/shard_map/ppermute | solution.py:646
  154.1 2.1 wrap.1.refs_8_
  156.2 4.4 %collective-permute-start.31 = (f32[144,512]{1,0:T(8,128)}, f32[144,512]{1,0:T(8,128)S(1)}, u32[]{:S(2)}, u32[]{:S(2)}) collective-permute-start(f32[144,512]{1,0:T(8,128)} %wrap.1.refs_8_), channel_id=1, source_target_pairs={{0,2},{1,3},{2,0},{3,1},{4,6},{5,7},{6,4},{7,5},{8,10},{9,11},{10,... | collective-permute-start | bytes 884744 | tf_op jit(solution)/shard_map/ppermute | solution.py:646
  160.7 2.9 %collective-permute-start.23 = (f32[128,512]{1,0:T(8,128)S(1)}, f32[128,512]{1,0:T(8,128)S(1)}, u32[]{:S(2)}, u32[]{:S(2)}) collective-permute-start(f32[128,512]{1,0:T(8,128)S(1)} %copy-done.12), channel_id=1, source_target_pairs={{0,2},{1,3},{2,0},{3,1},{4,6},{5,7},{6,4},{7,5},{8,10},{9,11},{10,... | collective-permute-start | bytes 786440 | tf_op jit(solution)/shard_map/ppermute | solution.py:646
  163.6 1.7 collective-permute-start.26
  165.3 15.3 %collective-permute-done.18 = f32[4,8,128]{2,1,0:T(8,128)S(1)} collective-permute-done((f32[4,8,128]{2,1,0:T(8,128)S(1)}, f32[4,8,128]{2,1,0:T(8,128)S(1)}, u32[]{:S(2)}, u32[]{:S(2)}) %collective-permute-start.18) | collective-permute-done | bytes 16416 | tf_op jit(solution)/shard_map/ppermute | solution.py:646
  180.5 7.3 %collective-permute-start.19 = (f32[4,8,128]{2,1,0:T(8,128)S(1)}, f32[4,8,128]{2,1,0:T(8,128)S(1)}, u32[]{:S(2)}, u32[]{:S(2)}) collective-permute-start(f32[4,8,128]{2,1,0:T(8,128)S(1)} %fusion.1), channel_id=1, source_target_pairs={{0,4},{4,0},{8,12},{12,8},{16,20},{20,16},{24,28},{28,24},{1,5},{5... | collective-permute-start | bytes 49160 | tf_op jit(solution)/shard_map/ppermute | solution.py:646
  188.6 3.7 %collective-permute-done.20 = f32[4,8,128]{2,1,0:T(8,128)S(1)} collective-permute-done((f32[4,8,128]{2,1,0:T(8,128)S(1)}, f32[4,8,128]{2,1,0:T(8,128)S(1)}, u32[]{:S(2)}, u32[]{:S(2)}) %collective-permute-start.20) | collective-permute-done | bytes 16416 | tf_op jit(solution)/shard_map/ppermute | solution.py:646
  192.4 2.0 collective-permute-start.32
  194.4 1.4 collective-permute-start.21
  195.9 2.4 %collective-permute-done.21 = f32[4,8,128]{2,1,0:T(8,128)S(1)} collective-permute-done((f32[4,8,128]{2,1,0:T(8,128)S(1)}, f32[4,8,128]{2,1,0:T(8,128)S(1)}, u32[]{:S(2)}, u32[]{:S(2)}) %collective-permute-start.21) | collective-permute-done | bytes 16416 | tf_op jit(solution)/shard_map/ppermute | solution.py:646
  198.3 2.0 collective-permute-start.27
  200.9 15.6 %collective-permute-done.24.refs_3_ = f32[128,512]{1,0:T(8,128)S(1)} collective-permute-done((f32[128,512]{1,0:T(8,128)S(1)}, f32[128,512]{1,0:T(8,128)S(1)}, u32[]{:S(2)}, u32[]{:S(2)}) %collective-permute-start.24) | collective-permute-done | bytes 262176 | tf_op jit(solution)/shard_map/ppermute | solution.py:646
  216.5 5.6 %collective-permute-done.25.refs_5_ = f32[128,512]{1,0:T(8,128)S(1)} collective-permute-done((f32[128,512]{1,0:T(8,128)S(1)}, f32[128,512]{1,0:T(8,128)S(1)}, u32[]{:S(2)}, u32[]{:S(2)}) %collective-permute-start.25) | collective-permute-done | bytes 262176 | tf_op jit(solution)/shard_map/ppermute | solution.py:646
  222.1 5.5 %collective-permute-done.27.refs_7_ = f32[128,512]{1,0:T(8,128)S(1)} collective-permute-done((f32[128,512]{1,0:T(8,128)S(1)}, f32[128,512]{1,0:T(8,128)S(1)}, u32[]{:S(2)}, u32[]{:S(2)}) %collective-permute-start.27) | collective-permute-done | bytes 262176 | tf_op jit(solution)/shard_map/ppermute | solution.py:646
  229.1 4.0 %final_images.1 = (f32[128,2048]{1,0:T(8,128)}, f32[128,2048]{1,0:T(8,128)}) custom-call(s32[2]{0:T(128)} %pad_add_fusion.1.place, f32[128,2048]{1,0:T(8,128)} %est.5, f32[4,8,128]{2,1,0:T(8,128)} %add.56.sums, f32[128,512]{1,0:T(8,128)} %get-tuple-element.76.refs_0_, f32[128,512]{1,0:T(8,128)} %copy-done.14, f32[128,512]{1,0:T(8,128)} %copy-done.13, ...), custom_call_target="tpu_custom_call" | custom-call | tf_op jit(solution)/shard_map/final_images/pallas_call | solution.py:625
  (115 shorter events, 14.2 us)
Async XLA Ops:
  1.7 6.6 %collective-permute-start = (f32[32,2048]{1,0:T(8,128)S(1)}, f32[32,2048]{1,0:T(8,128)S(1)}, u32[]{:S(2)}, u32[]{:S(2)}) collective-permute-start(f32[32,2048]{1,0:T(8,128)S(1)} %get-tuple-element.81), channel_id=1, source_target_pairs={{0,4},{8,12},{16,20},{24,28},{4,0},{12,8},{20,16},{28,24},{1,5},{9... | collective-permute-start | bytes 786440 | tf_op jit(solution)/shard_map/ppermute | solution.py:640
  1.8 7.7 %collective-permute-start.1 = (f32[32,2048]{1,0:T(8,128)S(1)}, f32[32,2048]{1,0:T(8,128)S(1)}, u32[]{:S(2)}, u32[]{:S(2)}) collective-permute-start(f32[32,2048]{1,0:T(8,128)S(1)} %get-tuple-element.80), channel_id=1, source_target_pairs={{4,8},{12,16},{20,24},{8,4},{16,12},{24,20},{5,9},{13,17},{21,25},... | collective-permute-start | bytes 786440 | tf_op jit(solution)/shard_map/ppermute | solution.py:640
  22.2 17.9 %copy-start.29 = (f32[264,512]{1,0:T(8,128)S(1)}, f32[264,512]{1,0:T(8,128)}, u32[]{:S(2)}) copy-start(f32[264,512]{1,0:T(8,128)} %get-tuple-element.58) | copy-start | bytes 1622020
  22.2 19.8 %copy-start.28 = (f32[264,512]{1,0:T(8,128)S(1)}, f32[264,512]{1,0:T(8,128)}, u32[]{:S(2)}) copy-start(f32[264,512]{1,0:T(8,128)} %get-tuple-element.57) | copy-start | bytes 1622020
  22.2 37.8 %copy-start.30 = (f32[136,512]{1,0:T(8,128)S(1)}, f32[136,512]{1,0:T(8,128)}, u32[]{:S(2)}) copy-start(f32[136,512]{1,0:T(8,128)} %get-tuple-element.59) | copy-start | bytes 835588
  22.2 5.5 %collective-permute-start.2 = (f32[32,2048]{1,0:T(8,128)}, f32[32,2048]{1,0:T(8,128)S(1)}, u32[]{:S(2)}, u32[]{:S(2)}) collective-permute-start(f32[32,2048]{1,0:T(8,128)} %get-tuple-element.45.send_a), channel_id=1, source_target_pairs={{0,4},{8,12},{16,20},{24,28},{4,0},{12,8},{20,16},{28,24},{1,5},{9... | collective-permute-start | bytes 786440 | tf_op jit(solution)/shard_map/ppermute | solution.py:640
  25.8 8.6 %collective-permute-start.3 = (f32[32,2048]{1,0:T(8,128)}, f32[32,2048]{1,0:T(8,128)S(1)}, u32[]{:S(2)}, u32[]{:S(2)}) collective-permute-start(f32[32,2048]{1,0:T(8,128)} %get-tuple-element.47.send_b), channel_id=1, source_target_pairs={{4,8},{12,16},{20,24},{8,4},{16,12},{24,20},{5,9},{13,17},{21,25},... | collective-permute-start | bytes 786440 | tf_op jit(solution)/shard_map/ppermute | solution.py:640
  38.0 20.9 %collective-permute-start.4 = (f32[144,512]{1,0:T(8,128)}, f32[144,512]{1,0:T(8,128)S(1)}, u32[]{:S(2)}, u32[]{:S(2)}) collective-permute-start(f32[144,512]{1,0:T(8,128)} %get-tuple-element.50), channel_id=1, source_target_pairs={{0,1},{1,0},{2,3},{3,2},{4,5},{5,4},{6,7},{7,6},{8,9},{9,8},{10,11... | collective-permute-start | bytes 884744 | tf_op jit(solution)/shard_map/ppermute | solution.py:646
  39.0 26.2 %collective-permute-start.6 = (f32[144,512]{1,0:T(8,128)}, f32[144,512]{1,0:T(8,128)S(1)}, u32[]{:S(2)}, u32[]{:S(2)}) collective-permute-start(f32[144,512]{1,0:T(8,128)} %get-tuple-element.51), channel_id=1, source_target_pairs={{0,1},{1,0},{2,3},{3,2},{4,5},{5,4},{6,7},{7,6},{8,9},{9,8},{10,11... | collective-permute-start | bytes 884744 | tf_op jit(solution)/shard_map/ppermute | solution.py:646
  40.0 52.1 %collective-permute-start.10 = (f32[264,512]{1,0:T(8,128)S(1)}, f32[264,512]{1,0:T(8,128)S(1)}, u32[]{:S(2)}, u32[]{:S(2)}) collective-permute-start(f32[264,512]{1,0:T(8,128)S(1)} %copy-done.29), channel_id=1, source_target_pairs={{0,2},{1,3},{2,0},{3,1},{4,6},{5,7},{6,4},{7,5},{8,10},{9,11},{10,... | collective-permute-start | bytes 1622024 | tf_op jit(solution)/shard_map/ppermute | solution.py:646
  42.0 50.1 %collective-permute-start.9 = (f32[264,512]{1,0:T(8,128)S(1)}, f32[264,512]{1,0:T(8,128)S(1)}, u32[]{:S(2)}, u32[]{:S(2)}) collective-permute-start(f32[264,512]{1,0:T(8,128)S(1)} %copy-done.28), channel_id=1, source_target_pairs={{0,1},{1,0},{2,3},{3,2},{4,5},{5,4},{6,7},{7,6},{8,9},{9,8},{10,11... | collective-permute-start | bytes 1622024 | tf_op jit(solution)/shard_map/ppermute | solution.py:646
  59.9 21.4 %collective-permute-start.5 = (f32[144,512]{1,0:T(8,128)S(1)}, f32[144,512]{1,0:T(8,128)S(1)}, u32[]{:S(2)}, u32[]{:S(2)}) collective-permute-start(f32[144,512]{1,0:T(8,128)S(1)} %add.45), channel_id=1, source_target_pairs={{0,2},{1,3},{2,0},{3,1},{4,6},{5,7},{6,4},{7,5},{8,10},{9,11},{10,... | collective-permute-start | bytes 884744 | tf_op jit(solution)/shard_map/ppermute | solution.py:646
  59.9 30.2 %collective-permute-start.11 = (f32[136,512]{1,0:T(8,128)S(1)}, f32[136,512]{1,0:T(8,128)S(1)}, u32[]{:S(2)}, u32[]{:S(2)}) collective-permute-start(f32[136,512]{1,0:T(8,128)S(1)} %copy-done.30), channel_id=1, source_target_pairs={{0,3},{1,2},{2,1},{3,0},{4,7},{5,6},{6,5},{7,4},{8,11},{9,10},{10,... | collective-permute-start | bytes 835592 | tf_op jit(solution)/shard_map/ppermute | solution.py:646
  65.2 16.1 %copy-start.9 = (f32[144,512]{1,0:T(8,128)}, f32[144,512]{1,0:T(8,128)S(1)}, u32[]{:S(2)}) copy-start(f32[144,512]{1,0:T(8,128)S(1)} %collective-permute-done.6.refs_2_) | copy-start | bytes 884740
  65.2 32.4 %collective-permute-start.12 = (f32[128,512]{1,0:T(8,128)}, f32[128,512]{1,0:T(8,128)}, u32[]{:S(2)}, u32[]{:S(2)}) collective-permute-start(f32[128,512]{1,0:T(8,128)} %get-tuple-element.64), channel_id=1, source_target_pairs={{0,3},{1,2},{2,1},{3,0},{4,7},{5,6},{6,5},{7,4},{8,11},{9,10},{10,... | collective-permute-start | bytes 786440 | tf_op jit(solution)/shard_map/ppermute | solution.py:646
  84.6 13.0 %collective-permute-start.7 = (f32[32,768]{1,0:T(8,128)}, f32[32,768]{1,0:T(8,128)S(1)}, u32[]{:S(2)}, u32[]{:S(2)}) collective-permute-start(f32[32,768]{1,0:T(8,128)} %get-tuple-element.54), channel_id=1, source_target_pairs={{0,4},{8,12},{16,20},{24,28},{4,0},{12,8},{20,16},{28,24},{1,5},{9... | collective-permute-start | bytes 294920 | tf_op jit(solution)/shard_map/ppermute | solution.py:640
  90.2 7.4 %collective-permute-start.8 = (f32[32,768]{1,0:T(8,128)}, f32[32,768]{1,0:T(8,128)S(1)}, u32[]{:S(2)}, u32[]{:S(2)}) collective-permute-start(f32[32,768]{1,0:T(8,128)} %get-tuple-element.55), channel_id=1, source_target_pairs={{4,8},{12,16},{20,24},{8,4},{16,12},{24,20},{5,9},{13,17},{21,25},... | collective-permute-start | bytes 294920 | tf_op jit(solution)/shard_map/ppermute | solution.py:640
  109.0 25.8 %copy-start.3 = (f32[192,768]{1,0:T(8,128)S(1)}, f32[192,768]{1,0:T(8,128)}, u32[]{:S(2)}) copy-start(f32[192,768]{1,0:T(8,128)} %get-tuple-element.72) | copy-start | bytes 1769476
  109.0 7.2 %collective-permute-start.13 = (f32[64,640]{1,0:T(8,128)}, f32[64,640]{1,0:T(8,128)S(1)}, u32[]{:S(2)}, u32[]{:S(2)}) collective-permute-start(f32[64,640]{1,0:T(8,128)} %get-tuple-element.66.send_a), channel_id=1, source_target_pairs={{0,4},{8,12},{16,20},{24,28},{4,0},{12,8},{20,16},{28,24},{1,5},{9... | collective-permute-start | bytes 491528 | tf_op jit(solution)/shard_map/ppermute | solution.py:640
  114.2 6.8 %collective-permute-start.14 = (f32[64,640]{1,0:T(8,128)}, f32[64,640]{1,0:T(8,128)S(1)}, u32[]{:S(2)}, u32[]{:S(2)}) collective-permute-start(f32[64,640]{1,0:T(8,128)} %get-tuple-element.68.send_b), channel_id=1, source_target_pairs={{4,8},{12,16},{20,24},{8,4},{16,12},{24,20},{5,9},{13,17},{21,25},... | collective-permute-start | bytes 491528 | tf_op jit(solution)/shard_map/ppermute | solution.py:640
  124.0 8.8 %collective-permute-start.15 = (f32[192,128]{1,0:T(8,128)}, f32[192,128]{1,0:T(8,128)S(1)}, u32[]{:S(2)}, u32[]{:S(2)}) collective-permute-start(f32[192,128]{1,0:T(8,128)} %get-tuple-element.70), channel_id=1, source_target_pairs={{0,1},{2,3},{1,0},{3,2},{4,5},{6,7},{5,4},{7,6},{8,9},{10,11},{9,8... | collective-permute-start | bytes 294920 | tf_op jit(solution)/shard_map/ppermute | solution.py:640
  129.3 3.5 %collective-permute-start.16 = (f32[192,128]{1,0:T(8,128)}, f32[192,128]{1,0:T(8,128)S(1)}, u32[]{:S(2)}, u32[]{:S(2)}) collective-permute-start(f32[192,128]{1,0:T(8,128)} %get-tuple-element.71), channel_id=1, source_target_pairs={{1,2},{2,1},{5,6},{6,5},{9,10},{10,9},{13,14},{14,13},{17,18},{18,... | collective-permute-start | bytes 294920 | tf_op jit(solution)/shard_map/ppermute | solution.py:640
  135.7 13.0 %copy-start = (f32[128,512]{1,0:T(8,128)}, f32[128,512]{1,0:T(8,128)S(1)}, u32[]{:S(2)}) copy-start(f32[128,512]{1,0:T(8,128)S(1)} %slice.21.before.refs_4_) | copy-start | bytes 786436
  135.7 13.2 %copy-start.25 = (f32[8,128]{1,0:T(8,128)S(1)}, f32[8,128]{1,0:T(8,128)}, u32[]{:S(2)}) copy-start(f32[8,128]{1,0:T(8,128)} %get-tuple-element.52) | copy-start | bytes 12292
  135.7 13.2 %copy-start.26 = (f32[8,128]{1,0:T(8,128)S(1)}, f32[8,128]{1,0:T(8,128)}, u32[]{:S(2)}) copy-start(f32[8,128]{1,0:T(8,128)} %get-tuple-element.65) | copy-start | bytes 12292
  146.5 14.1 %copy-start.27 = (f32[8,128]{1,0:T(8,128)S(1)}, f32[8,128]{1,0:T(8,128)}, u32[]{:S(2)}) copy-start(f32[8,128]{1,0:T(8,128)} %get-tuple-element.75) | copy-start | bytes 12292
  146.5 14.2 %copy-start.12 = (f32[128,512]{1,0:T(8,128)S(1)}, f32[128,512]{1,0:T(8,128)}, u32[]{:S(2)}) copy-start(f32[128,512]{1,0:T(8,128)} %get-tuple-element.76.refs_0_) | copy-start | bytes 786436
  146.5 6.9 %collective-permute-start.28 = (f32[32,640]{1,0:T(8,128)}, f32[32,640]{1,0:T(8,128)S(1)}, u32[]{:S(2)}, u32[]{:S(2)}) collective-permute-start(f32[32,640]{1,0:T(8,128)} %get-tuple-element.77.send_a), channel_id=1, source_target_pairs={{0,4},{8,12},{16,20},{24,28},{4,0},{12,8},{20,16},{28,24},{1,5},{9... | collective-permute-start | bytes 245768 | tf_op jit(solution)/shard_map/ppermute | solution.py:640
  146.8 6.7 %collective-permute-start.29 = (f32[32,640]{1,0:T(8,128)}, f32[32,640]{1,0:T(8,128)S(1)}, u32[]{:S(2)}, u32[]{:S(2)}) collective-permute-start(f32[32,640]{1,0:T(8,128)} %get-tuple-element.79.send_b), channel_id=1, source_target_pairs={{4,8},{12,16},{20,24},{8,4},{16,12},{24,20},{5,9},{13,17},{21,25},... | collective-permute-start | bytes 245768 | tf_op jit(solution)/shard_map/ppermute | solution.py:640
  148.7 14.9 %copy-start.1 = (f32[128,512]{1,0:T(8,128)S(1)}, f32[128,512]{1,0:T(8,128)}, u32[]{:S(2)}) copy-start(f32[128,512]{1,0:T(8,128)} %copy-done) | copy-start | bytes 786436
  149.5 11.0 %collective-permute-start.17 = (f32[4,8,128]{2,1,0:T(8,128)S(1)}, f32[4,8,128]{2,1,0:T(8,128)S(1)}, u32[]{:S(2)}, u32[]{:S(2)}) collective-permute-start(f32[4,8,128]{2,1,0:T(8,128)S(1)} %pad_maximum_fusion), channel_id=1, source_target_pairs={{0,1},{1,0},{2,3},{3,2},{4,5},{5,4},{6,7},{7,6},{8,9},{9,8},{10,11... | collective-permute-start | bytes 49160 | tf_op jit(solution)/shard_map/ppermute | solution.py:646
  156.2 36.2 %collective-permute-start.31 = (f32[144,512]{1,0:T(8,128)}, f32[144,512]{1,0:T(8,128)S(1)}, u32[]{:S(2)}, u32[]{:S(2)}) collective-permute-start(f32[144,512]{1,0:T(8,128)} %wrap.1.refs_8_), channel_id=1, source_target_pairs={{0,2},{1,3},{2,0},{3,1},{4,6},{5,7},{6,4},{7,5},{8,10},{9,11},{10,... | collective-permute-start | bytes 884744 | tf_op jit(solution)/shard_map/ppermute | solution.py:646
  160.6 19.9 %collective-permute-start.18 = (f32[4,8,128]{2,1,0:T(8,128)S(1)}, f32[4,8,128]{2,1,0:T(8,128)S(1)}, u32[]{:S(2)}, u32[]{:S(2)}) collective-permute-start(f32[4,8,128]{2,1,0:T(8,128)S(1)} %fusion), channel_id=1, source_target_pairs={{0,2},{1,3},{2,0},{3,1},{4,6},{5,7},{6,4},{7,5},{8,10},{9,11},{10,... | collective-permute-start | bytes 49160 | tf_op jit(solution)/shard_map/ppermute | solution.py:646
  160.7 33.7 %collective-permute-start.23 = (f32[128,512]{1,0:T(8,128)S(1)}, f32[128,512]{1,0:T(8,128)S(1)}, u32[]{:S(2)}, u32[]{:S(2)}) collective-permute-start(f32[128,512]{1,0:T(8,128)S(1)} %copy-done.12), channel_id=1, source_target_pairs={{0,2},{1,3},{2,0},{3,1},{4,6},{5,7},{6,4},{7,5},{8,10},{9,11},{10,... | collective-permute-start | bytes 786440 | tf_op jit(solution)/shard_map/ppermute | solution.py:646
  163.6 32.2 %collective-permute-start.22 = (f32[128,512]{1,0:T(8,128)S(1)}, f32[128,512]{1,0:T(8,128)S(1)}, u32[]{:S(2)}, u32[]{:S(2)}) collective-permute-start(f32[128,512]{1,0:T(8,128)S(1)} %copy-done.12), channel_id=1, source_target_pairs={{0,1},{1,0},{2,3},{3,2},{4,5},{5,4},{6,7},{7,6},{8,9},{9,8},{10,11... | collective-permute-start | bytes 786440 | tf_op jit(solution)/shard_map/ppermute | solution.py:646
  163.6 34.7 %collective-permute-start.26 = (f32[128,512]{1,0:T(8,128)S(1)}, f32[128,512]{1,0:T(8,128)S(1)}, u32[]{:S(2)}, u32[]{:S(2)}) collective-permute-start(f32[128,512]{1,0:T(8,128)S(1)} %copy-done.1), channel_id=1, source_target_pairs={{0,2},{1,3},{2,0},{3,1},{4,6},{5,7},{6,4},{7,5},{8,10},{9,11},{10,... | collective-permute-start | bytes 786440 | tf_op jit(solution)/shard_map/ppermute | solution.py:646
  180.5 8.1 %collective-permute-start.19 = (f32[4,8,128]{2,1,0:T(8,128)S(1)}, f32[4,8,128]{2,1,0:T(8,128)S(1)}, u32[]{:S(2)}, u32[]{:S(2)}) collective-permute-start(f32[4,8,128]{2,1,0:T(8,128)S(1)} %fusion.1), channel_id=1, source_target_pairs={{0,4},{4,0},{8,12},{12,8},{16,20},{20,16},{24,28},{28,24},{1,5},{5... | collective-permute-start | bytes 49160 | tf_op jit(solution)/shard_map/ppermute | solution.py:646
  188.6 3.7 %collective-permute-start.20 = (f32[4,8,128]{2,1,0:T(8,128)S(1)}, f32[4,8,128]{2,1,0:T(8,128)S(1)}, u32[]{:S(2)}, u32[]{:S(2)}) collective-permute-start(f32[4,8,128]{2,1,0:T(8,128)S(1)} %add.54), channel_id=1, source_target_pairs={{0,8},{4,12},{8,0},{12,4},{16,24},{20,28},{24,16},{28,20},{1,9},{5... | collective-permute-start | bytes 49160 | tf_op jit(solution)/shard_map/ppermute | solution.py:646
  192.4 29.7 %collective-permute-start.30 = (f32[144,512]{1,0:T(8,128)}, f32[144,512]{1,0:T(8,128)S(1)}, u32[]{:S(2)}, u32[]{:S(2)}) collective-permute-start(f32[144,512]{1,0:T(8,128)} %wrap.1.refs_8_), channel_id=1, source_target_pairs={{0,1},{1,0},{2,3},{3,2},{4,5},{5,4},{6,7},{7,6},{8,9},{9,8},{10,11... | collective-permute-start | bytes 884744 | tf_op jit(solution)/shard_map/ppermute | solution.py:646
  192.4 35.3 %copy-start.6 = (f32[144,512]{1,0:T(8,128)}, f32[144,512]{1,0:T(8,128)S(1)}, u32[]{:S(2)}) copy-start(f32[144,512]{1,0:T(8,128)S(1)} %collective-permute-done.31.refs_10_) | copy-start | bytes 884740
  192.4 35.3 %collective-permute-start.32 = (f32[144,512]{1,0:T(8,128)S(1)}, f32[144,512]{1,0:T(8,128)S(1)}, u32[]{:S(2)}, u32[]{:S(2)}) collective-permute-start(f32[144,512]{1,0:T(8,128)S(1)} %collective-permute-done.31.refs_10_), channel_id=1, source_target_pairs={{0,1},{1,0},{2,3},{3,2},{4,5},{5,4},{6,7},{7,6},{8,9},{9,8},{10,11... | collective-permute-start | bytes 884744 | tf_op jit(solution)/shard_map/ppermute | solution.py:646
  194.4 33.2 %copy-start.13 = (f32[128,512]{1,0:T(8,128)}, f32[128,512]{1,0:T(8,128)S(1)}, u32[]{:S(2)}) copy-start(f32[128,512]{1,0:T(8,128)S(1)} %collective-permute-done.23.refs_2_) | copy-start | bytes 786436
  194.4 3.8 %collective-permute-start.21 = (f32[4,8,128]{2,1,0:T(8,128)S(1)}, f32[4,8,128]{2,1,0:T(8,128)S(1)}, u32[]{:S(2)}, u32[]{:S(2)}) collective-permute-start(f32[4,8,128]{2,1,0:T(8,128)S(1)} %add.55), channel_id=1, source_target_pairs={{0,16},{4,20},{8,24},{12,28},{16,0},{20,4},{24,8},{28,12},{1,17},{... | collective-permute-start | bytes 49160 | tf_op jit(solution)/shard_map/ppermute | solution.py:646
  195.8 31.9 %copy-start.14 = (f32[128,512]{1,0:T(8,128)}, f32[128,512]{1,0:T(8,128)S(1)}, u32[]{:S(2)}) copy-start(f32[128,512]{1,0:T(8,128)S(1)} %collective-permute-done.22.refs_1_) | copy-start | bytes 786436
  195.8 20.7 %collective-permute-start.24 = (f32[128,512]{1,0:T(8,128)S(1)}, f32[128,512]{1,0:T(8,128)S(1)}, u32[]{:S(2)}, u32[]{:S(2)}) collective-permute-start(f32[128,512]{1,0:T(8,128)S(1)} %collective-permute-done.23.refs_2_), channel_id=1, source_target_pairs={{0,1},{1,0},{2,3},{3,2},{4,5},{5,4},{6,7},{7,6},{8,9},{9,8},{10,11... | collective-permute-start | bytes 786440 | tf_op jit(solution)/shard_map/ppermute | solution.py:646
  198.2 23.9 %collective-permute-start.25 = (f32[128,512]{1,0:T(8,128)S(1)}, f32[128,512]{1,0:T(8,128)S(1)}, u32[]{:S(2)}, u32[]{:S(2)}) collective-permute-start(f32[128,512]{1,0:T(8,128)S(1)} %copy-done.1), channel_id=1, source_target_pairs={{0,1},{1,0},{2,3},{3,2},{4,5},{5,4},{6,7},{7,6},{8,9},{9,8},{10,11... | collective-permute-start | bytes 786440 | tf_op jit(solution)/shard_map/ppermute | solution.py:646
  198.3 29.4 %copy-start.15 = (f32[128,512]{1,0:T(8,128)}, f32[128,512]{1,0:T(8,128)S(1)}, u32[]{:S(2)}) copy-start(f32[128,512]{1,0:T(8,128)S(1)} %collective-permute-done.26.refs_6_) | copy-start | bytes 786436
  198.3 29.3 %collective-permute-start.27 = (f32[128,512]{1,0:T(8,128)S(1)}, f32[128,512]{1,0:T(8,128)S(1)}, u32[]{:S(2)}, u32[]{:S(2)}) collective-permute-start(f32[128,512]{1,0:T(8,128)S(1)} %collective-permute-done.26.refs_6_), channel_id=1, source_target_pairs={{0,1},{1,0},{2,3},{3,2},{4,5},{5,4},{6,7},{7,6},{8,9},{9,8},{10,11... | collective-permute-start | bytes 786440 | tf_op jit(solution)/shard_map/ppermute | solution.py:646
  (20 other events, 46.4 us)
